TPU v7x, 32 devices: a whole 2x2x4 slice. The times are simulated.
32 devices in a mesh: seq: 8 (over z, y), batch: 4 (over x, core).
Axes of the slice: x: 2, y: 2, z: 4, core: 2. Of those that a mesh axis runs over, the one named last changes fastest.
Arguments:
- tokens_in: bfloat16 [4, 2048, 2048], P('batch', 'seq'), may hold values from -6 to 6
- cotangent: bfloat16 [4, 2048, 2048], P('batch', 'seq'), may hold values from -6 to 6
- segment_ids: int32 [4, 2048], P('batch'), may hold values from 0 to 5, never falling along the last dimension, each value on 1 to 682 neighbouring positions
- attn_gain: bfloat16 [2048], P(('seq', 'batch')), may hold values from 0.25 to 1.75
- attn_shift: bfloat16 [2048], P(('seq', 'batch')), may hold values from -2 to 2
- qkv_weight: bfloat16 [2048, 6144], P(('seq', 'batch')), may hold values from -0.125 to 0.125
- qkv_bias: bfloat16 [6144], P(('seq', 'batch')), may hold values from -3 to 3
- out_weight: bfloat16 [2048, 2048], P(('seq', 'batch')), may hold values from -1 to 1
- mlp_gain: bfloat16 [2048], P(('seq', 'batch')), may hold values from 0.25 to 1.75
- mlp_shift: bfloat16 [2048], P(('seq', 'batch')), may hold values from -2 to 2
- gate_weight: bfloat16 [2048, 5632], P(('seq', 'batch')), may hold values from -0.125 to 0.125
- up_weight: bfloat16 [2048, 5632], P(('seq', 'batch')), may hold values from -0.125 to 0.125
- down_weight: bfloat16 [5632, 2048], P(('seq', 'batch')), may hold values from -0.078125 to 0.078125
Outputs:
- block_out: bfloat16 [4, 2048, 2048], P('batch', 'seq')
- grad_tokens: bfloat16 [4, 2048, 2048], P('batch', 'seq')
- grad_attn_gain: float32 [2048], P(('seq', 'batch'))
- grad_attn_shift: float32 [2048], P(('seq', 'batch'))
- grad_qkv_weight: float32 [2048, 6144], P(('seq', 'batch'))
- grad_qkv_bias: float32 [6144], P(('seq', 'batch'))
- grad_out_weight: float32 [2048, 2048], P(('seq', 'batch'))
- grad_mlp_gain: float32 [2048], P(('seq', 'batch'))
- grad_mlp_shift: float32 [2048], P(('seq', 'batch'))
- grad_gate_weight: float32 [2048, 5632], P(('seq', 'batch'))
- grad_up_weight: float32 [2048, 5632], P(('seq', 'batch'))
- grad_down_weight: float32 [5632, 2048], P(('seq', 'batch'))
Inputs may be any that keep to these rules, and one draw needn't show every extreme that they name: `segment_ids`: each row holds 6 documents of consecutive ids, each 1 to 2048 // 3 tokens long, one exactly that long.
All inputs are finite; a program needn't handle non-finite values.
Results may differ from a plain program's by a relative error of at most 0.013.
Values may be sent and summed in bfloat16 or wider, within the bound.
No kernel may reach another device: no remote copies, remote signals or barrier semaphores. Data moves between devices by JAX's collectives and lax.ppermute only.
A program may use at most 448 MiB of HBM per device.

v0:
```python
import jax
import jax.numpy as jnp
from jax import lax
from jax.sharding import PartitionSpec as P

HEAD_DIM = 64
ROT = 16


epsilon = 1e-05


def layer_norm(value, gain, shift):
    centred = value - jnp.mean(value, axis=-1, keepdims=True)
    variance = jnp.mean(centred * centred, axis=-1, keepdims=True)
    return centred * lax.rsqrt(variance + epsilon) * gain + shift


def doc_positions(segment):
    length = segment.shape[-1]
    places = jnp.arange(length, dtype=jnp.int32)
    leading = jnp.ones(segment.shape[:-1] + (1,), dtype=bool)
    begins = jnp.concatenate([leading, segment[..., 1:] != segment[..., :-1]], axis=-1)
    starts = lax.cummax(jnp.where(begins, places, 0), axis=segment.ndim - 1)
    return places - starts


def angles(segment):
    position = doc_positions(segment).astype(jnp.float32)
    halfway = ROT // 2
    inverse = 10000.0 ** (-jnp.arange(halfway, dtype=jnp.float32) / halfway)
    theta = position[..., None] * inverse
    return (jnp.cos(theta), jnp.sin(theta))


def rotate(value, cosine, sine):
    halfway = ROT // 2
    first_part = value[..., :halfway]
    second_part = value[..., halfway:ROT]
    cos_part = cosine[..., None, :]
    sin_part = sine[..., None, :]
    return jnp.concatenate(
        [
            first_part * cos_part - second_part * sin_part,
            second_part * cos_part + first_part * sin_part,
            value[..., ROT:],
        ],
        axis=-1,
    )


def gated_product(gate_in, up_in):
    return jax.nn.silu(gate_in) * up_in


def block_scores(query_rows, keys, segment, first_row, block_rows, score_scale):
    length = keys.shape[0]
    columns = jnp.arange(length, dtype=jnp.int32)
    seg_rows = lax.dynamic_slice_in_dim(segment, first_row, block_rows, 0)
    scores = (
        jnp.einsum("bhd,khd->hbk", query_rows, keys, preferred_element_type=jnp.float32)
        * score_scale
    )
    row_index = first_row + jnp.arange(block_rows, dtype=jnp.int32)
    allowed = (columns[None, :] <= row_index[:, None]) & (segment[None, :] == seg_rows[:, None])
    return jnp.where(allowed[None], scores, -1e30)


def attend_forward(q_heads, k_heads, v_heads, segment, score_scale):
    length, feature_width = q_heads.shape
    local_heads = feature_width // HEAD_DIM
    queries = q_heads.reshape(length, local_heads, HEAD_DIM)
    keys = k_heads.reshape(length, local_heads, HEAD_DIM)
    values = v_heads.reshape(length, local_heads, HEAD_DIM)
    block_rows = min(512, length)
    blocks = length // block_rows

    def per_block(number):
        first_row = number * block_rows
        query_rows = lax.dynamic_slice_in_dim(queries, first_row, block_rows, 0)
        scores = block_scores(query_rows, keys, segment, first_row, block_rows, score_scale)
        row_max = jnp.max(scores, axis=-1, keepdims=True)
        weights = jnp.exp(scores - row_max)
        row_total = jnp.sum(weights, axis=-1, keepdims=True)
        weights = weights / row_total
        outputs = jnp.einsum(
            "hbk,khd->bhd", weights.astype(jnp.bfloat16), values, preferred_element_type=jnp.float32
        )
        return (outputs, row_max[..., 0] + jnp.log(row_total[..., 0]))

    outputs, logsum = lax.map(per_block, jnp.arange(blocks, dtype=jnp.int32))
    return (outputs.reshape(length, feature_width), logsum)


def attend_backward(q_heads, k_heads, v_heads, grad_heads, logsum, segment, score_scale):
    length, feature_width = q_heads.shape
    local_heads = feature_width // HEAD_DIM
    queries = q_heads.reshape(length, local_heads, HEAD_DIM)
    keys = k_heads.reshape(length, local_heads, HEAD_DIM)
    values = v_heads.reshape(length, local_heads, HEAD_DIM)
    grad_out = grad_heads.reshape(length, local_heads, HEAD_DIM)
    block_rows = min(512, length)
    blocks = length // block_rows

    def per_block(running, number):
        grad_keys, grad_values = running
        first_row = number * block_rows
        query_rows = lax.dynamic_slice_in_dim(queries, first_row, block_rows, 0)
        grad_rows = lax.dynamic_slice_in_dim(grad_out, first_row, block_rows, 0)
        scores = block_scores(query_rows, keys, segment, first_row, block_rows, score_scale)
        weights = jnp.exp(scores - logsum[number][..., None])
        grad_weights = jnp.einsum(
            "bhd,khd->hbk", grad_rows, values, preferred_element_type=jnp.float32
        )
        inner_sum = jnp.sum(weights * grad_weights, axis=-1, keepdims=True)
        grad_scores = (weights * (grad_weights - inner_sum)).astype(jnp.bfloat16)
        grad_query_rows = (
            jnp.einsum("hbk,khd->bhd", grad_scores, keys, preferred_element_type=jnp.float32)
            * score_scale
        )
        grad_keys = (
            grad_keys
            + jnp.einsum(
                "hbk,bhd->khd", grad_scores, query_rows, preferred_element_type=jnp.float32
            )
            * score_scale
        )
        grad_values = grad_values + jnp.einsum(
            "hbk,bhd->khd",
            weights.astype(jnp.bfloat16),
            grad_rows,
            preferred_element_type=jnp.float32,
        )
        return ((grad_keys, grad_values), grad_query_rows)

    zero_state = jnp.zeros((length, local_heads, HEAD_DIM), jnp.float32)
    (grad_keys, grad_values), grad_queries = lax.scan(
        per_block, (zero_state, zero_state), jnp.arange(blocks, dtype=jnp.int32)
    )
    return (
        grad_queries.reshape(length, feature_width),
        grad_keys.reshape(length, feature_width),
        grad_values.reshape(length, feature_width),
    )


def local(
    tokens_in,
    cotangent,
    segment_ids,
    attn_gain,
    attn_shift,
    qkv_weight,
    qkv_bias,
    out_weight,
    mlp_gain,
    mlp_shift,
    gate_weight,
    up_weight,
    down_weight,
):
    tokens = tokens_in.shape[1]
    inputs = tokens_in[0].astype(jnp.float32)
    segment = segment_ids[0]
    score_scale = HEAD_DIM ** (-0.5)
    norm_gain, norm_shift, qkv_full, bias_full, out_full = (
        lax.all_gather(attn_gain, ("seq", "batch"), axis=0, tiled=True),
        lax.all_gather(attn_shift, ("seq", "batch"), axis=0, tiled=True),
        lax.all_gather(qkv_weight, ("seq", "batch"), axis=0, tiled=True),
        lax.all_gather(qkv_bias, ("seq", "batch"), axis=0, tiled=True),
        lax.all_gather(out_weight, ("seq", "batch"), axis=0, tiled=True),
    )
    gain_one = norm_gain.astype(jnp.float32)
    normed = layer_norm(inputs, gain_one, norm_shift.astype(jnp.float32)).astype(jnp.bfloat16)
    projected = jnp.dot(normed, qkv_full, preferred_element_type=jnp.float32) + bias_full.astype(
        jnp.float32
    )
    cosine, sine = angles(segment)
    offset = lax.axis_index("seq") * tokens
    cosine = lax.dynamic_slice_in_dim(cosine, offset, tokens, 0)
    sine = lax.dynamic_slice_in_dim(sine, offset, tokens, 0)
    feature_width = projected.shape[1] // 3
    head_shape = (tokens, feature_width // HEAD_DIM, HEAD_DIM)
    queries = rotate(projected[:, :feature_width].reshape(head_shape), cosine, sine)
    keys = rotate(projected[:, feature_width : 2 * feature_width].reshape(head_shape), cosine, sine)
    queries = queries.reshape(tokens, feature_width).astype(jnp.bfloat16)
    keys = keys.reshape(tokens, feature_width).astype(jnp.bfloat16)
    values = projected[:, 2 * feature_width :].astype(jnp.bfloat16)
    q_heads, k_heads, v_heads = (
        lax.all_to_all(queries, "seq", split_axis=1, concat_axis=0, tiled=True),
        lax.all_to_all(keys, "seq", split_axis=1, concat_axis=0, tiled=True),
        lax.all_to_all(values, "seq", split_axis=1, concat_axis=0, tiled=True),
    )
    mixed, logsum = attend_forward(q_heads, k_heads, v_heads, segment, score_scale)
    mixed_tokens = lax.all_to_all(
        mixed.astype(jnp.bfloat16), "seq", split_axis=0, concat_axis=1, tiled=True
    )
    hidden = inputs + jnp.dot(mixed_tokens, out_full, preferred_element_type=jnp.float32)
    mlp_norm_gain, mlp_norm_shift, gate_full, up_full, down_full = (
        lax.all_gather(mlp_gain, ("seq", "batch"), axis=0, tiled=True),
        lax.all_gather(mlp_shift, ("seq", "batch"), axis=0, tiled=True),
        lax.all_gather(gate_weight, ("seq", "batch"), axis=0, tiled=True),
        lax.all_gather(up_weight, ("seq", "batch"), axis=0, tiled=True),
        lax.all_gather(down_weight, ("seq", "batch"), axis=0, tiled=True),
    )
    gain_two = mlp_norm_gain.astype(jnp.float32)
    normed_two = layer_norm(hidden, gain_two, mlp_norm_shift.astype(jnp.float32)).astype(
        jnp.bfloat16
    )
    gate_sum = jnp.dot(normed_two, gate_full, preferred_element_type=jnp.float32)
    up_sum = jnp.dot(normed_two, up_full, preferred_element_type=jnp.float32)
    activated = gated_product(gate_sum, up_sum).astype(jnp.bfloat16)
    output = hidden + jnp.dot(activated, down_full, preferred_element_type=jnp.float32)
    block_out = output.astype(jnp.bfloat16).reshape(tokens_in.shape)
    mlp_norm_gain, gate_full, up_full, down_full = (
        lax.all_gather(mlp_gain, ("seq", "batch"), axis=0, tiled=True),
        lax.all_gather(gate_weight, ("seq", "batch"), axis=0, tiled=True),
        lax.all_gather(up_weight, ("seq", "batch"), axis=0, tiled=True),
        lax.all_gather(down_weight, ("seq", "batch"), axis=0, tiled=True),
    )
    gain_two = mlp_norm_gain.astype(jnp.float32)
    grad_output = cotangent[0]
    grad_activated = jnp.dot(grad_output, down_full.T, preferred_element_type=jnp.float32)
    grad_down = jnp.dot(activated.T, grad_output, preferred_element_type=jnp.float32)
    unused_value, gating_back = jax.vjp(gated_product, gate_sum, up_sum)
    grad_gate_sum, grad_up_sum = gating_back(grad_activated)
    grad_gate_sum = grad_gate_sum.astype(jnp.bfloat16)
    grad_up_sum = grad_up_sum.astype(jnp.bfloat16)
    grad_gate = jnp.dot(normed_two.T, grad_gate_sum, preferred_element_type=jnp.float32)
    grad_up = jnp.dot(normed_two.T, grad_up_sum, preferred_element_type=jnp.float32)
    grad_normed_two = jnp.dot(
        grad_gate_sum, gate_full.T, preferred_element_type=jnp.float32
    ) + jnp.dot(grad_up_sum, up_full.T, preferred_element_type=jnp.float32)
    unused_norm, norm_back_two = jax.vjp(layer_norm, hidden, gain_two, jnp.zeros_like(gain_two))
    grad_hidden_norm, grad_gain_two, grad_shift_two = norm_back_two(grad_normed_two)
    grad_hidden = grad_output.astype(jnp.float32) + grad_hidden_norm
    mlp_grads = (
        lax.psum_scatter(grad_gain_two, ("seq", "batch"), scatter_dimension=0, tiled=True),
        lax.psum_scatter(grad_shift_two, ("seq", "batch"), scatter_dimension=0, tiled=True),
        lax.psum_scatter(grad_gate, ("seq", "batch"), scatter_dimension=0, tiled=True),
        lax.psum_scatter(grad_up, ("seq", "batch"), scatter_dimension=0, tiled=True),
        lax.psum_scatter(grad_down, ("seq", "batch"), scatter_dimension=0, tiled=True),
    )
    norm_gain, qkv_full, out_full = (
        lax.all_gather(attn_gain, ("seq", "batch"), axis=0, tiled=True),
        lax.all_gather(qkv_weight, ("seq", "batch"), axis=0, tiled=True),
        lax.all_gather(out_weight, ("seq", "batch"), axis=0, tiled=True),
    )
    gain_one = norm_gain.astype(jnp.float32)
    grad_branch = grad_hidden.astype(jnp.bfloat16)
    grad_out = jnp.dot(mixed_tokens.T, grad_branch, preferred_element_type=jnp.float32)
    grad_mixed = jnp.dot(grad_branch, out_full.T, preferred_element_type=jnp.float32).astype(
        jnp.bfloat16
    )
    grad_heads = lax.all_to_all(grad_mixed, "seq", split_axis=1, concat_axis=0, tiled=True)
    grad_queries, grad_keys, grad_values = attend_backward(
        q_heads, k_heads, v_heads, grad_heads, logsum, segment, score_scale
    )
    query_grad_tok, key_grad_tok, value_grad_tok = (
        lax.all_to_all(
            grad_queries.astype(jnp.bfloat16), "seq", split_axis=0, concat_axis=1, tiled=True
        ),
        lax.all_to_all(
            grad_keys.astype(jnp.bfloat16), "seq", split_axis=0, concat_axis=1, tiled=True
        ),
        lax.all_to_all(
            grad_values.astype(jnp.bfloat16), "seq", split_axis=0, concat_axis=1, tiled=True
        ),
    )
    query_raw = rotate(query_grad_tok.astype(jnp.float32).reshape(head_shape), cosine, -sine)
    key_raw = rotate(key_grad_tok.astype(jnp.float32).reshape(head_shape), cosine, -sine)
    grad_projected = jnp.concatenate(
        [
            query_raw.reshape(tokens, feature_width),
            key_raw.reshape(tokens, feature_width),
            value_grad_tok.astype(jnp.float32),
        ],
        axis=1,
    ).astype(jnp.bfloat16)
    grad_qkv = jnp.dot(normed.T, grad_projected, preferred_element_type=jnp.float32)
    grad_bias = jnp.sum(grad_projected.astype(jnp.float32), axis=0)
    grad_normed = jnp.dot(grad_projected, qkv_full.T, preferred_element_type=jnp.float32)
    unused_first, norm_back_one = jax.vjp(layer_norm, inputs, gain_one, jnp.zeros_like(gain_one))
    grad_inputs_norm, grad_gain_one, grad_shift_one = norm_back_one(grad_normed)
    grad_tokens = (grad_hidden + grad_inputs_norm).astype(jnp.bfloat16).reshape(tokens_in.shape)
    attn_grads = (
        lax.psum_scatter(grad_gain_one, ("seq", "batch"), scatter_dimension=0, tiled=True),
        lax.psum_scatter(grad_shift_one, ("seq", "batch"), scatter_dimension=0, tiled=True),
        lax.psum_scatter(grad_qkv, ("seq", "batch"), scatter_dimension=0, tiled=True),
        lax.psum_scatter(grad_bias, ("seq", "batch"), scatter_dimension=0, tiled=True),
        lax.psum_scatter(grad_out, ("seq", "batch"), scatter_dimension=0, tiled=True),
    )
    return (
        block_out,
        grad_tokens,
        attn_grads[0],
        attn_grads[1],
        attn_grads[2],
        attn_grads[3],
        attn_grads[4],
        mlp_grads[0],
        mlp_grads[1],
        mlp_grads[2],
        mlp_grads[3],
        mlp_grads[4],
    )


def solution(mesh):
    return jax.shard_map(
        local,
        mesh=mesh,
        in_specs=(
            P("batch", "seq", None),
            P("batch", "seq", None),
            P("batch", None),
            P(("seq", "batch")),
            P(("seq", "batch")),
            P(("seq", "batch"), None),
            P(("seq", "batch")),
            P(("seq", "batch"), None),
            P(("seq", "batch")),
            P(("seq", "batch")),
            P(("seq", "batch"), None),
            P(("seq", "batch"), None),
            P(("seq", "batch"), None),
        ),
        out_specs=(
            P("batch", "seq", None),
            P("batch", "seq", None),
            P(("seq", "batch")),
            P(("seq", "batch")),
            P(("seq", "batch"), None),
            P(("seq", "batch")),
            P(("seq", "batch"), None),
            P(("seq", "batch")),
            P(("seq", "batch")),
            P(("seq", "batch"), None),
            P(("seq", "batch"), None),
            P(("seq", "batch"), None),
        ),
        check_vma=False,
    )
```

profile of v0, /device:TPU:0, one launch (start us, length us, event | category | flops | bytes accessed | tf_op | source)
XLA Modules:
  0.0 3149.0 jit_solution(3610313463786880236)
XLA Ops:
  11.9 44.7 %all-reduce.11 = (bf16[6144]{0:T(1024)(128)(2,1)S(1)}, bf16[2048]{0:T(1024)(128)(2,1)S(1)}, bf16[2048]{0:T(1024)(128)(2,1)S(1)}, bf16[2048]{0:T(1024)(128)(2,1)}, bf16[2048]{0:T(1024)(128)(2,1)}) all-reduce(bf16[6144]{0:T(1024)(128)(2,1)S(1)} %dynamic-update-slice.2, ...), channel_id=1, replica_groups=mesh['seq'=8,'batch'=4] {'seq','batch'}, use_global_device_ids=true, to_apply=%add.2 | all-reduce | flops 14336 | bytes 57344
  59.6 109.6 %all-gather.6.cloned.1.call-done = bf16[2048,6144]{1,0:T(8,128)(2,1)} async-done(((bf16[64,6144]{1,0:T(8,128)(2,1)}), bf16[2048,6144]{1,0:T(8,128)(2,1)}) %all-gather.6.cloned.1.call-update) | async-done | bytes 25165840 | tf_op jit(solution)/shard_map/all_gather | solution.py:169
  194.7 38.6 %all_to_all.104 = bf16[256,8,256]{0,2,1:T(8,128)(2,1)S(1)} all-to-all(bf16[256,8,256]{0,2,1:T(8,128)(2,1)S(1)} %bitcast.230), channel_id=1, replica_groups=mesh['seq'=8,'batch'=4] {'seq'}, dimensions={1} | all-to-all | bytes 2097152 | tf_op jit(solution)/shard_map/all_to_all | solution.py:190
  239.6 39.4 %all-to-all-done.1 = bf16[256,8,256]{0,2,1:T(8,128)(2,1)S(1)} async-done(((bf16[256,8,256]{0,2,1:T(8,128)(2,1)}), bf16[256,8,256]{0,2,1:T(8,128)(2,1)S(1)}, u32[]{:S(2)}, u32[]{:S(2)}) %all-to-all-start.1) | async-done | bytes 1048608 | tf_op jit(solution)/shard_map/all_to_all | solution.py:191
  288.0 37.3 %all-to-all-done.2 = bf16[256,8,256]{2,0,1:T(8,128)(2,1)} async-done(((bf16[256,8,256]{2,0,1:T(8,128)(2,1)}), bf16[256,8,256]{2,0,1:T(8,128)(2,1)}, u32[]{:S(2)}, u32[]{:S(2)}) %all-to-all-start.2) | async-done | bytes 1048608 | tf_op jit(solution)/shard_map/all_to_all | solution.py:192
  330.8 71.4 %while.27 = (s32[]{:T(128)}, bf16[4,512,4,64]{1,3,2,0:T(8,128)(2,1)}, f32[4,4,512]{2,1,0:T(4,128)}, s32[4]{0:T(128)S(1)}, s32[1,2048]{1,0:T(1,128)}, /*index=5*/...) while((s32[]{:T(128)}, ...), condition=%wide.region_7.8_spmd, body=%wide.region_4.7_spmd.sunk | while | flops 1127217664 | bytes 57494720 | solution.py:91
  415.3 43.2 %all-to-all-done.3 = bf16[8,256,256]{1,2,0:T(8,128)(2,1)} async-done(((bf16[8,256,256]{1,2,0:T(8,128)(2,1)}), bf16[8,256,256]{1,2,0:T(8,128)(2,1)}, u32[]{:S(2)}, u32[]{:S(2)}) %all-to-all-start.3) | async-done | bytes 1048608 | tf_op jit(solution)/shard_map/all_to_all | solution.py:195
  480.8 123.7 %all-gather.12.cloned.1.call-done = bf16[2048,5632]{1,0:T(8,128)(2,1)} async-done(((bf16[64,5632]{1,0:T(8,128)(2,1)}), bf16[2048,5632]{1,0:T(8,128)(2,1)}) %all-gather.12.cloned.1.call-update) | async-done | bytes 23068688 | tf_op jit(solution)/shard_map/all_gather | solution.py:203
  617.7 131.6 %all-gather.14.cloned.1.call-done = bf16[5632,2048]{1,0:T(8,128)(2,1)} async-done(((bf16[176,2048]{1,0:T(8,128)(2,1)}), bf16[5632,2048]{1,0:T(8,128)(2,1)}) %all-gather.14.cloned.1.call-update) | async-done | bytes 23068688 | tf_op jit(solution)/shard_map/all_gather | solution.py:204
  749.3 18.7 multiply_convert_fusion.1
  820.8 19.6 all-to-all-done.4
  844.7 270.3 %while.28 = (s32[]{:T(128)}, f32[2048,4,64]{0,2,1:T(8,128)}, f32[2048,4,64]{0,2,1:T(8,128)}, bf16[4,512,4,64]{1,3,2,0:T(8,128)(2,1)}, s32[4]{0:T(128)S(1)}, /*in...) while((s32[]{:T(128)}, f32[2048,4,64]{0,2,1:T(8,128)}, ...), condition=%wide.region_14.15_spmd.clone, body=%wide.region_12.14_spmd.clone.sunk | while | flops 2753165824 | bytes 248064560 | solution.py:137
  1131.6 24.4 all-to-all-done.5
  1162.9 22.7 all-to-all-done.6
  1191.7 23.5 all-to-all-done.7
  1215.2 19.3 fusion.66
  1235.8 29.9 fusion.80
  1265.8 30.4 fusion.81
  1297.6 21.3 fusion.59
  1349.3 41.3 %all-reduce.10 = (f32[2048]{0:T(1024)S(1)}, f32[2048]{0:T(1024)S(1)}, f32[6144]{0:T(1024)S(1)}, f32[2048]{0:T(1024)S(1)}, f32[2048]{0:T(1024)S(1)}) all-reduce(f32[2048]{0:T(1024)S(1)} %get-tuple-element.191, f32[2048]{0:T(1024)S(1)} %get-tuple-element.194, ...), channel_id=2, replica_groups=mesh['seq'=8,'batch'=4] {'seq','batch'}, use_global_device_ids=true, to_apply=%region_18.19.clone | all-reduce | flops 14336 | bytes 114688
  1397.4 265.3 %reduce-scatter.6.cloned.1.call-done = f32[64,6144]{1,0:T(8,128)} async-done(((f32[2048,6144]{1,0:T(8,128)}), f32[64,6144]{1,0:T(8,128)}) %reduce-scatter.6.cloned.1.call-update) | async-done | bytes 1572880 | tf_op jit(solution)/shard_map/reduce_scatter | solution.py:289
  1662.7 487.1 %reduce-scatter.10.cloned.1.call-done = f32[64,5632]{1,0:T(8,128)} async-done(((f32[2048,5632]{1,0:T(8,128)}), f32[64,5632]{1,0:T(8,128)}) %reduce-scatter.10.cloned.1.call-update) | async-done | bytes 1441808 | tf_op jit(solution)/shard_map/reduce_scatter | solution.py:240
  2149.8 496.1 %reduce-scatter.12.cloned.1.call-done = f32[64,5632]{1,0:T(8,128)} async-done(((f32[2048,5632]{1,0:T(8,128)}), f32[64,5632]{1,0:T(8,128)}) %reduce-scatter.12.cloned.1.call-update) | async-done | bytes 1441808 | tf_op jit(solution)/shard_map/reduce_scatter | solution.py:241
  2645.9 496.0 %reduce-scatter.14.cloned.1.call-done = f32[176,2048]{1,0:T(8,128)} async-done(((f32[5632,2048]{1,0:T(8,128)}), f32[176,2048]{1,0:T(8,128)}) %reduce-scatter.14.cloned.1.call-update) | async-done | bytes 1441808 | tf_op jit(solution)/shard_map/reduce_scatter | solution.py:242
  (383 shorter events, 556.1 us)
Async XLA Ops:
  7.2 161.9 %all-gather.6.cloned.1.call-start = ((), (), s32[]{:S(2)}) async-start(), calls=%async_computation.13 | async-start | bytes 25952256 | tf_op jit(solution)/shard_map/all_gather | solution.py:169
  8.0 407.4 %all-gather.8.cloned.1.call-start = ((), (), s32[]{:S(2)}) async-start(), calls=%async_computation.14 | async-start | bytes 8650752 | tf_op jit(solution)/shard_map/all_gather | solution.py:171
  8.7 457.8 %all-gather.10.cloned.1.call-start = ((), (), s32[]{:S(2)}) async-start(), calls=%async_computation.15 | async-start | bytes 23789568 | tf_op jit(solution)/shard_map/all_gather | solution.py:202
  9.5 595.0 %all-gather.12.cloned.1.call-start = ((), (), s32[]{:S(2)}) async-start(), calls=%async_computation.16 | async-start | bytes 23789568 | tf_op jit(solution)/shard_map/all_gather | solution.py:203
  10.0 739.2 %all-gather.14.cloned.1.call-start = ((), (), s32[]{:S(2)}) async-start(), calls=%async_computation.17 | async-start | bytes 23789568 | tf_op jit(solution)/shard_map/all_gather | solution.py:204
  56.6 112.6 %copy-start.28 = (f32[2048]{0:T(1024)}, f32[2048]{0:T(1024)S(1)}, u32[]{:S(2)}) copy-start(f32[2048]{0:T(1024)S(1)} %convert_element_type.141) | copy-start | bytes 24580
  56.6 112.6 %copy-start.30 = (f32[2048]{0:T(1024)}, f32[2048]{0:T(1024)S(1)}, u32[]{:S(2)}) copy-start(f32[2048]{0:T(1024)S(1)} %convert_element_type.142) | copy-start | bytes 24580
  58.9 133.3 %copy-start.36 = (f32[256,8]{0,1:T(8,128)}, f32[256,8]{0,1:T(8,128)S(1)}, u32[]{:S(2)}) copy-start(f32[256,8]{0,1:T(8,128)S(1)} %get-tuple-element.269) | copy-start | bytes 24580
  59.1 110.1 %copy-start.32 = (f32[256]{0:T(256)}, f32[256]{0:T(256)S(1)}, u32[]{:S(2)}) copy-start(f32[256]{0:T(256)S(1)} %broadcast_multiply_fusion.2) | copy-start | bytes 3076
  59.6 109.6 %copy-start.41 = (f32[256]{0:T(256)}, f32[256]{0:T(256)S(1)}, u32[]{:S(2)}) copy-start(f32[256]{0:T(256)S(1)} %fusion.55) | copy-start | bytes 3076
  59.6 109.6 %copy-start.34 = (f32[256]{0:T(256)}, f32[256]{0:T(256)S(1)}, u32[]{:S(2)}) copy-start(f32[256]{0:T(256)S(1)} %fusion.64) | copy-start | bytes 3076
  233.3 45.7 %all-to-all-start.1 = ((bf16[256,8,256]{0,2,1:T(8,128)(2,1)}), bf16[256,8,256]{0,2,1:T(8,128)(2,1)S(1)}, u32[]{:S(2)}, u32[]{:S(2)}) async-start(bf16[256,8,256]{0,2,1:T(8,128)(2,1)} %bitcast.13), calls=%async_computation.1 | async-start | bytes 2097152 | tf_op jit(solution)/shard_map/all_to_all | solution.py:191
  279.0 46.3 %all-to-all-start.2 = ((bf16[256,8,256]{2,0,1:T(8,128)(2,1)}), bf16[256,8,256]{2,0,1:T(8,128)(2,1)}, u32[]{:S(2)}, u32[]{:S(2)}) async-start(bf16[256,8,256]{2,0,1:T(8,128)(2,1)} %bitcast.168), calls=%async_computation.2 | async-start | bytes 2097152 | tf_op jit(solution)/shard_map/all_to_all | solution.py:192
  410.8 47.8 %all-to-all-start.3 = ((bf16[8,256,256]{1,2,0:T(8,128)(2,1)}), bf16[8,256,256]{1,2,0:T(8,128)(2,1)}, u32[]{:S(2)}, u32[]{:S(2)}) async-start(bf16[8,256,256]{1,2,0:T(8,128)(2,1)} %copy.72), calls=%async_computation.3 | async-start | bytes 2097152 | tf_op jit(solution)/shard_map/all_to_all | solution.py:195
  466.5 138.0 %copy-start.13 = (bf16[256,2048]{1,0:T(8,128)(2,1)}, bf16[256,2048]{1,0:T(8,128)(2,1)S(1)}, u32[]{:S(2)}) copy-start(bf16[256,2048]{1,0:T(8,128)(2,1)S(1)} %add_convert_fusion.1) | copy-start | bytes 3145732
  807.1 33.3 %all-to-all-start.4 = ((bf16[256,8,256]{2,0,1:T(8,128)(2,1)}), bf16[256,8,256]{2,0,1:T(8,128)(2,1)}, u32[]{:S(2)}, u32[]{:S(2)}) async-start(bf16[256,8,256]{2,0,1:T(8,128)(2,1)} %bitcast.226), calls=%async_computation.4 | async-start | bytes 2097152 | tf_op jit(solution)/shard_map/all_to_all | solution.py:255
  811.3 586.1 %reduce-scatter.8.cloned.1.call-start = ((), (), s32[]{:S(2)}) async-start(), calls=%async_computation.19 | async-start | bytes 17301504 | tf_op jit(solution)/shard_map/reduce_scatter | solution.py:291
  1120.6 35.4 %all-to-all-start.5 = ((bf16[8,256,256]{1,2,0:T(8,128)(2,1)}), bf16[8,256,256]{1,2,0:T(8,128)(2,1)S(1)}, u32[]{:S(2)}, u32[]{:S(2)}) async-start(bf16[8,256,256]{1,2,0:T(8,128)(2,1)} %copy.76), calls=%async_computation.5 | async-start | bytes 2097152 | tf_op jit(solution)/shard_map/all_to_all | solution.py:260
  1156.0 29.6 all-to-all-start.6
  1185.6 29.6 all-to-all-start.7
  1189.2 473.5 %reduce-scatter.6.cloned.1.call-start = ((), (), s32[]{:S(2)}) async-start(), calls=%async_computation.18 | async-start | bytes 51904512 | tf_op jit(solution)/shard_map/reduce_scatter | solution.py:289
  1234.6 915.2 %reduce-scatter.10.cloned.1.call-start = ((), (), s32[]{:S(2)}) async-start(), calls=%async_computation.20 | async-start | bytes 47579136 | tf_op jit(solution)/shard_map/reduce_scatter | solution.py:240
  1265.7 1380.2 %reduce-scatter.12.cloned.1.call-start = ((), (), s32[]{:S(2)}) async-start(), calls=%async_computation.21 | async-start | bytes 47579136 | tf_op jit(solution)/shard_map/reduce_scatter | solution.py:241
  1296.2 1845.7 %reduce-scatter.14.cloned.1.call-start = ((), (), s32[]{:S(2)}) async-start(), calls=%async_computation.22 | async-start | bytes 47579136 | tf_op jit(solution)/shard_map/reduce_scatter | solution.py:242
  (79 other events, 1016.8 us)
Sparse Core Ops, SparseCore 0:
  10.9 158.2 all-gather.5
  172.0 107.1 all-gather.7
  282.1 177.9 all-gather.9
  462.7 141.7 all-gather.11
  607.2 142.0 all-gather.13
  820.9 184.8 reduce-scatter.7
  1234.7 427.9 reduce-scatter.5
  1665.6 484.1 reduce-scatter.9
  2152.7 493.1 reduce-scatter.11
  2648.6 493.2 reduce-scatter.13
where the time goes:
time: 3160 us; the launch traced here: 3150 us
  waiting for transfers between devices  2320 us (73%)
  matrix products  460 us (15%)
  blocking collectives  125 us (4%)
  other arithmetic  100 us (3%)
  local copies, waits for them, and re-layouts  78.1 us (2%)
  starting transfers between devices  34 us (1%)
    reduce_scatter x1, waiting for transfers between devices, local(): lax.psum_scatter(grad_up, ('seq', 'batch'), scatter_dimension=0, tiled=True)  496 us
    reduce_scatter x1, waiting for transfers between devices, local(): lax.psum_scatter(grad_down, ('seq', 'batch'), scatter_dimension=0, tiled=...  496 us
    reduce_scatter x1, waiting for transfers between devices, local(): lax.psum_scatter(grad_gate, ('seq', 'batch'), scatter_dimension=0, tiled=...  487 us
    reduce_scatter x1, waiting for transfers between devices, local(): lax.psum_scatter(grad_qkv, ('seq', 'batch'), scatter_dimension=0, tiled=T...  265 us
    all_gather x1, waiting for transfers between devices, local(): lax.all_gather(down_weight, ('seq', 'batch'), axis=0, tiled=True)  132 us
    all_gather x1, waiting for transfers between devices, local(): lax.all_gather(up_weight, ('seq', 'batch'), axis=0, tiled=True)  124 us
    all_gather x1, waiting for transfers between devices, local(): lax.all_gather(qkv_weight, ('seq', 'batch'), axis=0, tiled=True)  110 us
    unnamed x2, blocking collectives  86 us
  transfers between devices with their start and end apart: 17, of which 14 were waited for; matrix products, arithmetic and copies ran while one was open for 18% of the time, Pallas kernels for 0%

commit v1 on v0

v1 whole, which is shorter than its diff:
```python
import functools

import jax
import jax.numpy as jnp
from jax import lax
from jax.experimental import pallas as pl
from jax.experimental.pallas import tpu as pltpu
from jax.sharding import Mesh
from jax.sharding import PartitionSpec as P

HEAD_DIM = 64
ROT = 16
DOCS = 6
LANES = 128
EPS = 1e-05
BF = jnp.bfloat16
F32 = jnp.float32
NEG = -1e30
ALL = ("z", "y", "x", "c")
SEQ = ("z", "y")
BATCH = ("x", "c")
SWAP = ((0, 1), (1, 0))


def dot(a, b, out=F32):
    return jnp.dot(a, b, preferred_element_type=out)


def dot_nt(a, b, out=F32):
    return lax.dot_general(a, b, (((1,), (1,)), ((), ())), preferred_element_type=out)


def dot_tn(a, b, out=F32):
    return lax.dot_general(a, b, (((0,), (0,)), ((), ())), preferred_element_type=out)


def gather_batch(x, pair):
    if not pair:
        return lax.all_gather(x, BATCH, axis=0, tiled=True)
    other = lax.ppermute(x, "x", SWAP)
    near = jnp.concatenate([x, other], axis=0)
    far = lax.ppermute(near, "c", SWAP)
    return jnp.concatenate([near, far], axis=0)


def reduce_batch(part, pair):
    if not pair:
        return lax.psum_scatter(part, BATCH, scatter_dimension=0, tiled=True).astype(F32)
    rows = part.shape[0] // 4
    got = lax.ppermute(part[2 * rows :], "c", SWAP)
    send = (part[rows : 2 * rows].astype(F32) + got[rows:].astype(F32)).astype(BF)
    last = lax.ppermute(send, "x", SWAP)
    return part[:rows].astype(F32) + got[:rows].astype(F32) + last.astype(F32)


def gather_seq(w, ny):
    near = lax.all_gather(w, "z", axis=0, tiled=True)
    if ny != 2:
        full = lax.all_gather(near.reshape((-1,) + w.shape), "y", axis=1)
        return full.reshape((-1,) + w.shape[1:])
    far = lax.ppermute(near, "y", SWAP)
    near = near.reshape((-1, 1) + w.shape)
    far = far.reshape((-1, 1) + w.shape)
    first = lax.axis_index("y") == 0
    full = jnp.concatenate([jnp.where(first, near, far), jnp.where(first, far, near)], axis=1)
    return full.reshape((-1,) + w.shape[1:])


def reduce_seq(g, nz, ny):
    rows = g.shape[0] // (nz * ny)
    g = g.reshape((nz, ny, rows) + g.shape[1:])
    if ny != 2:
        g = lax.psum_scatter(g, "y", scatter_dimension=1, tiled=True)
        return lax.psum_scatter(
            g.reshape((nz * rows,) + g.shape[3:]), "z", scatter_dimension=0, tiled=True
        )
    here = lax.axis_index("y")
    send = lax.dynamic_index_in_dim(g, 1 - here, 1, keepdims=False)
    got = lax.ppermute(send, "y", SWAP)
    keep = lax.dynamic_index_in_dim(g, here, 1, keepdims=False)
    both = (keep.astype(F32) + got.astype(F32)).astype(BF)
    return lax.psum_scatter(
        both.reshape((nz * rows,) + both.shape[2:]), "z", scatter_dimension=0, tiled=True
    )


def swap_batch(x):
    return lax.all_to_all(x, BATCH, split_axis=0, concat_axis=0, tiled=True)


def swap_seq(x):
    return lax.all_to_all(x, SEQ, split_axis=0, concat_axis=0, tiled=True)


def norm_stats(value):
    centred = value - jnp.mean(value, axis=-1, keepdims=True)
    scale = lax.rsqrt(jnp.mean(centred * centred, axis=-1, keepdims=True) + EPS)
    return centred * scale, scale


def norm_back(grad, unit, scale, gain):
    e = grad * gain
    back = scale * (
        e - jnp.mean(e, axis=-1, keepdims=True) - unit * jnp.mean(e * unit, axis=-1, keepdims=True)
    )
    return back, jnp.sum(grad * unit, axis=0), jnp.sum(grad, axis=0)


def turn(value, cosine, sine, lane):
    inner = lane % HEAD_DIM
    ahead = pltpu.roll(value, LANES - ROT // 2, 1)
    behind = pltpu.roll(value, ROT // 2, 1)
    return value * cosine + jnp.where(inner < ROT // 2, ahead, behind) * sine


def rotary_out_body(proj_ref, bias_ref, cos_ref, sin_ref, out_ref):
    value = proj_ref[...] + bias_ref[...]
    lane = lax.broadcasted_iota(jnp.int32, value.shape, 1)
    turned = turn(value, cos_ref[...], sin_ref[...], lane)
    value = jnp.where(pl.program_id(1) < 2, turned, value)
    out_ref[...] = value.astype(BF).reshape(out_ref.shape)


def rotary_out(proj, bias, cosine, sine, pairs, rpg, t):
    groups = proj.shape[0] // (rpg * t)
    block = rpg * t
    return pl.pallas_call(
        rotary_out_body,
        grid=(pairs * groups, 3),
        in_specs=[
            pl.BlockSpec((block, LANES), lambda d, p: (d % groups, p * pairs + d // groups)),
            pl.BlockSpec((1, LANES), lambda d, p: (0, p * pairs + d // groups)),
            pl.BlockSpec((block, LANES), lambda d, p: (d % groups, 0)),
            pl.BlockSpec((block, LANES), lambda d, p: (d % groups, 0)),
        ],
        out_specs=pl.BlockSpec((1, 1, rpg, t, LANES), lambda d, p: (d, p, 0, 0, 0)),
        out_shape=jax.ShapeDtypeStruct((pairs * groups, 3, rpg, t, LANES), BF),
        cost_estimate=pl.CostEstimate(
            flops=6 * proj.size, bytes_accessed=6 * proj.size, transcendentals=0
        ),
        name="rotary_out",
    )(proj, bias, cosine, sine)


def rotary_in_body(grad_ref, cos_ref, sin_ref, out_ref):
    value = grad_ref[...].reshape(out_ref.shape).astype(F32)
    lane = lax.broadcasted_iota(jnp.int32, value.shape, 1)
    turned = turn(value, cos_ref[...], -sin_ref[...], lane)
    out_ref[...] = jnp.where(pl.program_id(1) < 2, turned, value).astype(BF)


def rotary_in(grad, cosine, sine, pairs):
    dests, _, rpg, t, _ = grad.shape
    groups = dests // pairs
    block = rpg * t
    return pl.pallas_call(
        rotary_in_body,
        grid=(dests, 3),
        in_specs=[
            pl.BlockSpec((1, 1, rpg, t, LANES), lambda d, p: (d, p, 0, 0, 0)),
            pl.BlockSpec((block, LANES), lambda d, p: (d % groups, 0)),
            pl.BlockSpec((block, LANES), lambda d, p: (d % groups, 0)),
        ],
        out_specs=pl.BlockSpec((block, LANES), lambda d, p: (d % groups, p * pairs + d // groups)),
        out_shape=jax.ShapeDtypeStruct((groups * block, 3 * pairs * LANES), BF),
        cost_estimate=pl.CostEstimate(
            flops=6 * grad.size, bytes_accessed=4 * grad.size, transcendentals=0
        ),
        name="rotary_in",
    )(grad, cosine, sine)


def by_head(x):
    lane = lax.broadcasted_iota(jnp.int32, x.shape, 1)
    zero = jnp.zeros_like(x)
    return jnp.concatenate(
        [jnp.where(lane < HEAD_DIM, x, zero), jnp.where(lane >= HEAD_DIM, x, zero)], axis=0
    )


def one_head(x):
    t = x.shape[0] // 2
    lane = lax.broadcasted_iota(jnp.int32, (t, LANES), 1)
    return jnp.where(lane < HEAD_DIM, x[:t], x[t:])


def window_weights(q2, keys, start, row0, col0):
    scores = dot_nt(q2, keys) * (HEAD_DIM**-0.5)
    t = q2.shape[0] // 2
    shape = (t, keys.shape[0])
    rows = row0 + lax.broadcasted_iota(jnp.int32, shape, 0)
    cols = col0 + lax.broadcasted_iota(jnp.int32, shape, 1)
    allowed = (cols <= rows) & (cols >= start)
    allowed = jnp.concatenate([allowed, allowed], axis=0)
    scores = jnp.where(allowed, scores, NEG)
    weights = jnp.exp(scores - jnp.max(scores, axis=-1, keepdims=True))
    return weights / jnp.sum(weights, axis=-1, keepdims=True)


def forward_body(window, q_ref, k_ref, v_ref, start_ref, out_ref):
    number = pl.program_id(1)
    t = q_ref.shape[3]
    first = jnp.maximum(number - (window - 1), 0)
    keys = k_ref[pl.ds(first, window), 0, 0].reshape(window * t, LANES)
    values = v_ref[pl.ds(first, window), 0, 0].reshape(window * t, LANES)
    q2 = by_head(q_ref[0, 0, 0])
    weights = window_weights(q2, keys, start_ref[0, 0], number * t, first * t)
    out_ref[0, 0] = one_head(dot(weights.astype(BF), values)).astype(BF)


def attention_specs(blocks, t):
    return [
        pl.BlockSpec((1, 1, 1, t, LANES), lambda r, i: (i, 0, r, 0, 0)),
        pl.BlockSpec((blocks, 1, 1, t, LANES), lambda r, i: (0, 1, r, 0, 0)),
        pl.BlockSpec((blocks, 1, 1, t, LANES), lambda r, i: (0, 2, r, 0, 0)),
        pl.BlockSpec((1, 1, t, 1), lambda r, i: (r, i, 0, 0)),
    ]


def attend(qkv, start, window):
    blocks, _, rpg, t, _ = qkv.shape
    work = rpg * blocks * 2 * t * window * t
    return pl.pallas_call(
        functools.partial(forward_body, window),
        grid=(rpg, blocks),
        in_specs=attention_specs(blocks, t),
        out_specs=pl.BlockSpec((1, 1, t, LANES), lambda r, i: (i, r, 0, 0)),
        out_shape=jax.ShapeDtypeStruct((blocks, rpg, t, LANES), BF),
        cost_estimate=pl.CostEstimate(
            flops=4 * LANES * work, bytes_accessed=4 * qkv.size, transcendentals=work
        ),
        name="attend",
    )(qkv, qkv, qkv, start)


def backward_body(window, q_ref, k_ref, v_ref, start_ref, do_ref, out_ref, dk_ref, dv_ref):
    number = pl.program_id(1)
    t = q_ref.shape[3]
    scale = HEAD_DIM**-0.5

    @pl.when(number == 0)
    def _():
        dk_ref[...] = jnp.zeros_like(dk_ref)
        dv_ref[...] = jnp.zeros_like(dv_ref)

    first = jnp.maximum(number - (window - 1), 0)
    keys = k_ref[pl.ds(first, window), 0, 0].reshape(window * t, LANES)
    values = v_ref[pl.ds(first, window), 0, 0].reshape(window * t, LANES)
    q2 = by_head(q_ref[0, 0, 0])
    do2 = by_head(do_ref[0, 0])
    weights = window_weights(q2, keys, start_ref[0, 0], number * t, first * t)
    grad = dot_nt(do2, values)
    inner = jnp.sum(weights * grad, axis=-1, keepdims=True)
    ds = (weights * (grad - inner)).astype(BF)
    out_ref[number, 0, 0] = one_head(dot(ds, keys) * scale).astype(BF)
    shape = (window, t, LANES)
    dk_ref[pl.ds(first, window)] += dot_tn(ds, q2).reshape(shape)
    dv_ref[pl.ds(first, window)] += dot_tn(weights.astype(BF), do2).reshape(shape)

    @pl.when(number == pl.num_programs(1) - 1)
    def _():
        out_ref[:, 1, 0] = (dk_ref[...] * scale).astype(BF)
        out_ref[:, 2, 0] = dv_ref[...].astype(BF)


def attend_back(qkv, start, grad, window):
    blocks, _, rpg, t, _ = qkv.shape
    work = rpg * blocks * 2 * t * window * t
    return pl.pallas_call(
        functools.partial(backward_body, window),
        grid=(rpg, blocks),
        in_specs=attention_specs(blocks, t)
        + [pl.BlockSpec((1, 1, t, LANES), lambda r, i: (i, r, 0, 0))],
        out_specs=pl.BlockSpec((blocks, 3, 1, t, LANES), lambda r, i: (0, 0, r, 0, 0)),
        out_shape=jax.ShapeDtypeStruct((blocks, 3, rpg, t, LANES), BF),
        scratch_shapes=[
            pltpu.VMEM((blocks, t, LANES), F32),
            pltpu.VMEM((blocks, t, LANES), F32),
        ],
        cost_estimate=pl.CostEstimate(
            flops=10 * LANES * work, bytes_accessed=4 * qkv.size, transcendentals=work
        ),
        name="attend_back",
    )(qkv, qkv, qkv, start, grad)


def local(
    sizes,
    tokens_in,
    cotangent,
    segment_ids,
    attn_gain,
    attn_shift,
    qkv_weight,
    qkv_bias,
    out_weight,
    mlp_gain,
    mlp_shift,
    gate_weight,
    up_weight,
    down_weight,
):
    nz, ny, nx, nc = sizes
    seq, peers = nz * ny, nx * nc
    devices = seq * peers
    pair = nx == 2
    t, width = tokens_in.shape[1:]
    length = segment_ids.shape[1]
    heads = width // HEAD_DIM // peers
    pairs = heads // 2
    groups = seq // pairs
    rpg = peers // groups
    ff = down_weight.shape[0] * devices
    strip = ff // devices
    own_head = width // devices == HEAD_DIM
    window = min((length // 3 - 1 + t - 1) // t + 1, length // t)
    me_seq = lax.axis_index(SEQ)
    me_peer = lax.axis_index(BATCH)

    small = jnp.concatenate([attn_gain, attn_shift, mlp_gain, mlp_shift, qkv_bias])
    small = jnp.broadcast_to(small[None], (devices, small.size))
    small = lax.all_to_all(small, ALL, split_axis=0, concat_axis=0, tiled=True).astype(F32)
    each = attn_gain.size
    gain_one, shift_one, gain_two, shift_two = [
        small[:, i * each : (i + 1) * each].reshape(1, width) for i in range(4)
    ]
    bias = small[:, 4 * each :].reshape(3, heads, peers, HEAD_DIM)
    bias = lax.dynamic_index_in_dim(bias, me_peer, 2, keepdims=False).reshape(1, -1)

    rows = qkv_weight.shape[0]
    qkv_mine = qkv_weight.reshape(rows, 3, heads, peers, HEAD_DIM).transpose(3, 0, 1, 2, 4)
    qkv_mine = swap_batch(qkv_mine.reshape(peers, rows, -1)).reshape(peers * rows, -1)
    qkv_full = gather_seq(qkv_mine, ny)
    if own_head:
        out_full = gather_seq(out_weight, ny)
    else:
        out_full = lax.all_gather(out_weight, ALL, axis=0, tiled=True)
        out_full = out_full.reshape(heads, peers, HEAD_DIM, width)
        out_full = lax.dynamic_index_in_dim(out_full, me_peer, 1, keepdims=False)
        out_full = out_full.reshape(heads * HEAD_DIM, width)

    def columns(w):
        w = w.reshape(rows, seq, peers, strip).transpose(2, 0, 1, 3)
        w = swap_batch(w.reshape(peers, rows, -1))
        return gather_seq(w.reshape(peers * rows, -1), ny)

    gate_full = columns(gate_weight)
    up_full = columns(up_weight)
    down_full = gather_seq(down_weight, ny)

    segment = gather_batch(segment_ids, pair)
    start = jnp.zeros_like(segment)
    for doc in range(DOCS):
        count = jnp.sum((segment == doc).astype(jnp.int32), axis=1, keepdims=True)
        start = start + jnp.where(segment > doc, count, 0)
    places = me_seq * t + jnp.arange(t, dtype=jnp.int32)
    here = places[None] - lax.dynamic_slice_in_dim(start, me_seq * t, t, 1)
    half = ROT // 2
    inverse = 10000.0 ** (-jnp.arange(half, dtype=F32) / half)
    theta = inverse[:, None] * here.reshape(1, -1).astype(F32)
    cosine, sine = jnp.cos(theta), jnp.sin(theta)
    rest = jnp.ones((HEAD_DIM - ROT, theta.shape[1]), F32)
    cosine = jnp.concatenate([cosine, cosine, rest] * 2, axis=0).T
    sine = jnp.concatenate([-sine, sine, 0.0 * rest] * 2, axis=0).T
    start = lax.dynamic_slice_in_dim(start, (me_seq % groups) * rpg, rpg, 0)
    start = start.reshape(rpg, length // t, t, 1)

    inputs = tokens_in[0].astype(F32)
    unit_one, scale_one = norm_stats(inputs)
    normed = (unit_one * gain_one + shift_one).astype(BF)
    normed_all = gather_batch(normed, pair)
    proj = dot(normed_all, qkv_full)
    qkv = rotary_out(proj, bias, cosine, sine, pairs, rpg, t)
    qkv = swap_seq(qkv)
    mixed = swap_seq(attend(qkv, start, window))

    def token_rows(x):
        x = x.reshape(pairs, groups * rpg * t, LANES).transpose(1, 0, 2)
        return x.reshape(groups * rpg * t, pairs * LANES)

    def head_rows(x):
        x = x.reshape(groups * rpg * t, pairs, LANES).transpose(1, 0, 2)
        return x.reshape(seq, rpg, t, LANES)

    mixed = token_rows(mixed)
    hidden = inputs + reduce_batch(dot(mixed, out_full, BF), pair)

    unit_two, scale_two = norm_stats(hidden)
    normed_two = (unit_two * gain_two + shift_two).astype(BF)
    normed_two_all = gather_batch(normed_two, pair)
    grad_output = cotangent[0]
    grad_all = gather_batch(grad_output, pair)
    gate = dot(normed_two_all, gate_full)
    up = dot(normed_two_all, up_full)
    sigmoid = jax.nn.sigmoid(gate)
    act = (gate * sigmoid * up).astype(BF)
    block_out = hidden + reduce_batch(dot(act, down_full, BF), pair)
    block_out = block_out.astype(BF).reshape(tokens_in.shape)

    grad_down = reduce_seq(dot_tn(act, grad_all, BF), nz, ny).astype(F32)
    grad_act = dot_nt(grad_all, down_full)
    grad_gate = (grad_act * up * sigmoid * (1.0 + gate * (1.0 - sigmoid))).astype(BF)
    grad_up = (grad_act * gate * sigmoid).astype(BF)
    part = dot_nt(grad_gate, gate_full) + dot_nt(grad_up, up_full)
    grad_normed_two = reduce_batch(part.astype(BF), pair)

    def uncolumns(g):
        g = reduce_seq(g, nz, ny).reshape(peers, rows, -1)
        return swap_batch(g)

    def ff_columns(g):
        g = uncolumns(g).reshape(peers, rows, seq, strip).transpose(1, 2, 0, 3)
        return g.reshape(rows, ff).astype(F32)

    grad_gate_w = ff_columns(dot_tn(normed_two_all, grad_gate, BF))
    grad_up_w = ff_columns(dot_tn(normed_two_all, grad_up, BF))
    back, grad_gain_two, grad_shift_two = norm_back(grad_normed_two, unit_two, scale_two, gain_two)
    grad_hidden = grad_output.astype(F32) + back

    branch = gather_batch(grad_hidden.astype(BF), pair)
    grad_out = dot_tn(mixed, branch, BF)
    if own_head:
        grad_out = reduce_seq(grad_out, nz, ny).astype(F32)
    else:
        mine = (jnp.arange(peers) == me_peer).astype(BF)[None, :, None, None]
        grad_out = grad_out.reshape(heads, 1, HEAD_DIM, width) * mine
        grad_out = lax.psum_scatter(
            grad_out.reshape(width, width), ALL, scatter_dimension=0, tiled=True
        ).astype(F32)
    grad_mixed = head_rows(dot_nt(branch, out_full, BF))
    grad_qkv = attend_back(qkv, start, swap_seq(grad_mixed), window)
    grad_proj = rotary_in(swap_seq(grad_qkv), cosine, sine, pairs)
    grad_qkv_w = uncolumns(dot_tn(normed_all, grad_proj, BF))
    grad_qkv_w = grad_qkv_w.reshape(peers, rows, 3, heads, HEAD_DIM).transpose(1, 2, 3, 0, 4)
    grad_qkv_w = grad_qkv_w.reshape(rows, 3 * width).astype(F32)
    grad_bias = jnp.sum(grad_proj.astype(F32), axis=0).reshape(3, heads, 1, HEAD_DIM)
    mine = (jnp.arange(peers) == me_peer).astype(F32)[None, None, :, None]
    grad_bias = (grad_bias * mine).reshape(devices, -1)
    grad_normed = reduce_batch(dot_nt(grad_proj, qkv_full, BF), pair)
    back, grad_gain_one, grad_shift_one = norm_back(grad_normed, unit_one, scale_one, gain_one)
    grad_tokens = (grad_hidden + back).astype(BF).reshape(tokens_in.shape)

    vectors = [grad_gain_one, grad_shift_one, grad_gain_two, grad_shift_two]
    vectors = [v.reshape(devices, each) for v in vectors] + [grad_bias]
    vectors = jnp.concatenate(vectors, axis=1)
    vectors = lax.all_to_all(vectors, ALL, split_axis=0, concat_axis=0, tiled=True)
    vectors = jnp.sum(vectors, axis=0)
    g1, s1, g2, s2 = [vectors[i * each : (i + 1) * each] for i in range(4)]
    return (
        block_out,
        grad_tokens,
        g1,
        s1,
        grad_qkv_w,
        vectors[4 * each :],
        grad_out,
        g2,
        s2,
        grad_gate_w,
        grad_up_w,
        grad_down,
    )


def solution(mesh):
    seq, batch = mesh.shape["seq"], mesh.shape["batch"]
    sizes = (4, seq // 4, batch // 2, 2)
    fine = Mesh(mesh.devices.reshape(sizes), ALL)
    token = P(BATCH, SEQ, None)
    vector = P(ALL)
    matrix = P(ALL, None)
    return jax.shard_map(
        functools.partial(local, sizes),
        mesh=fine,
        in_specs=(
            token,
            token,
            P(BATCH, None),
            vector,
            vector,
            matrix,
            vector,
            matrix,
            vector,
            vector,
            matrix,
            matrix,
            matrix,
        ),
        out_specs=(
            token,
            token,
            vector,
            vector,
            matrix,
            vector,
            matrix,
            vector,
            vector,
            matrix,
            matrix,
            matrix,
        ),
        check_vma=False,
    )
```

time: 3160 us -> 1220 us (0.39)
  waiting for transfers between devices: 2320 us -> 701 us
  matrix products: 460 us -> 138 us
  blocking collectives: 125 us -> 15.8 us
  Pallas kernels: 0 us -> 105 us
  starting transfers between devices: 34 us -> 81.1 us
    reduce_scatter x5, waiting for transfers between devices: 1740 us -> 0.03 us  [reduce_seq(): lax.psum_scatter(both.reshape((nz * rows,) + both.shape[2:]), 'z', scatte...]
    ppermute x0 -> x28, waiting for transfers between devices: none -> 463 us  [the longest x5 250 us: reduce_seq(): got = lax.ppermute(send, 'y', SWAP)]
    dot_general x43 -> x15, matrix products: 460 us -> 138 us  [the longest x5 50.4 us: dot(): return jnp.dot(a, b, preferred_element_type=out)]
    all_gather x5, waiting for transfers between devices: 365 us -> 55.4 us  [gather_seq(): near = lax.all_gather(w, 'z', axis=0, tiled=True)]
    pallas_call x0 -> x4, Pallas kernels: none -> 105 us  [the longest x1 40.7 us: attend_back(): pl.pallas_call(functools.partial(backward_body, window), grid=(rpg, block...]
    unnamed x2 -> x0, blocking collectives: 86 us -> none
    all_to_all x7 -> x11, waiting for transfers between devices: 210 us -> 180 us  [the longest x4 149 us: swap_seq(): return lax.all_to_all(x, SEQ, split_axis=0, concat_axis=0, tiled=True)]
  transfers between devices with their start and end apart: 17 -> 49, of which waited for: 14 -> 23; matrix products, arithmetic and copies ran while one was open for 18% -> 18% of each run, Pallas kernels for 0% -> 9%
where the time goes in v1:
time: 1220 us
  waiting for transfers between devices  701 us (57%)
  matrix products  138 us (11%)
  Pallas kernels  105 us (9%)
  local copies, waits for them, and re-layouts  81.7 us (7%)
  starting transfers between devices  81.1 us (7%)
  other arithmetic  78.1 us (6%)
  blocking collectives  15.8 us (1%)
  between operations  15.6 us (1%)
    ppermute x5, waiting for transfers between devices, reduce_seq(): got = lax.ppermute(send, 'y', SWAP)  250 us
    all_to_all x4, waiting for transfers between devices, swap_seq(): return lax.all_to_all(x, SEQ, split_axis=0, concat_axis=0, tiled=True)  149 us
    ppermute x5, waiting for transfers between devices, gather_seq(): far = lax.ppermute(near, 'y', SWAP)  97.8 us
    ppermute x4, waiting for transfers between devices, reduce_batch(): last = lax.ppermute(send, 'x', SWAP)  59.2 us
    all_gather x5, waiting for transfers between devices, gather_seq(): near = lax.all_gather(w, 'z', axis=0, tiled=True)  55.4 us
    ppermute x5, waiting for transfers between devices, gather_batch(): other = lax.ppermute(x, 'x', SWAP)  53.7 us
    dot_general x5, matrix products, dot(): return jnp.dot(a, b, preferred_element_type=out)  50.4 us
    dot_general x5, matrix products, dot_nt(): lax.dot_general(a, b, (((1,), (1,)), ((), ())), preferred_element_type=out)  44.9 us
  transfers between devices with their start and end apart: 49, of which 23 were waited for; matrix products, arithmetic and copies ran while one was open for 18% of the time, Pallas kernels for 9%

profile of v1, /device:TPU:0, one launch (start us, length us, event | category | flops | bytes accessed | tf_op | source)
XLA Modules:
  0.0 1216.6 jit_solution(4998966144407104119)
XLA Ops:
  13.3 15.8 %all_to_all.65 = bf16[4,64,1536]{2,1,0:T(8,128)(2,1)} all-to-all(bf16[4,64,1536]{2,1,0:T(8,128)(2,1)S(1)} %reshape.498), channel_id=1, replica_groups=mesh['z'=4,'y'=2,'x'=2,'c'=2] {'x','c'}, dimensions={0} | all-to-all | bytes 1572864 | tf_op jit(solution)/shard_map/all_to_all | solution.py:88
  38.1 55.4 %all-gather.6.cloned.1.call-done = bf16[1024,1536]{1,0:T(8,128)(2,1)} async-done(((bf16[256,1536]{1,0:T(8,128)(2,1)}), bf16[1024,1536]{1,0:T(8,128)(2,1)}) %all-gather.6.cloned.1.call-update) | async-done | bytes 3145744 | tf_op jit(solution)/shard_map/all_gather | solution.py:57
  108.1 15.2 %collective-permute-done.3 = s32[1,2048]{1,0:T(1,128)S(1)} collective-permute-done((s32[1,2048]{1,0:T(1,128)S(1)}, s32[1,2048]{1,0:T(1,128)S(1)}, u32[]{:S(2)}, u32[]{:S(2)}) %collective-permute-start.3) | collective-permute-done | bytes 8224 | tf_op jit(solution)/shard_map/ppermute | solution.py:40
  134.5 29.1 %collective-permute-done.2 = bf16[1024,1536]{1,0:T(8,128)(2,1)} collective-permute-done((bf16[1024,1536]{1,0:T(8,128)(2,1)}, bf16[1024,1536]{1,0:T(8,128)(2,1)}, u32[]{:S(2)}, u32[]{:S(2)}) %collective-permute-start.2) | collective-permute-done | bytes 3145760 | tf_op jit(solution)/shard_map/ppermute | solution.py:61
  167.5 13.0 %fusion.29.proj_ref = f32[1024,1536]{1,0:T(8,128)} fusion(bf16[2048,1536]{1,0:T(8,128)(2,1)S(1)} %bitcast.186, bf16[512,2048]{1,0:T(8,128)(2,1)} %collective-permute-done.1, bf16[256,2048]{1,0:T(8,128)(2,1)} %collective-permute-done, bf16[256,2048]{1,0:T(8,128)(2,1)} %fusion.17), kind=kOutput, calls=%fused_computation.82 | convolution fusion | flops 6455033856 | bytes 16777216 | tf_op jit(solution)/shard_map/dot_general | solution.py:26
  180.6 17.3 %rotary_out.1 = bf16[8,3,2,256,128]{4,3,2,1,0:T(8,128)(2,1)} custom-call(f32[1024,1536]{1,0:T(8,128)} %fusion.29.proj_ref, f32[1,1536]{1,0:T(1,128)} %reshape.502.bias_ref, f32[1024,128]{1,0:T(8,128)} %bitcast.205, f32[1024,128]{1,0:T(8,128)} %bitcast.207), custom_call_target="tpu_custom_call" | custom-call | flops 9437184 | bytes 9437184 | tf_op jit(solution)/shard_map/rotary_out/pallas_call | solution.py:127
  207.3 111.6 %all-to-all-done.2.q_ref.k_ref.v_ref = bf16[8,3,2,256,128]{4,3,2,1,0:T(8,128)(2,1)} async-done(((bf16[8,3,2,256,128]{4,3,2,1,0:T(8,128)(2,1)}), bf16[8,3,2,256,128]{4,3,2,1,0:T(8,128)(2,1)}, u32[]{:S(2)}, u32[]{:S(2)}) %all-to-all-start.2) | async-done | bytes 3145760 | tf_op jit(solution)/shard_map/all_to_all | solution.py:92
  327.2 30.5 %attend.1 = bf16[8,2,256,128]{3,2,1,0:T(8,128)(2,1)} custom-call(bf16[8,3,2,256,128]{4,3,2,1,0:T(8,128)(2,1)} %all-to-all-done.2.q_ref.k_ref.v_ref, bf16[8,3,2,256,128]{4,3,2,1,0:T(8,128)(2,1)} %all-to-all-done.2.q_ref.k_ref.v_ref, bf16[8,3,2,256,128]{4,3,2,1,0:T(8,128)(2,1)} %all-to-all-done.2.q_ref.k_ref.v_ref, s32[2,8,256,1]{3,2,1,0:T(8,128)} %reshape.549.start_ref), custom_call_target="tpu_custom_call" | custom-call | flops 4294967296 | bytes 6291456 | tf_op jit(solution)/shard_map/attend/pallas_call | solution.py:223
  367.5 37.2 %all-to-all-done.3 = bf16[8,2,256,128]{3,2,1,0:T(8,128)(2,1)S(1)} async-done(((bf16[8,2,256,128]{3,2,1,0:T(8,128)(2,1)}), bf16[8,2,256,128]{3,2,1,0:T(8,128)(2,1)S(1)}, u32[]{:S(2)}, u32[]{:S(2)}) %all-to-all-start.3) | async-done | bytes 1048608 | tf_op jit(solution)/shard_map/all_to_all | solution.py:92
  415.9 23.6 %collective-permute-done.15 = bf16[256,2048]{1,0:T(8,128)(2,1)S(1)} collective-permute-done((bf16[256,2048]{1,0:T(8,128)(2,1)S(1)}, bf16[256,2048]{1,0:T(8,128)(2,1)S(1)}, u32[]{:S(2)}, u32[]{:S(2)}) %collective-permute-start.15) | collective-permute-done | bytes 1048608 | tf_op jit(solution)/shard_map/ppermute | solution.py:40
  449.8 20.6 %collective-permute-done.7 = bf16[256,2048]{1,0:T(8,128)(2,1)S(1)} collective-permute-done((bf16[256,2048]{1,0:T(8,128)(2,1)S(1)}, bf16[256,2048]{1,0:T(8,128)(2,1)S(1)}, u32[]{:S(2)}, u32[]{:S(2)}) %collective-permute-start.7) | collective-permute-done | bytes 1048608 | tf_op jit(solution)/shard_map/ppermute | solution.py:52
  484.7 13.1 %collective-permute-done.8 = bf16[256,2048]{1,0:T(8,128)(2,1)S(1)} collective-permute-done((bf16[256,2048]{1,0:T(8,128)(2,1)S(1)}, bf16[256,2048]{1,0:T(8,128)(2,1)S(1)}, u32[]{:S(2)}, u32[]{:S(2)}) %collective-permute-start.8) | collective-permute-done | bytes 1048608 | tf_op jit(solution)/shard_map/ppermute | solution.py:40
  506.8 61.3 %collective-permute-done.11 = bf16[1024,1408]{1,0:T(8,128)(2,1)} collective-permute-done((bf16[1024,1408]{1,0:T(8,128)(2,1)}, bf16[1024,1408]{1,0:T(8,128)(2,1)}, u32[]{:S(2)}, u32[]{:S(2)}) %collective-permute-start.11) | collective-permute-done | bytes 2883616 | tf_op jit(solution)/shard_map/ppermute | solution.py:61
  584.8 16.5 %multiply_convert_fusion.1 = (bf16[1024,1408]{1,0:T(8,128)(2,1)}, bf16[1024,1408]{1,0:T(8,128)(2,1)}, bf16[1024,1408]{1,0:T(8,128)(2,1)}) fusion(f32[1024,1408]{1,0:T(8,128)} %fusion.27, f32[1024,1408]{1,0:T(8,128)} %fusion.43, bf16[2048,1408]{1,0:T(8,128)(2,1)} %bitcast.201, bf16[512,2048]{1,0:T(8,128)(2,1)} %collective-permute-done.9, ...), kind=kOutput, calls=%fused_computation.15 | convolution fusion | flops 5941231616 | bytes 30146560 | tf_op jit(solution)/shard_map/dot_general | solution.py:26
  611.7 10.8 add_convert_fusion
  649.1 19.3 %collective-permute-done.18 = bf16[256,2048]{1,0:T(8,128)(2,1)S(1)} collective-permute-done((bf16[256,2048]{1,0:T(8,128)(2,1)S(1)}, bf16[256,2048]{1,0:T(8,128)(2,1)S(1)}, u32[]{:S(2)}, u32[]{:S(2)}) %collective-permute-start.18) | collective-permute-done | bytes 1048608 | tf_op jit(solution)/shard_map/ppermute | solution.py:52
  670.2 19.4 %collective-permute-done.14 = bf16[256,2048]{1,0:T(8,128)(2,1)S(1)} collective-permute-done((bf16[256,2048]{1,0:T(8,128)(2,1)S(1)}, bf16[256,2048]{1,0:T(8,128)(2,1)S(1)}, u32[]{:S(2)}, u32[]{:S(2)}) %collective-permute-start.14) | collective-permute-done | bytes 1048608 | tf_op jit(solution)/shard_map/ppermute | solution.py:52
  694.6 15.4 %collective-permute-done.26 = bf16[4,256,1408]{2,1,0:T(8,128)(2,1)} collective-permute-done((bf16[4,256,1408]{2,1,0:T(8,128)(2,1)}, bf16[4,256,1408]{2,1,0:T(8,128)(2,1)}, u32[]{:S(2)}, u32[]{:S(2)}) %collective-permute-start.26) | collective-permute-done | bytes 2883616 | tf_op jit(solution)/shard_map/ppermute | solution.py:79
  744.7 60.5 %collective-permute-done.25 = bf16[4,256,1408]{2,1,0:T(8,128)(2,1)} collective-permute-done((bf16[4,256,1408]{2,1,0:T(8,128)(2,1)}, bf16[4,256,1408]{2,1,0:T(8,128)(2,1)}, u32[]{:S(2)}, u32[]{:S(2)}) %collective-permute-start.25) | collective-permute-done | bytes 2883616 | tf_op jit(solution)/shard_map/ppermute | solution.py:79
  811.3 40.7 %attend_back.1 = bf16[8,3,2,256,128]{4,3,2,1,0:T(8,128)(2,1)} custom-call(bf16[8,3,2,256,128]{4,3,2,1,0:T(8,128)(2,1)} %all-to-all-done.2.q_ref.k_ref.v_ref, bf16[8,3,2,256,128]{4,3,2,1,0:T(8,128)(2,1)} %all-to-all-done.2.q_ref.k_ref.v_ref, bf16[8,3,2,256,128]{4,3,2,1,0:T(8,128)(2,1)} %all-to-all-done.2.q_ref.k_ref.v_ref, ...), custom_call_target="tpu_custom_call" | custom-call | flops 10737418240 | bytes 6291456 | tf_op jit(solution)/shard_map/attend_back/pallas_call | solution.py:269
  870.8 85.8 %collective-permute-done.27 = bf16[4,176,2048]{2,1,0:T(8,128)(2,1)S(1)} collective-permute-done((bf16[4,176,2048]{2,1,0:T(8,128)(2,1)S(1)}, bf16[4,176,2048]{2,1,0:T(8,128)(2,1)S(1)}, u32[]{:S(2)}, u32[]{:S(2)}) %collective-permute-start.27) | collective-permute-done | bytes 2883616 | tf_op jit(solution)/shard_map/ppermute | solution.py:79
  967.1 16.7 %rotary_in.1 = bf16[1024,1536]{1,0:T(8,128)(2,1)} custom-call(bf16[8,3,2,256,128]{4,3,2,1,0:T(8,128)(2,1)} %copy-done.3, f32[1024,128]{1,0:T(8,128)} %bitcast.206, f32[1024,128]{1,0:T(8,128)} %bitcast.208), custom_call_target="tpu_custom_call" | custom-call | flops 9437184 | bytes 6291456 | tf_op jit(solution)/shard_map/rotary_in/pallas_call | solution.py:156
  998.4 88.7 %collective-permute-done.24 = bf16[4,64,2048]{2,1,0:T(8,128)(2,1)S(1)} collective-permute-done((bf16[4,64,2048]{2,1,0:T(8,128)(2,1)S(1)}, bf16[4,64,2048]{2,1,0:T(8,128)(2,1)S(1)}, u32[]{:S(2)}, u32[]{:S(2)}) %collective-permute-start.24) | collective-permute-done | bytes 1048608 | tf_op jit(solution)/shard_map/ppermute | solution.py:79
  1141.2 11.8 all-to-all-done.10
  (321 shorter events, 371.9 us)
Async XLA Ops:
  7.2 86.4 %all-gather.6.cloned.1.call-start = ((), (), s32[]{:S(2)}) async-start(), calls=%async_computation.17 | async-start | bytes 3932160 | tf_op jit(solution)/shard_map/all_gather | solution.py:57
  36.7 289.0 %all-gather.8.cloned.1.call-start = ((), (), s32[]{:S(2)}) async-start(), calls=%async_computation.18 | async-start | bytes 1310720 | tf_op jit(solution)/shard_map/all_gather | solution.py:57
  93.6 70.1 %collective-permute-start.2 = (bf16[1024,1536]{1,0:T(8,128)(2,1)}, bf16[1024,1536]{1,0:T(8,128)(2,1)}, u32[]{:S(2)}, u32[]{:S(2)}) collective-permute-start(bf16[1024,1536]{1,0:T(8,128)(2,1)} %all-gather.6.cloned.1.call-done), channel_id=1, source_target_pairs={{0,4},{4,0},{1,5},{5,1},{2,6},{6,2},{3,7},{7,3},{8,12},{12,8},{9,1... | collective-permute-start | bytes 9437192 | tf_op jit(solution)/shard_map/ppermute | solution.py:61
  103.1 94.7 %all-to-all-start.4 = ((bf16[4,64,1408]{2,1,0:T(8,128)(2,1)}), bf16[4,64,1408]{2,1,0:T(8,128)(2,1)}, u32[]{:S(2)}, u32[]{:S(2)}) async-start(bf16[4,64,1408]{2,1,0:T(8,128)(2,1)} %reshape.508), calls=%async_computation.4 | async-start | bytes 1441792 | tf_op jit(solution)/shard_map/all_to_all | solution.py:88
  107.3 258.3 %all-gather.14.cloned.1.call-start = ((), (), s32[]{:S(2)}) async-start(), calls=%async_computation.21 | async-start | bytes 3604480 | tf_op jit(solution)/shard_map/all_gather | solution.py:57
  197.8 121.0 %all-to-all-start.2 = ((bf16[8,3,2,256,128]{4,3,2,1,0:T(8,128)(2,1)}), bf16[8,3,2,256,128]{4,3,2,1,0:T(8,128)(2,1)}, u32[]{:S(2)}, u32[]{:S(2)}) async-start(bf16[8,3,2,256,128]{4,3,2,1,0:T(8,128)(2,1)} %rotary_out.1), calls=%async_computation.2 | async-start | bytes 6291456 | tf_op jit(solution)/shard_map/all_to_all | solution.py:92
  202.4 238.7 %all-gather.10.cloned.1.call-start = ((), (), s32[]{:S(2)}) async-start(), calls=%async_computation.19 | async-start | bytes 3604480 | tf_op jit(solution)/shard_map/all_gather | solution.py:57
  361.3 81.6 %all-gather.12.cloned.1.call-start = ((), (), s32[]{:S(2)}) async-start(), calls=%async_computation.20 | async-start | bytes 3604480 | tf_op jit(solution)/shard_map/all_gather | solution.py:57
  361.9 746.4 %reduce-scatter.12.cloned.1.call-start = ((), (), s32[]{:S(2)}) async-start(), calls=%async_computation.25 | async-start | bytes 3604480 | tf_op jit(solution)/shard_map/reduce_scatter | solution.py:82
  365.6 81.5 %collective-permute-start.12 = (bf16[704,2048]{1,0:T(8,128)(2,1)}, bf16[704,2048]{1,0:T(8,128)(2,1)}, u32[]{:S(2)}, u32[]{:S(2)}) collective-permute-start(bf16[704,2048]{1,0:T(8,128)(2,1)} %all-gather.14.cloned.1.call-done), channel_id=1, source_target_pairs={{0,4},{4,0},{1,5},{5,1},{2,6},{6,2},{3,7},{7,3},{8,12},{12,8},{9,1... | collective-permute-start | bytes 8650760 | tf_op jit(solution)/shard_map/ppermute | solution.py:61
  441.2 65.7 %collective-permute-start.10 = (bf16[1024,1408]{1,0:T(8,128)(2,1)}, bf16[1024,1408]{1,0:T(8,128)(2,1)}, u32[]{:S(2)}, u32[]{:S(2)}) collective-permute-start(bf16[1024,1408]{1,0:T(8,128)(2,1)} %all-gather.10.cloned.1.call-done), channel_id=1, source_target_pairs={{0,4},{4,0},{1,5},{5,1},{2,6},{6,2},{3,7},{7,3},{8,12},{12,8},{9,1... | collective-permute-start | bytes 8650760 | tf_op jit(solution)/shard_map/ppermute | solution.py:61
  442.9 125.3 %collective-permute-start.11 = (bf16[1024,1408]{1,0:T(8,128)(2,1)}, bf16[1024,1408]{1,0:T(8,128)(2,1)}, u32[]{:S(2)}, u32[]{:S(2)}) collective-permute-start(bf16[1024,1408]{1,0:T(8,128)(2,1)} %all-gather.12.cloned.1.call-done), channel_id=1, source_target_pairs={{0,4},{4,0},{1,5},{5,1},{2,6},{6,2},{3,7},{7,3},{8,12},{12,8},{9,1... | collective-permute-start | bytes 8650760 | tf_op jit(solution)/shard_map/ppermute | solution.py:61
  499.5 75.6 %collective-permute-start.9 = (bf16[512,2048]{1,0:T(8,128)(2,1)}, bf16[512,2048]{1,0:T(8,128)(2,1)}, u32[]{:S(2)}, u32[]{:S(2)}) collective-permute-start(bf16[512,2048]{1,0:T(8,128)(2,1)} %pad_maximum_fusion.10), channel_id=1, source_target_pairs={{0,1},{1,0},{2,3},{3,2},{4,5},{5,4},{6,7},{7,6},{8,9},{9,8},{10,11... | collective-permute-start | bytes 6291464 | tf_op jit(solution)/shard_map/ppermute | solution.py:42
  645.9 64.1 %collective-permute-start.26 = (bf16[4,256,1408]{2,1,0:T(8,128)(2,1)}, bf16[4,256,1408]{2,1,0:T(8,128)(2,1)}, u32[]{:S(2)}, u32[]{:S(2)}) collective-permute-start(bf16[4,256,1408]{2,1,0:T(8,128)(2,1)} %dynamic-slice_bitcast_fusion.2), channel_id=1, source_target_pairs={{0,4},{4,0},{1,5},{5,1},{2,6},{6,2},{3,7},{7,3},{8,12},{12,8},{9,1... | collective-permute-start | bytes 8650760 | tf_op jit(solution)/shard_map/ppermute | solution.py:79
  731.1 74.1 %collective-permute-start.25 = (bf16[4,256,1408]{2,1,0:T(8,128)(2,1)}, bf16[4,256,1408]{2,1,0:T(8,128)(2,1)}, u32[]{:S(2)}, u32[]{:S(2)}) collective-permute-start(bf16[4,256,1408]{2,1,0:T(8,128)(2,1)} %dynamic-slice_bitcast_fusion.3), channel_id=1, source_target_pairs={{0,4},{4,0},{1,5},{5,1},{2,6},{6,2},{3,7},{7,3},{8,12},{12,8},{9,1... | collective-permute-start | bytes 8650760 | tf_op jit(solution)/shard_map/ppermute | solution.py:79
  738.3 72.0 %all-to-all-start.6 = ((bf16[8,2,256,128]{3,2,1,0:T(8,128)(2,1)}), bf16[8,2,256,128]{3,2,1,0:T(8,128)(2,1)S(1)}, u32[]{:S(2)}, u32[]{:S(2)}) async-start(bf16[8,2,256,128]{3,2,1,0:T(8,128)(2,1)} %bitcast.34), calls=%async_computation.6 | async-start | bytes 2097152 | tf_op jit(solution)/shard_map/all_to_all | solution.py:92
  744.7 373.0 %reduce-scatter.10.cloned.1.call-start = ((), (), s32[]{:S(2)}) async-start(), calls=%async_computation.24 | async-start | bytes 3604480 | tf_op jit(solution)/shard_map/reduce_scatter | solution.py:82
  851.9 113.6 %all-to-all-start.7 = ((bf16[8,3,2,256,128]{4,3,2,1,0:T(8,128)(2,1)}), bf16[8,3,2,256,128]{4,3,2,1,0:T(8,128)(2,1)S(1)}, u32[]{:S(2)}, u32[]{:S(2)}) async-start(bf16[8,3,2,256,128]{4,3,2,1,0:T(8,128)(2,1)} %attend_back.1), calls=%async_computation.7 | async-start | bytes 6291456 | tf_op jit(solution)/shard_map/all_to_all | solution.py:92
  859.3 270.3 %reduce-scatter.14.cloned.1.call-start = ((), (), s32[]{:S(2)}) async-start(), calls=%async_computation.26 | async-start | bytes 3604480 | tf_op jit(solution)/shard_map/reduce_scatter | solution.py:82
  868.7 87.8 %collective-permute-start.27 = (bf16[4,176,2048]{2,1,0:T(8,128)(2,1)S(1)}, bf16[4,176,2048]{2,1,0:T(8,128)(2,1)S(1)}, u32[]{:S(2)}, u32[]{:S(2)}) collective-permute-start(bf16[4,176,2048]{2,1,0:T(8,128)(2,1)S(1)} %dynamic-slice_bitcast_fusion.1), channel_id=1, source_target_pairs={{0,4},{4,0},{1,5},{5,1},{2,6},{6,2},{3,7},{7,3},{8,12},{12,8},{9,1... | collective-permute-start | bytes 8650760 | tf_op jit(solution)/shard_map/ppermute | solution.py:79
  959.3 202.8 %reduce-scatter.8.cloned.1.call-start = ((), (), s32[]{:S(2)}) async-start(), calls=%async_computation.23 | async-start | bytes 1310720 | tf_op jit(solution)/shard_map/reduce_scatter | solution.py:82
  996.2 92.3 %collective-permute-start.23 = (bf16[4,256,1536]{2,1,0:T(8,128)(2,1)S(1)}, bf16[4,256,1536]{2,1,0:T(8,128)(2,1)}, u32[]{:S(2)}, u32[]{:S(2)}) collective-permute-start(bf16[4,256,1536]{2,1,0:T(8,128)(2,1)S(1)} %dynamic-slice_bitcast_fusion), channel_id=1, source_target_pairs={{0,4},{4,0},{1,5},{5,1},{2,6},{6,2},{3,7},{7,3},{8,12},{12,8},{9,1... | collective-permute-start | bytes 9437192 | tf_op jit(solution)/shard_map/ppermute | solution.py:79
  996.6 90.5 %collective-permute-start.24 = (bf16[4,64,2048]{2,1,0:T(8,128)(2,1)S(1)}, bf16[4,64,2048]{2,1,0:T(8,128)(2,1)S(1)}, u32[]{:S(2)}, u32[]{:S(2)}) collective-permute-start(bf16[4,64,2048]{2,1,0:T(8,128)(2,1)S(1)} %dynamic-slice_bitcast_fusion.4), channel_id=1, source_target_pairs={{0,4},{4,0},{1,5},{5,1},{2,6},{6,2},{3,7},{7,3},{8,12},{12,8},{9,1... | collective-permute-start | bytes 3145736 | tf_op jit(solution)/shard_map/ppermute | solution.py:79
  1088.5 94.3 %reduce-scatter.6.cloned.1.call-start = ((), (), s32[]{:S(2)}) async-start(), calls=%async_computation.22 | async-start | bytes 3932160 | tf_op jit(solution)/shard_map/reduce_scatter | solution.py:82
  (76 other events, 1510.3 us)
Sparse Core Ops, SparseCore 0:
  29.2 64.2 all-gather.5
  95.1 26.4 all-gather.7
  123.2 58.4 all-gather.13
  204.5 112.9 all-gather.9
  363.9 70.4 all-gather.11
  715.1 75.6 reduce-scatter.11
  810.4 64.1 reduce-scatter.9
  959.5 56.5 reduce-scatter.13
  1088.6 28.3 reduce-scatter.7
  1119.2 58.9 reduce-scatter.5

commit v2 on v1

--- a/solution.py
+++ b/solution.py
@@ -34,58 +34,80 @@
     return lax.dot_general(a, b, (((0,), (0,)), ((), ())), preferred_element_type=out)
 
 
-def gather_batch(x, pair):
-    if not pair:
+def after(x, *first):
+    return lax.optimization_barrier((x,) + first)[0]
+
+
+def gather_peers(x, axis):
+    if axis is None:
         return lax.all_gather(x, BATCH, axis=0, tiled=True)
-    other = lax.ppermute(x, "x", SWAP)
+    other = lax.ppermute(x, axis, SWAP)
     near = jnp.concatenate([x, other], axis=0)
     far = lax.ppermute(near, "c", SWAP)
     return jnp.concatenate([near, far], axis=0)
 
 
-def reduce_batch(part, pair):
-    if not pair:
+def reduce_peers(part, axis):
+    if axis is None:
         return lax.psum_scatter(part, BATCH, scatter_dimension=0, tiled=True).astype(F32)
     rows = part.shape[0] // 4
     got = lax.ppermute(part[2 * rows :], "c", SWAP)
     send = (part[rows : 2 * rows].astype(F32) + got[rows:].astype(F32)).astype(BF)
-    last = lax.ppermute(send, "x", SWAP)
+    last = lax.ppermute(send, axis, SWAP)
     return part[:rows].astype(F32) + got[:rows].astype(F32) + last.astype(F32)
 
 
-def gather_seq(w, ny):
-    near = lax.all_gather(w, "z", axis=0, tiled=True)
-    if ny != 2:
-        full = lax.all_gather(near.reshape((-1,) + w.shape), "y", axis=1)
-        return full.reshape((-1,) + w.shape[1:])
-    far = lax.ppermute(near, "y", SWAP)
-    near = near.reshape((-1, 1) + w.shape)
-    far = far.reshape((-1, 1) + w.shape)
-    first = lax.axis_index("y") == 0
+def gather_z(w):
+    return lax.all_gather(w, "z", axis=0, tiled=True)
+
+
+def gather_far(near, axis):
+    if axis is None:
+        return lax.all_gather(near, "y", axis=0)
+    return lax.ppermute(near, axis, SWAP)
+
+
+def merge_rows(near, far, axis, nz, inner=1):
+    wide = near.shape[-1]
+    if axis is None:
+        far = far.reshape(far.shape[0], nz, -1, wide).transpose(1, 0, 2, 3)
+        return far.reshape(-1, wide)
+    near = near.reshape(nz * inner, 1, -1, wide)
+    far = far.reshape(near.shape)
+    first = lax.axis_index(axis) == 0
     full = jnp.concatenate([jnp.where(first, near, far), jnp.where(first, far, near)], axis=1)
-    return full.reshape((-1,) + w.shape[1:])
-
-
-def reduce_seq(g, nz, ny):
-    rows = g.shape[0] // (nz * ny)
-    g = g.reshape((nz, ny, rows) + g.shape[1:])
-    if ny != 2:
-        g = lax.psum_scatter(g, "y", scatter_dimension=1, tiled=True)
-        return lax.psum_scatter(
-            g.reshape((nz * rows,) + g.shape[3:]), "z", scatter_dimension=0, tiled=True
-        )
-    here = lax.axis_index("y")
+    return full.reshape(-1, wide)
+
+
+def send_rows(g, axis, nz, na, inner=1):
+    rows = g.shape[0] // (nz * na)
+    if axis is None:
+        g = g.reshape(nz, na, rows, -1).transpose(1, 0, 2, 3).reshape(na, nz * rows, -1)
+        return None, lax.psum_scatter(g, "y", scatter_dimension=0, tiled=True)[0]
+    g = g.reshape(nz * inner, na, rows // inner, g.shape[1])
+    here = lax.axis_index(axis)
     send = lax.dynamic_index_in_dim(g, 1 - here, 1, keepdims=False)
-    got = lax.ppermute(send, "y", SWAP)
     keep = lax.dynamic_index_in_dim(g, here, 1, keepdims=False)
-    both = (keep.astype(F32) + got.astype(F32)).astype(BF)
-    return lax.psum_scatter(
-        both.reshape((nz * rows,) + both.shape[2:]), "z", scatter_dimension=0, tiled=True
-    )
-
-
-def swap_batch(x):
-    return lax.all_to_all(x, BATCH, split_axis=0, concat_axis=0, tiled=True)
+    return keep, lax.ppermute(send, axis, SWAP)
+
+
+def add_rows(keep, got):
+    if keep is None:
+        return got
+    got = (keep.astype(F32) + got.astype(F32)).astype(BF)
+    return got.reshape(-1, got.shape[-1])
+
+
+def scatter_z(g):
+    return lax.psum_scatter(g, "z", scatter_dimension=0, tiled=True)
+
+
+def reduce_z(keep, got):
+    return scatter_z(add_rows(keep, got))
+
+
+def swap_peers(x, axes):
+    return lax.all_to_all(x, axes, split_axis=0, concat_axis=0, tiled=True)
 
 
 def swap_seq(x):
@@ -113,61 +135,76 @@
     return value * cosine + jnp.where(inner < ROT // 2, ahead, behind) * sine
 
 
-def rotary_out_body(proj_ref, bias_ref, cos_ref, sin_ref, out_ref):
-    value = proj_ref[...] + bias_ref[...]
-    lane = lax.broadcasted_iota(jnp.int32, value.shape, 1)
-    turned = turn(value, cos_ref[...], sin_ref[...], lane)
-    value = jnp.where(pl.program_id(1) < 2, turned, value)
-    out_ref[...] = value.astype(BF).reshape(out_ref.shape)
-
-
-def rotary_out(proj, bias, cosine, sine, pairs, rpg, t):
-    groups = proj.shape[0] // (rpg * t)
-    block = rpg * t
-    return pl.pallas_call(
-        rotary_out_body,
-        grid=(pairs * groups, 3),
+def rotary_out_body(turned, proj_ref, bias_ref, cos_ref, sin_ref, out_ref):
+    pairs = out_ref.shape[0]
+    cosine, sine = cos_ref[...], sin_ref[...]
+    lane = lax.broadcasted_iota(jnp.int32, cosine.shape, 1)
+    rotate = pl.program_id(1) < turned
+    for i in range(pairs):
+        at = slice(i * LANES, (i + 1) * LANES)
+        value = proj_ref[:, at] + bias_ref[:, at]
+        value = jnp.where(rotate, turn(value, cosine, sine, lane), value)
+        out_ref[i] = value.astype(BF).reshape(out_ref.shape[1:])
+
+
+def rotary_out(proj, bias, cosine, sine, pairs, rpg, t, turned):
+    peers = proj.shape[0] // t
+    groups = peers // rpg
+    wide = pairs * LANES
+    parts = proj.shape[1] // wide
+    out = pl.pallas_call(
+        functools.partial(rotary_out_body, turned),
+        grid=(peers, parts),
         in_specs=[
-            pl.BlockSpec((block, LANES), lambda d, p: (d % groups, p * pairs + d // groups)),
-            pl.BlockSpec((1, LANES), lambda d, p: (0, p * pairs + d // groups)),
-            pl.BlockSpec((block, LANES), lambda d, p: (d % groups, 0)),
-            pl.BlockSpec((block, LANES), lambda d, p: (d % groups, 0)),
+            pl.BlockSpec((t, wide), lambda b, p: (b, p)),
+            pl.BlockSpec((1, wide), lambda b, p: (0, p)),
+            pl.BlockSpec((t, LANES), lambda b, p: (b, 0)),
+            pl.BlockSpec((t, LANES), lambda b, p: (b, 0)),
         ],
-        out_specs=pl.BlockSpec((1, 1, rpg, t, LANES), lambda d, p: (d, p, 0, 0, 0)),
-        out_shape=jax.ShapeDtypeStruct((pairs * groups, 3, rpg, t, LANES), BF),
+        out_specs=pl.BlockSpec(
+            (pairs, 1, 1, 1, t, LANES), lambda b, p: (0, b // rpg, p, b % rpg, 0, 0)
+        ),
+        out_shape=jax.ShapeDtypeStruct((pairs, groups, parts, rpg, t, LANES), BF),
         cost_estimate=pl.CostEstimate(
-            flops=6 * proj.size, bytes_accessed=6 * proj.size, transcendentals=0
+            flops=1, bytes_accessed=1, transcendentals=0
         ),
         name="rotary_out",
     )(proj, bias, cosine, sine)
+    return out.reshape((pairs * groups,) + out.shape[2:])
 
 
 def rotary_in_body(grad_ref, cos_ref, sin_ref, out_ref):
-    value = grad_ref[...].reshape(out_ref.shape).astype(F32)
-    lane = lax.broadcasted_iota(jnp.int32, value.shape, 1)
-    turned = turn(value, cos_ref[...], -sin_ref[...], lane)
-    out_ref[...] = jnp.where(pl.program_id(1) < 2, turned, value).astype(BF)
+    pairs = grad_ref.shape[0]
+    cosine, sine = cos_ref[...], -sin_ref[...]
+    lane = lax.broadcasted_iota(jnp.int32, cosine.shape, 1)
+    rotate = pl.program_id(1) < 2
+    for i in range(pairs):
+        value = grad_ref[i].reshape(cosine.shape).astype(F32)
+        value = jnp.where(rotate, turn(value, cosine, sine, lane), value)
+        out_ref[:, i * LANES : (i + 1) * LANES] = value.astype(BF)
 
 
 def rotary_in(grad, cosine, sine, pairs):
-    dests, _, rpg, t, _ = grad.shape
+    dests, parts, rpg, t, _ = grad.shape
     groups = dests // pairs
-    block = rpg * t
+    wide = pairs * LANES
     return pl.pallas_call(
         rotary_in_body,
-        grid=(dests, 3),
+        grid=(groups * rpg, parts),
         in_specs=[
-            pl.BlockSpec((1, 1, rpg, t, LANES), lambda d, p: (d, p, 0, 0, 0)),
-            pl.BlockSpec((block, LANES), lambda d, p: (d % groups, 0)),
-            pl.BlockSpec((block, LANES), lambda d, p: (d % groups, 0)),
+            pl.BlockSpec(
+                (pairs, 1, 1, 1, t, LANES), lambda b, p: (0, b // rpg, p, b % rpg, 0, 0)
+            ),
+            pl.BlockSpec((t, LANES), lambda b, p: (b, 0)),
+            pl.BlockSpec((t, LANES), lambda b, p: (b, 0)),
         ],
-        out_specs=pl.BlockSpec((block, LANES), lambda d, p: (d % groups, p * pairs + d // groups)),
-        out_shape=jax.ShapeDtypeStruct((groups * block, 3 * pairs * LANES), BF),
+        out_specs=pl.BlockSpec((t, wide), lambda b, p: (b, p)),
+        out_shape=jax.ShapeDtypeStruct((groups * rpg * t, parts * wide), BF),
         cost_estimate=pl.CostEstimate(
-            flops=6 * grad.size, bytes_accessed=4 * grad.size, transcendentals=0
+            flops=1, bytes_accessed=1, transcendentals=0
         ),
         name="rotary_in",
-    )(grad, cosine, sine)
+    )(grad.reshape((pairs, groups) + grad.shape[1:]), cosine, sine)
 
 
 def by_head(x):
@@ -211,14 +248,14 @@
 def attention_specs(blocks, t):
     return [
         pl.BlockSpec((1, 1, 1, t, LANES), lambda r, i: (i, 0, r, 0, 0)),
+        pl.BlockSpec((blocks, 1, 1, t, LANES), lambda r, i: (0, 0, r, 0, 0)),
         pl.BlockSpec((blocks, 1, 1, t, LANES), lambda r, i: (0, 1, r, 0, 0)),
-        pl.BlockSpec((blocks, 1, 1, t, LANES), lambda r, i: (0, 2, r, 0, 0)),
         pl.BlockSpec((1, 1, t, 1), lambda r, i: (r, i, 0, 0)),
     ]
 
 
-def attend(qkv, start, window):
-    blocks, _, rpg, t, _ = qkv.shape
+def attend(q, kv, start, window):
+    blocks, _, rpg, t, _ = q.shape
     work = rpg * blocks * 2 * t * window * t
     return pl.pallas_call(
         functools.partial(forward_body, window),
@@ -227,10 +264,10 @@
         out_specs=pl.BlockSpec((1, 1, t, LANES), lambda r, i: (i, r, 0, 0)),
         out_shape=jax.ShapeDtypeStruct((blocks, rpg, t, LANES), BF),
         cost_estimate=pl.CostEstimate(
-            flops=4 * LANES * work, bytes_accessed=4 * qkv.size, transcendentals=work
+            flops=1, bytes_accessed=1, transcendentals=0
         ),
         name="attend",
-    )(qkv, qkv, qkv, start)
+    )(q, kv, kv, start)
 
 
 def backward_body(window, q_ref, k_ref, v_ref, start_ref, do_ref, out_ref, dk_ref, dv_ref):
@@ -263,8 +300,8 @@
         out_ref[:, 2, 0] = dv_ref[...].astype(BF)
 
 
-def attend_back(qkv, start, grad, window):
-    blocks, _, rpg, t, _ = qkv.shape
+def attend_back(q, kv, start, grad, window):
+    blocks, _, rpg, t, _ = q.shape
     work = rpg * blocks * 2 * t * window * t
     return pl.pallas_call(
         functools.partial(backward_body, window),
@@ -278,10 +315,142 @@
             pltpu.VMEM((blocks, t, LANES), F32),
         ],
         cost_estimate=pl.CostEstimate(
-            flops=10 * LANES * work, bytes_accessed=4 * qkv.size, transcendentals=work
+            flops=1, bytes_accessed=1, transcendentals=0
         ),
         name="attend_back",
-    )(qkv, qkv, qkv, start, grad)
+    )(q, kv, kv, start, grad)
+
+
+FREE = pl.CostEstimate(flops=1, bytes_accessed=1, transcendentals=0)
+
+
+def split_body(here_ref, x_ref, out_ref):
+    count = x_ref.shape[1] // LANES
+    first = here_ref[0] == 0
+    for i in range(count):
+        place = (i % 2) * (count // 2) + i // 2
+        other = (1 - i % 2) * (count // 2) + i // 2
+        value = x_ref[:, i * LANES : (i + 1) * LANES]
+
+        @pl.when(first)
+        def _():
+            out_ref[:, place * LANES : (place + 1) * LANES] = value
+
+        @pl.when(jnp.logical_not(first))
+        def _():
+            out_ref[:, other * LANES : (other + 1) * LANES] = value
+
+
+def join_body(here_ref, x_ref, out_ref):
+    count = x_ref.shape[1] // LANES
+    first = here_ref[0] == 0
+    for i in range(count):
+        place = (i % 2) * (count // 2) + i // 2
+        other = (1 - i % 2) * (count // 2) + i // 2
+        one = x_ref[:, place * LANES : (place + 1) * LANES]
+        two = x_ref[:, other * LANES : (other + 1) * LANES]
+        out_ref[:, i * LANES : (i + 1) * LANES] = jnp.where(first, one, two)
+
+
+def regroup(body, here, x, name):
+    return pl.pallas_call(
+        body,
+        in_specs=[
+            pl.BlockSpec(memory_space=pltpu.SMEM),
+            pl.BlockSpec(memory_space=pltpu.VMEM),
+        ],
+        out_specs=pl.BlockSpec(memory_space=pltpu.VMEM),
+        out_shape=jax.ShapeDtypeStruct(x.shape, x.dtype),
+        cost_estimate=FREE,
+        name=name,
+    )(here.reshape(1), x)
+
+
+def hidden_body(x_ref, gn_ref, gf_ref, un_ref, uf_ref, gate_ref, up_ref, act_ref):
+    k = gn_ref.shape[0]
+    tile = gn_ref.shape[1]
+    near = jnp.concatenate([gn_ref[...], un_ref[...]], axis=1)
+    far = jnp.concatenate([gf_ref[...], uf_ref[...]], axis=1)
+    both = dot(x_ref[:, :k], near) + dot(x_ref[:, k:], far)
+    gate, up = both[:, :tile], both[:, tile:]
+    gate_ref[...] = gate
+    up_ref[...] = up
+    act_ref[...] = (gate * jax.nn.sigmoid(gate) * up).astype(BF)
+
+
+def hidden_units(x, gate, up):
+    m, width = x.shape
+    k, n = gate[0].shape
+    weight = pl.BlockSpec((k, LANES), lambda j: (0, j))
+    tile = pl.BlockSpec((m, LANES), lambda j: (0, j))
+    return pl.pallas_call(
+        hidden_body,
+        grid=(pl.cdiv(n, LANES),),
+        in_specs=[pl.BlockSpec((m, width), lambda j: (0, 0))] + [weight] * 4,
+        out_specs=[tile] * 3,
+        out_shape=[jax.ShapeDtypeStruct((m, n), d) for d in (F32, F32, BF)],
+        cost_estimate=FREE,
+        name="hidden_units",
+    )(x, *gate, *up)
+
+
+def hidden_back_body(grad_ref, down_ref, gate_ref, up_ref, gg_ref, gu_ref):
+    grad = dot_nt(grad_ref[...], down_ref[...])
+    gate = gate_ref[...]
+    sigmoid = jax.nn.sigmoid(gate)
+    gg_ref[...] = (grad * up_ref[...] * sigmoid * (1.0 + gate * (1.0 - sigmoid))).astype(BF)
+    gu_ref[...] = (grad * gate * sigmoid).astype(BF)
+
+
+def hidden_back(grad, down, gate, up, t):
+    m, width = grad.shape
+    n = down.shape[0]
+    tile = pl.BlockSpec((t, n), lambda i: (i, 0))
+    return pl.pallas_call(
+        hidden_back_body,
+        grid=(m // t,),
+        in_specs=[
+            pl.BlockSpec((t, width), lambda i: (i, 0)),
+            pl.BlockSpec((n, width), lambda i: (0, 0)),
+            tile,
+            tile,
+        ],
+        out_specs=[tile] * 2,
+        out_shape=[jax.ShapeDtypeStruct((m, n), BF)] * 2,
+        cost_estimate=FREE,
+        name="hidden_back",
+    )(grad, down, gate, up)
+
+
+def input_back_body(steps, gg_ref, gu_ref, gn_ref, gf_ref, un_ref, uf_ref, out_ref):
+    @pl.when(pl.program_id(0) < steps)
+    def _():
+        part = dot_nt(gg_ref[...], gn_ref[...]) + dot_nt(gu_ref[...], un_ref[...])
+        out_ref[...] = part.astype(BF)
+
+    @pl.when(pl.program_id(0) >= steps)
+    def _():
+        part = dot_nt(gg_ref[...], gf_ref[...]) + dot_nt(gu_ref[...], uf_ref[...])
+        out_ref[...] = part.astype(BF)
+
+
+def input_back(grad_gate, grad_up, gate, up):
+    m, n = grad_gate.shape
+    k = gate[0].shape[0]
+    tile = 2 * LANES
+    steps = k // tile
+    whole = pl.BlockSpec((m, n), lambda i: (0, 0))
+    near = pl.BlockSpec((tile, n), lambda i: (jnp.minimum(i, steps - 1), 0))
+    far = pl.BlockSpec((tile, n), lambda i: (jnp.maximum(i - steps, 0), 0))
+    return pl.pallas_call(
+        functools.partial(input_back_body, steps),
+        grid=(2 * steps,),
+        in_specs=[whole, whole, near, far, near, far],
+        out_specs=pl.BlockSpec((m, tile), lambda i: (0, i)),
+        out_shape=jax.ShapeDtypeStruct((m, 2 * k), BF),
+        cost_estimate=FREE,
+        name="input_back",
+    )(grad_gate, grad_up, *gate, *up)
 
 
 def local(
@@ -303,7 +472,10 @@
     nz, ny, nx, nc = sizes
     seq, peers = nz * ny, nx * nc
     devices = seq * peers
-    pair = nx == 2
+    pair = nx == 2 and ny == 2
+    att, att_rows = ("x", "y") if pair else (None, None)
+    fwd, fwd_rows = ("y", "x") if pair else (None, None)
+    fwd_axes = ("y", "c") if pair else BATCH
     t, width = tokens_in.shape[1:]
     length = segment_ids.shape[1]
     heads = width // HEAD_DIM // peers
@@ -328,27 +500,41 @@
     bias = lax.dynamic_index_in_dim(bias, me_peer, 2, keepdims=False).reshape(1, -1)
 
     rows = qkv_weight.shape[0]
+    third = width // peers
     qkv_mine = qkv_weight.reshape(rows, 3, heads, peers, HEAD_DIM).transpose(3, 0, 1, 2, 4)
-    qkv_mine = swap_batch(qkv_mine.reshape(peers, rows, -1)).reshape(peers * rows, -1)
-    qkv_full = gather_seq(qkv_mine, ny)
+    qkv_mine = swap_peers(qkv_mine.reshape(peers, rows, -1), BATCH).reshape(peers * rows, -1)
+
+    def columns(w):
+        if pair:
+            w = w.reshape(rows, nz, 2, 2, nc, strip).transpose(2, 4, 0, 1, 3, 5)
+        else:
+            w = w.reshape(rows, seq, peers, strip).transpose(2, 0, 1, 3)
+        return w.reshape(peers, rows, -1)
+
+    mine = jnp.concatenate([columns(gate_weight), columns(up_weight)], axis=1)
+    mine = swap_peers(mine, fwd_axes)
+    gate_mine = mine[:, :rows].reshape(peers * rows, -1)
+    up_mine = mine[:, rows:].reshape(peers * rows, -1)
+
+    merge_att = functools.partial(merge_rows, axis=att_rows, nz=nz)
+    merge_ff = functools.partial(merge_rows, axis=fwd_rows, nz=nz)
+    split = 2 if pair else 1
+    q_near = gather_z(qkv_mine[:, :third])
+    kv_near = gather_z(qkv_mine[:, third:])
+    q_near, gate_mine, up_mine = lax.optimization_barrier((q_near, gate_mine, up_mine))
+    q_full = merge_att(q_near, gather_far(q_near, att_rows))
+    kv_full = merge_att(kv_near, gather_far(kv_near, att_rows))
     if own_head:
-        out_full = gather_seq(out_weight, ny)
+        out_near = gather_z(out_weight)
     else:
         out_full = lax.all_gather(out_weight, ALL, axis=0, tiled=True)
         out_full = out_full.reshape(heads, peers, HEAD_DIM, width)
         out_full = lax.dynamic_index_in_dim(out_full, me_peer, 1, keepdims=False)
         out_full = out_full.reshape(heads * HEAD_DIM, width)
-
-    def columns(w):
-        w = w.reshape(rows, seq, peers, strip).transpose(2, 0, 1, 3)
-        w = swap_batch(w.reshape(peers, rows, -1))
-        return gather_seq(w.reshape(peers * rows, -1), ny)
-
-    gate_full = columns(gate_weight)
-    up_full = columns(up_weight)
-    down_full = gather_seq(down_weight, ny)
-
-    segment = gather_batch(segment_ids, pair)
+    gate_near = gather_z(gate_mine)
+    gate_far = gather_far(gate_near, fwd_rows)
+
+    segment = gather_peers(segment_ids, att)
     start = jnp.zeros_like(segment)
     for doc in range(DOCS):
         count = jnp.sum((segment == doc).astype(jnp.int32), axis=1, keepdims=True)
@@ -368,11 +554,25 @@
     inputs = tokens_in[0].astype(F32)
     unit_one, scale_one = norm_stats(inputs)
     normed = (unit_one * gain_one + shift_one).astype(BF)
-    normed_all = gather_batch(normed, pair)
-    proj = dot(normed_all, qkv_full)
-    qkv = rotary_out(proj, bias, cosine, sine, pairs, rpg, t)
-    qkv = swap_seq(qkv)
-    mixed = swap_seq(attend(qkv, start, window))
+    normed_all = gather_peers(normed, att)
+    query = rotary_out(dot(normed_all, q_full), bias[:, :third], cosine, sine, pairs, rpg, t, 1)
+    query = swap_seq(query)
+    key_value = dot(normed_all, kv_full)
+    key_value = rotary_out(key_value, bias[:, third:], cosine, sine, pairs, rpg, t, 1)
+    if own_head:
+        key_value, out_near = lax.optimization_barrier((key_value, out_near))
+        out_full = merge_att(out_near, gather_far(out_near, att_rows))
+    key_value = swap_seq(key_value)
+    up_near = gather_z(up_mine)
+    up_far = gather_far(up_near, fwd_rows)
+    down_near = gather_z(down_weight)
+    grad_output = cotangent[0]
+    grad_all = gather_peers(grad_output, fwd)
+    query, key_value, gate_far = lax.optimization_barrier((query, key_value, gate_far))
+    mixed = swap_seq(attend(query, key_value, start, window))
+    mixed, up_far, down_near, grad_all = lax.optimization_barrier(
+        (mixed, up_far, down_near, grad_all)
+    )
 
     def token_rows(x):
         x = x.reshape(pairs, groups * rpg * t, LANES).transpose(1, 0, 2)
@@ -383,62 +583,115 @@
         return x.reshape(seq, rpg, t, LANES)
 
     mixed = token_rows(mixed)
-    hidden = inputs + reduce_batch(dot(mixed, out_full, BF), pair)
+    hidden = inputs + reduce_peers(dot(mixed, out_full, BF), att)
 
     unit_two, scale_two = norm_stats(hidden)
     normed_two = (unit_two * gain_two + shift_two).astype(BF)
-    normed_two_all = gather_batch(normed_two, pair)
-    grad_output = cotangent[0]
-    grad_all = gather_batch(grad_output, pair)
-    gate = dot(normed_two_all, gate_full)
-    up = dot(normed_two_all, up_full)
-    sigmoid = jax.nn.sigmoid(gate)
-    act = (gate * sigmoid * up).astype(BF)
-    block_out = hidden + reduce_batch(dot(act, down_full, BF), pair)
-    block_out = block_out.astype(BF).reshape(tokens_in.shape)
-
-    grad_down = reduce_seq(dot_tn(act, grad_all, BF), nz, ny).astype(F32)
-    grad_act = dot_nt(grad_all, down_full)
-    grad_gate = (grad_act * up * sigmoid * (1.0 + gate * (1.0 - sigmoid))).astype(BF)
-    grad_up = (grad_act * gate * sigmoid).astype(BF)
-    part = dot_nt(grad_gate, gate_full) + dot_nt(grad_up, up_full)
-    grad_normed_two = reduce_batch(part.astype(BF), pair)
-
-    def uncolumns(g):
-        g = reduce_seq(g, nz, ny).reshape(peers, rows, -1)
-        return swap_batch(g)
-
-    def ff_columns(g):
-        g = uncolumns(g).reshape(peers, rows, seq, strip).transpose(1, 2, 0, 3)
-        return g.reshape(rows, ff).astype(F32)
-
-    grad_gate_w = ff_columns(dot_tn(normed_two_all, grad_gate, BF))
-    grad_up_w = ff_columns(dot_tn(normed_two_all, grad_up, BF))
+    down_far = gather_far(after(down_near, hidden), fwd_rows)
+    if pair:
+        here_x = lax.axis_index("x")
+        normed_two = regroup(split_body, here_x, normed_two, "own_first")
+        gate_full, up_full = (gate_near, gate_far), (up_near, up_far)
+    else:
+        gate_full = jnp.split(merge_ff(gate_near, gate_far), 2)
+        up_full = jnp.split(merge_ff(up_near, up_far), 2)
+    normed_two_all = gather_peers(normed_two, fwd)
+    gate, up, act = hidden_units(normed_two_all, gate_full, up_full)
+    down_full = merge_ff(down_near, down_far)
+    down_part = dot(act, down_full, BF)
+
+    send_att = functools.partial(send_rows, axis=att_rows, nz=nz, na=ny)
+    send_ff = functools.partial(send_rows, axis=fwd_rows, nz=nz, na=nx if pair else ny)
+    wide = width // 2
+    down_one = send_ff(dot_tn(act, grad_all[:, :wide], BF))
+    down_two = send_ff(dot_tn(act, grad_all[:, wide:], BF))
+    grad_gate, grad_up = hidden_back(grad_all, down_full, gate, up, t)
+    part = input_back(grad_gate, grad_up, gate_full, up_full)
+    branch_two = reduce_peers(down_part, fwd)
+    part, branch_two, down_one = lax.optimization_barrier((part, branch_two, down_one))
+    block_out = (hidden + branch_two).astype(BF).reshape(tokens_in.shape)
+    grad_normed_two = reduce_peers(part, fwd)
+
+    def send_columns(g):
+        if not pair:
+            return send_ff(dot_tn(normed_two_all, g, BF))
+        far = dot_tn(normed_two_all[:, wide:], g, BF)
+        near = dot_tn(normed_two_all[:, :wide], g, BF)
+        return near, lax.ppermute(far, "x", SWAP)
+
+    cut_ff = grad_gate.shape[1] // 256 * 128 + LANES
+    pieces = [g[:, at] for g in (grad_gate, grad_up) for at in (slice(0, cut_ff), slice(cut_ff, None))]
+    gate_one, gate_two, up_one, up_two = [send_columns(g) for g in pieces]
+    grad_normed_two, down_two = lax.optimization_barrier((grad_normed_two, down_two))
+    grad_down = [reduce_z(*down_one), reduce_z(*down_two)]
+    if pair:
+        grad_normed_two = regroup(join_body, here_x, grad_normed_two, "own_back")
     back, grad_gain_two, grad_shift_two = norm_back(grad_normed_two, unit_two, scale_two, gain_two)
     grad_hidden = grad_output.astype(F32) + back
 
-    branch = gather_batch(grad_hidden.astype(BF), pair)
+    def ff_columns(*parts):
+        g = jnp.concatenate(parts, axis=1)
+        g = swap_peers(g.reshape(peers, rows, -1), fwd_axes)
+        if pair:
+            g = g.reshape(2, nc, rows, nz, 2, strip).transpose(2, 3, 0, 4, 1, 5)
+        else:
+            g = g.reshape(peers, rows, seq, strip).transpose(1, 2, 0, 3)
+        return g.reshape(rows, ff).astype(F32)
+
+    branch = gather_peers(grad_hidden.astype(BF), att)
+    grad_mixed = head_rows(dot_nt(branch, out_full, BF))
+    grad_mixed = swap_seq(grad_mixed)
     grad_out = dot_tn(mixed, branch, BF)
+    grad_mixed, gate_one, grad_out = lax.optimization_barrier((grad_mixed, gate_one, grad_out))
+    gate_one = reduce_z(*gate_one)
+    grad_qkv = attend_back(query, key_value, start, grad_mixed, window)
     if own_head:
-        grad_out = reduce_seq(grad_out, nz, ny).astype(F32)
-    else:
+        grad_out = send_att(grad_out)
+    grad_qkv, gate_two = lax.optimization_barrier((grad_qkv, gate_two))
+    gate_two = reduce_z(*gate_two)
+    grad_qkv = swap_seq(grad_qkv)
+    grad_down = jnp.concatenate(grad_down, axis=1).astype(F32)
+    up_one, up_two = add_rows(*up_one), add_rows(*up_two)
+    if own_head:
+        grad_out = add_rows(*grad_out)
+    grad_qkv, up_one, up_two, grad_out, grad_down = lax.optimization_barrier(
+        (grad_qkv, up_one, up_two, grad_out, grad_down)
+    )
+    if own_head:
+        grad_out = scatter_z(grad_out)
+    up_one, up_two = scatter_z(up_one), scatter_z(up_two)
+    if not own_head:
         mine = (jnp.arange(peers) == me_peer).astype(BF)[None, :, None, None]
         grad_out = grad_out.reshape(heads, 1, HEAD_DIM, width) * mine
         grad_out = lax.psum_scatter(
             grad_out.reshape(width, width), ALL, scatter_dimension=0, tiled=True
-        ).astype(F32)
-    grad_mixed = head_rows(dot_nt(branch, out_full, BF))
-    grad_qkv = attend_back(qkv, start, swap_seq(grad_mixed), window)
-    grad_proj = rotary_in(swap_seq(grad_qkv), cosine, sine, pairs)
-    grad_qkv_w = uncolumns(dot_tn(normed_all, grad_proj, BF))
+        )
+    grad_proj = rotary_in(grad_qkv, cosine, sine, pairs)
+    cut = 3 * third // 2
+    first = dot_tn(normed_all, grad_proj[:, :cut], BF)
+    second = dot_tn(normed_all, grad_proj[:, cut:], BF)
+    grad_proj, first, second = lax.optimization_barrier((grad_proj, first, second))
+    first, second = send_att(first), send_att(second)
+    grad_normed = dot_nt(grad_proj[:, :third], q_full) + dot_nt(grad_proj[:, third:], kv_full)
+    grad_normed = reduce_peers(grad_normed.astype(BF), att)
+    grad_gate_w = ff_columns(gate_one, gate_two)
+    grad_normed, first, grad_gate_w, grad_out = lax.optimization_barrier(
+        (grad_normed, first, grad_gate_w, grad_out)
+    )
+    first = reduce_z(*first)
+    back, grad_gain_one, grad_shift_one = norm_back(grad_normed, unit_one, scale_one, gain_one)
+    grad_tokens = (grad_hidden + back).astype(BF).reshape(tokens_in.shape)
+    second, grad_tokens = lax.optimization_barrier((second, grad_tokens))
+    second = reduce_z(*second)
+    grad_up_w = ff_columns(up_one, up_two)
+    grad_out = grad_out.astype(F32)
+    grad_qkv_w = jnp.concatenate([first, second], axis=1)
+    grad_qkv_w = swap_peers(grad_qkv_w.reshape(peers, rows, -1), BATCH)
     grad_qkv_w = grad_qkv_w.reshape(peers, rows, 3, heads, HEAD_DIM).transpose(1, 2, 3, 0, 4)
     grad_qkv_w = grad_qkv_w.reshape(rows, 3 * width).astype(F32)
     grad_bias = jnp.sum(grad_proj.astype(F32), axis=0).reshape(3, heads, 1, HEAD_DIM)
     mine = (jnp.arange(peers) == me_peer).astype(F32)[None, None, :, None]
     grad_bias = (grad_bias * mine).reshape(devices, -1)
-    grad_normed = reduce_batch(dot_nt(grad_proj, qkv_full, BF), pair)
-    back, grad_gain_one, grad_shift_one = norm_back(grad_normed, unit_one, scale_one, gain_one)
-    grad_tokens = (grad_hidden + back).astype(BF).reshape(tokens_in.shape)
 
     vectors = [grad_gain_one, grad_shift_one, grad_gain_two, grad_shift_two]
     vectors = [v.reshape(devices, each) for v in vectors] + [grad_bias]

time: 1220 us -> 1170 us (0.959)
  waiting for transfers between devices: 701 us -> 565 us
  Pallas kernels: 105 us -> 152 us
  blocking collectives: 15.8 us -> 57.2 us
  matrix products: 138 us -> 108 us
  other arithmetic: 78.1 us -> 101 us
    ppermute x28 -> x33, waiting for transfers between devices: 463 us -> 339 us  [the longest x5 106 us: gather_peers(): other = lax.ppermute(x, axis, SWAP)]
    all_to_all x4 -> x5, waiting for transfers between devices: 149 us -> 66.2 us  [swap_seq(): return lax.all_to_all(x, SEQ, split_axis=0, concat_axis=0, tiled=True)]
    reduce_scatter x5 -> x9, waiting for transfers between devices: 0.03 us -> 51.1 us  [scatter_z(): return lax.psum_scatter(g, 'z', scatter_dimension=0, tiled=True)]
    pallas_call x2 -> x8, Pallas kernels: 33.9 us -> 81 us  [the longest x1 20 us: hidden_units(): pl.pallas_call(hidden_body, grid=(pl.cdiv(n, LANES),), in_specs=[pl.Block...]
    all_to_all x1 -> x2, blocking collectives: 15.8 us -> 57.2 us  [swap_peers(): return lax.all_to_all(x, axes, split_axis=0, concat_axis=0, tiled=True)]
    dot_general x5 -> x3, matrix products: 44.9 us -> 18 us  [dot_nt(): lax.dot_general(a, b, (((1,), (1,)), ((), ())), preferred_element_type=out)]
    dot_general x5 -> x4, matrix products: 50.4 us -> 27.3 us  [dot(): return jnp.dot(a, b, preferred_element_type=out)]
    all_gather x5 -> x6, waiting for transfers between devices: 55.4 us -> 76.2 us  [gather_z(): return lax.all_gather(w, 'z', axis=0, tiled=True)]
  transfers between devices with their start and end apart: 49 -> 58, of which waited for: 23 -> 31; matrix products, arithmetic and copies ran while one was open for 18% -> 20% of each run, Pallas kernels for 9% -> 11%
where the time goes in v2:
time: 1170 us; the launch traced here: 1160 us
  waiting for transfers between devices  565 us (48%)
  Pallas kernels  152 us (13%)
  matrix products  108 us (9%)
  other arithmetic  101 us (9%)
  local copies, waits for them, and re-layouts  87.8 us (8%)
  starting transfers between devices  71.2 us (6%)
  blocking collectives  57.2 us (5%)
  between operations  15.5 us (1%)
    ppermute x5, waiting for transfers between devices, gather_peers(): other = lax.ppermute(x, axis, SWAP)  106 us
    ppermute x6, waiting for transfers between devices, gather_far(): return lax.ppermute(near, axis, SWAP)  84.2 us
    all_gather x6, waiting for transfers between devices, gather_z(): return lax.all_gather(w, 'z', axis=0, tiled=True)  76.2 us
    all_to_all x5, waiting for transfers between devices, swap_seq(): return lax.all_to_all(x, SEQ, split_axis=0, concat_axis=0, tiled=True)  66.2 us
    dot_general x13, matrix products, dot_tn(): lax.dot_general(a, b, (((0,), (0,)), ((), ())), preferred_element_type=out)  62.8 us
    all_to_all x2, blocking collectives, swap_peers(): return lax.all_to_all(x, axes, split_axis=0, concat_axis=0, tiled=True)  57.2 us
    reduce_scatter x9, waiting for transfers between devices, scatter_z(): return lax.psum_scatter(g, 'z', scatter_dimension=0, tiled=True)  51.1 us
    ppermute x4, waiting for transfers between devices, send_columns(): return (near, lax.ppermute(far, 'x', SWAP))  47 us
  transfers between devices with their start and end apart: 58, of which 31 were waited for; matrix products, arithmetic and copies ran while one was open for 20% of the time, Pallas kernels for 11%

profile of v2, /device:TPU:0, one launch (start us, length us, event | category | flops | bytes accessed | tf_op | source)
XLA Modules:
  0.0 1157.6 jit_solution(14675934933174511706)
XLA Ops:
  10.9 15.8 %all_to_all.65 = bf16[4,64,1536]{2,1,0:T(8,128)(2,1)S(1)} all-to-all(bf16[4,64,1536]{2,1,0:T(8,128)(2,1)S(1)} %reshape.455), channel_id=1, replica_groups=mesh['z'=4,'y'=2,'x'=2,'c'=2] {'x','c'}, dimensions={0} | all-to-all | bytes 1572864 | tf_op jit(solution)/shard_map/all_to_all | solution.py:110
  42.2 17.8 %all-to-all-done.2 = bf16[4,128,1408]{2,1,0:T(8,128)(2,1)S(1)} async-done(((bf16[4,128,1408]{2,1,0:T(8,128)(2,1)}), bf16[4,128,1408]{2,1,0:T(8,128)(2,1)S(1)}, u32[]{:S(2)}, u32[]{:S(2)}) %all-to-all-start.2) | async-done | bytes 1441824 | tf_op jit(solution)/shard_map/all_to_all | solution.py:110
  76.4 24.8 %collective-permute-done = bf16[256,2048]{1,0:T(8,128)(2,1)S(1)} collective-permute-done((bf16[256,2048]{1,0:T(8,128)(2,1)S(1)}, bf16[256,2048]{1,0:T(8,128)(2,1)S(1)}, u32[]{:S(2)}, u32[]{:S(2)}) %collective-permute-start) | collective-permute-done | bytes 1048608 | tf_op jit(solution)/shard_map/ppermute | solution.py:44
  115.7 17.5 %collective-permute-done.2 = bf16[1024,512]{1,0:T(8,128)(2,1)} collective-permute-done((bf16[1024,512]{1,0:T(8,128)(2,1)}, bf16[1024,512]{1,0:T(8,128)(2,1)}, u32[]{:S(2)}, u32[]{:S(2)}) %collective-permute-start.2) | collective-permute-done | bytes 1048608 | tf_op jit(solution)/shard_map/ppermute | solution.py:67
  151.1 35.5 %collective-permute-done.5 = bf16[1024,1024]{1,0:T(8,128)(2,1)} collective-permute-done((bf16[1024,1024]{1,0:T(8,128)(2,1)}, bf16[1024,1024]{1,0:T(8,128)(2,1)}, u32[]{:S(2)}, u32[]{:S(2)}) %collective-permute-start.5) | collective-permute-done | bytes 2097184 | tf_op jit(solution)/shard_map/ppermute | solution.py:67
  223.5 35.0 %collective-permute-done.8 = bf16[256,2048]{1,0:T(8,128)(2,1)} collective-permute-done((bf16[256,2048]{1,0:T(8,128)(2,1)}, bf16[256,2048]{1,0:T(8,128)(2,1)}, u32[]{:S(2)}, u32[]{:S(2)}) %collective-permute-start.8) | collective-permute-done | bytes 1048608 | tf_op jit(solution)/shard_map/ppermute | solution.py:44
  261.7 44.4 %all-gather.15.cloned.1.call-done.un_ref = bf16[1024,1408]{1,0:T(8,128)(2,1)} async-done(((bf16[256,1408]{1,0:T(8,128)(2,1)}), bf16[1024,1408]{1,0:T(8,128)(2,1)}) %all-gather.15.cloned.1.call-update) | async-done | bytes 2883600 | tf_op jit(solution)/shard_map/all_gather | solution.py:61
  313.7 30.6 %attend.1 = bf16[8,2,256,128]{3,2,1,0:T(8,128)(2,1)} custom-call(bf16[8,1,2,256,128]{4,3,2,1,0:T(8,128)(2,1)} %copy-done.15, bf16[8,2,2,256,128]{4,3,2,1,0:T(8,128)(2,1)} %copy-done, bf16[8,2,2,256,128]{4,3,2,1,0:T(8,128)(2,1)} %copy-done, s32[2,8,256,1]{3,2,1,0:T(8,128)} %reshape.505.start_ref), custom_call_target="tpu_custom_call" | custom-call | flops 1 | bytes 1 | tf_op jit(solution)/shard_map/attend/pallas_call | solution.py:260
  354.7 29.0 %all-gather.17.cloned.1.call-done = bf16[704,2048]{1,0:T(8,128)(2,1)} async-done(((bf16[176,2048]{1,0:T(8,128)(2,1)}), bf16[704,2048]{1,0:T(8,128)(2,1)}) %all-gather.17.cloned.1.call-update) | async-done | bytes 2883600 | tf_op jit(solution)/shard_map/all_gather | solution.py:61
  399.6 23.7 %collective-permute-done.12 = bf16[256,2048]{1,0:T(8,128)(2,1)} collective-permute-done((bf16[256,2048]{1,0:T(8,128)(2,1)S(1)}, bf16[256,2048]{1,0:T(8,128)(2,1)}, u32[]{:S(2)}, u32[]{:S(2)}) %collective-permute-start.12) | collective-permute-done | bytes 1048608 | tf_op jit(solution)/shard_map/ppermute | solution.py:56
  433.1 22.8 %collective-permute-done.14 = bf16[256,2048]{1,0:T(8,128)(2,1)S(1)} collective-permute-done((bf16[256,2048]{1,0:T(8,128)(2,1)}, bf16[256,2048]{1,0:T(8,128)(2,1)S(1)}, u32[]{:S(2)}, u32[]{:S(2)}) %collective-permute-start.14) | collective-permute-done | bytes 1048608 | tf_op jit(solution)/shard_map/ppermute | solution.py:44
  458.6 31.2 %collective-permute-done.13 = bf16[704,2048]{1,0:T(8,128)(2,1)} collective-permute-done((bf16[704,2048]{1,0:T(8,128)(2,1)}, bf16[704,2048]{1,0:T(8,128)(2,1)}, u32[]{:S(2)}, u32[]{:S(2)}) %collective-permute-start.13) | collective-permute-done | bytes 2883616 | tf_op jit(solution)/shard_map/ppermute | solution.py:67
  499.8 20.0 %hidden_units.1 = (f32[1024,1408]{1,0:T(8,128)}, f32[1024,1408]{1,0:T(8,128)}, bf16[1024,1408]{1,0:T(8,128)(2,1)}) custom-call(bf16[1024,2048]{1,0:T(8,128)(2,1)} %pad_maximum_fusion.4.x_ref, bf16[1024,1408]{1,0:T(8,128)(2,1)} %all-gather.13.cloned.1.call-done.gn_ref, bf16[1024,1408]{1,0:T(8,128)(2,1)} %collective-permute-done.6.gf_ref, ...), custom_call_target="tpu_custom_call" | custom-call | flops 1 | bytes 1 | tf_op jit(solution)/shard_map/hidden_units/pallas_call | solution.py:386
  549.1 14.6 %hidden_back.1 = (bf16[1024,1408]{1,0:T(8,128)(2,1)}, bf16[1024,1408]{1,0:T(8,128)(2,1)}) custom-call(bf16[1024,2048]{1,0:T(8,128)(2,1)} %pad_maximum_fusion.3.grad_ref, bf16[1408,2048]{1,0:T(8,128)(2,1)} %bitcast.153, f32[1024,1408]{1,0:T(8,128)} %get-tuple-element.73.gate_ref, f32[1024,1408]{1,0:T(8,128)} %get-tuple-element.74.up_ref), custom_call_target="tpu_custom_call" | custom-call | flops 1 | bytes 1 | tf_op jit(solution)/shard_map/hidden_back/pallas_call | solution.py:409
  563.7 19.3 %input_back.1 = bf16[1024,2048]{1,0:T(8,128)(2,1)} custom-call(bf16[1024,1408]{1,0:T(8,128)(2,1)} %get-tuple-element.75.gg_ref, bf16[1024,1408]{1,0:T(8,128)(2,1)} %get-tuple-element.76.gu_ref, bf16[1024,1408]{1,0:T(8,128)(2,1)} %all-gather.13.cloned.1.call-done.gn_ref, bf16[1024,1408]{1,0:T(8,128)(2,1)} %collective-permute-done.6.gf_ref, ...), custom_call_target="tpu_custom_call" | custom-call | flops 1 | bytes 1 | tf_op jit(solution)/shard_map/input_back/pallas_call | solution.py:445
  597.5 19.2 %collective-permute-done.20 = bf16[256,2048]{1,0:T(8,128)(2,1)S(1)} collective-permute-done((bf16[256,2048]{1,0:T(8,128)(2,1)S(1)}, bf16[256,2048]{1,0:T(8,128)(2,1)S(1)}, u32[]{:S(2)}, u32[]{:S(2)}) %collective-permute-start.20) | collective-permute-done | bytes 1048608 | tf_op jit(solution)/shard_map/ppermute | solution.py:56
  644.3 20.3 %collective-permute-done.22 = bf16[256,2048]{1,0:T(8,128)(2,1)S(1)} collective-permute-done((bf16[256,2048]{1,0:T(8,128)(2,1)S(1)}, bf16[256,2048]{1,0:T(8,128)(2,1)S(1)}, u32[]{:S(2)}, u32[]{:S(2)}) %collective-permute-start.22) | collective-permute-done | bytes 1048608 | tf_op jit(solution)/shard_map/ppermute | solution.py:44
  708.5 24.1 %all-to-all-done.6.do_ref = bf16[8,2,256,128]{3,2,1,0:T(8,128)(2,1)S(1)} async-done(((bf16[8,2,256,128]{3,2,1,0:T(8,128)(2,1)}), bf16[8,2,256,128]{3,2,1,0:T(8,128)(2,1)S(1)}, u32[]{:S(2)}, u32[]{:S(2)}) %all-to-all-start.6) | async-done | bytes 1048608 | tf_op jit(solution)/shard_map/all_to_all | solution.py:114
  733.6 40.7 %attend_back.1 = bf16[8,3,2,256,128]{4,3,2,1,0:T(8,128)(2,1)} custom-call(bf16[8,1,2,256,128]{4,3,2,1,0:T(8,128)(2,1)} %copy-done.15, bf16[8,2,2,256,128]{4,3,2,1,0:T(8,128)(2,1)} %copy-done, bf16[8,2,2,256,128]{4,3,2,1,0:T(8,128)(2,1)} %copy-done, s32[2,8,256,1]{3,2,1,0:T(8,128)} %reshape.505.start_ref, bf16[8,2,256,128]{3,2,1,0:T(8,128)(2,1)} %copy-done.28), custom_call_target="tpu_custom_call" | custom-call | flops 1 | bytes 1 | tf_op jit(solution)/shard_map/attend_back/pallas_call | solution.py:306
  821.0 29.8 %collective-permute-done.26 = bf16[1024,768]{1,0:T(8,128)(2,1)} collective-permute-done((bf16[1024,768]{1,0:T(8,128)(2,1)}, bf16[1024,768]{1,0:T(8,128)(2,1)}, u32[]{:S(2)}, u32[]{:S(2)}) %collective-permute-start.26) | collective-permute-done | bytes 1572896 | tf_op jit(solution)/shard_map/ppermute | solution.py:620
  859.4 38.4 %all-to-all-done.7 = bf16[8,3,2,256,128]{4,3,2,1,0:T(8,128)(2,1)S(1)} async-done(((bf16[8,3,2,256,128]{4,3,2,1,0:T(8,128)(2,1)}), bf16[8,3,2,256,128]{4,3,2,1,0:T(8,128)(2,1)S(1)}, u32[]{:S(2)}, u32[]{:S(2)}) %all-to-all-start.7) | async-done | bytes 3145760 | tf_op jit(solution)/shard_map/all_to_all | solution.py:114
  953.2 41.4 %all_to_all.66 = bf16[4,64,1408]{2,1,0:T(8,128)(2,1)S(1)} all-to-all(bf16[4,64,1408]{2,1,0:T(8,128)(2,1)S(1)} %bitcast.194), channel_id=1, replica_groups=mesh['z'=4,'y'=2,'x'=2,'c'=2] {'y','c'}, dimensions={0} | all-to-all | bytes 1441792 | tf_op jit(solution)/shard_map/all_to_all | solution.py:110
  1018.0 29.4 %collective-permute-done.29 = bf16[4,256,768]{2,1,0:T(8,128)(2,1)} collective-permute-done((bf16[4,256,768]{2,1,0:T(8,128)(2,1)}, bf16[4,256,768]{2,1,0:T(8,128)(2,1)}, u32[]{:S(2)}, u32[]{:S(2)}) %collective-permute-start.29) | collective-permute-done | bytes 1572896 | tf_op jit(solution)/shard_map/ppermute | solution.py:91
  1085.1 36.5 %reduce-scatter.20.cloned.1.call-done = bf16[256,768]{1,0:T(8,128)(2,1)} async-done(((bf16[1024,768]{1,0:T(8,128)(2,1)}), bf16[256,768]{1,0:T(8,128)(2,1)}) %reduce-scatter.20.cloned.1.call-update) | async-done | bytes 393232 | tf_op jit(solution)/shard_map/reduce_scatter | solution.py:102
  (397 shorter events, 480.5 us)
Async XLA Ops:
  27.5 80.7 %all-gather.9.cloned.1.call-start = ((), (), s32[]{:S(2)}) async-start(), calls=%async_computation.22 | async-start | bytes 2621440 | tf_op jit(solution)/shard_map/all_gather | solution.py:61
  41.4 165.8 %all-gather.11.cloned.1.call-start = ((), (), s32[]{:S(2)}) async-start(), calls=%async_computation.23 | async-start | bytes 1310720 | tf_op jit(solution)/shard_map/all_gather | solution.py:61
  42.1 172.7 %all-gather.13.cloned.1.call-start = ((), (), s32[]{:S(2)}) async-start(), calls=%async_computation.24 | async-start | bytes 3604480 | tf_op jit(solution)/shard_map/all_gather | solution.py:61
  67.4 238.7 %all-gather.15.cloned.1.call-start = ((), (), s32[]{:S(2)}) async-start(), calls=%async_computation.25 | async-start | bytes 3604480 | tf_op jit(solution)/shard_map/all_gather | solution.py:61
  108.2 78.4 %collective-permute-start.5 = (bf16[1024,1024]{1,0:T(8,128)(2,1)}, bf16[1024,1024]{1,0:T(8,128)(2,1)}, u32[]{:S(2)}, u32[]{:S(2)}) collective-permute-start(bf16[1024,1024]{1,0:T(8,128)(2,1)} %all-gather.9.cloned.1.call-done), channel_id=1, source_target_pairs={{0,4},{4,0},{1,5},{5,1},{2,6},{6,2},{3,7},{7,3},{8,12},{12,8},{9,1... | collective-permute-start | bytes 6291464 | tf_op jit(solution)/shard_map/ppermute | solution.py:67
  208.1 104.2 %all-to-all-start.4 = ((bf16[8,2,2,256,128]{4,3,2,1,0:T(8,128)(2,1)}), bf16[8,2,2,256,128]{4,3,2,1,0:T(8,128)(2,1)S(1)}, u32[]{:S(2)}, u32[]{:S(2)}) async-start(bf16[8,2,2,256,128]{4,3,2,1,0:T(8,128)(2,1)} %bitcast.167), calls=%async_computation.4 | async-start | bytes 4194304 | tf_op jit(solution)/shard_map/all_to_all | solution.py:114
  211.8 171.9 %all-gather.17.cloned.1.call-start = ((), (), s32[]{:S(2)}) async-start(), calls=%async_computation.26 | async-start | bytes 3604480 | tf_op jit(solution)/shard_map/all_gather | solution.py:61
  214.8 97.5 %collective-permute-start.6 = (bf16[1024,1408]{1,0:T(8,128)(2,1)}, bf16[1024,1408]{1,0:T(8,128)(2,1)}, u32[]{:S(2)}, u32[]{:S(2)}) collective-permute-start(bf16[1024,1408]{1,0:T(8,128)(2,1)} %all-gather.13.cloned.1.call-done.gn_ref), channel_id=1, source_target_pairs={{0,2},{2,0},{1,3},{3,1},{4,6},{6,4},{5,7},{7,5},{8,10},{10,8},{9,1... | collective-permute-start | bytes 8650760 | tf_op jit(solution)/shard_map/ppermute | solution.py:67
  261.7 86.4 %collective-permute-start.9 = (bf16[512,2048]{1,0:T(8,128)(2,1)}, bf16[512,2048]{1,0:T(8,128)(2,1)}, u32[]{:S(2)}, u32[]{:S(2)}) collective-permute-start(bf16[512,2048]{1,0:T(8,128)(2,1)} %pad_maximum_fusion.8), channel_id=1, source_target_pairs={{0,1},{1,0},{2,3},{3,2},{4,5},{5,4},{6,7},{7,6},{8,9},{9,8},{10,11... | collective-permute-start | bytes 6291464 | tf_op jit(solution)/shard_map/ppermute | solution.py:46
  306.1 77.6 %collective-permute-start.7 = (bf16[1024,1408]{1,0:T(8,128)(2,1)}, bf16[1024,1408]{1,0:T(8,128)(2,1)}, u32[]{:S(2)}, u32[]{:S(2)}) collective-permute-start(bf16[1024,1408]{1,0:T(8,128)(2,1)} %all-gather.15.cloned.1.call-done.un_ref), channel_id=1, source_target_pairs={{0,2},{2,0},{1,3},{3,1},{4,6},{6,4},{5,7},{7,5},{8,10},{10,8},{9,1... | collective-permute-start | bytes 8650760 | tf_op jit(solution)/shard_map/ppermute | solution.py:67
  348.0 506.3 %reduce-scatter.10.cloned.1.call-start = ((), (), s32[]{:S(2)}) async-start(), calls=%async_computation.27 | async-start | bytes 1802240 | tf_op jit(solution)/shard_map/reduce_scatter | solution.py:102
  425.7 64.0 %collective-permute-start.13 = (bf16[704,2048]{1,0:T(8,128)(2,1)}, bf16[704,2048]{1,0:T(8,128)(2,1)}, u32[]{:S(2)}, u32[]{:S(2)}) collective-permute-start(bf16[704,2048]{1,0:T(8,128)(2,1)} %all-gather.17.cloned.1.call-done), channel_id=1, source_target_pairs={{0,2},{2,0},{1,3},{3,1},{4,6},{6,4},{5,7},{7,5},{8,10},{10,8},{9,1... | collective-permute-start | bytes 8650760 | tf_op jit(solution)/shard_map/ppermute | solution.py:67
  644.3 210.0 %reduce-scatter.12.cloned.1.call-start = ((), (), s32[]{:S(2)}) async-start(), calls=%async_computation.28 | async-start | bytes 1802240 | tf_op jit(solution)/shard_map/reduce_scatter | solution.py:102
  683.5 268.5 %reduce-scatter.16.cloned.1.call-start = ((), (), s32[]{:S(2)}) async-start(), calls=%async_computation.30 | async-start | bytes 1638400 | tf_op jit(solution)/shard_map/reduce_scatter | solution.py:102
  688.8 85.4 %collective-permute-start.25 = (bf16[1024,640]{1,0:T(8,128)(2,1)}, bf16[1024,640]{1,0:T(8,128)(2,1)S(1)}, u32[]{:S(2)}, u32[]{:S(2)}) collective-permute-start(bf16[1024,640]{1,0:T(8,128)(2,1)} %fusion.41), channel_id=1, source_target_pairs={{0,2},{2,0},{1,3},{3,1},{4,6},{6,4},{5,7},{7,5},{8,10},{10,8},{9,1... | collective-permute-start | bytes 3932168 | tf_op jit(solution)/shard_map/ppermute | solution.py:620
  777.0 120.8 %all-to-all-start.7 = ((bf16[8,3,2,256,128]{4,3,2,1,0:T(8,128)(2,1)}), bf16[8,3,2,256,128]{4,3,2,1,0:T(8,128)(2,1)S(1)}, u32[]{:S(2)}, u32[]{:S(2)}) async-start(bf16[8,3,2,256,128]{4,3,2,1,0:T(8,128)(2,1)} %attend_back.1), calls=%async_computation.7 | async-start | bytes 6291456 | tf_op jit(solution)/shard_map/all_to_all | solution.py:114
  780.6 171.4 %reduce-scatter.14.cloned.1.call-start = ((), (), s32[]{:S(2)}) async-start(), calls=%async_computation.29 | async-start | bytes 1966080 | tf_op jit(solution)/shard_map/reduce_scatter | solution.py:102
  790.8 223.8 %reduce-scatter.18.cloned.1.call-start = ((), (), s32[]{:S(2)}) async-start(), calls=%async_computation.31 | async-start | bytes 1310720 | tf_op jit(solution)/shard_map/reduce_scatter | solution.py:102
  909.0 149.6 %reduce-scatter.26.cloned.1.call-start = ((), (), s32[]{:S(2)}) async-start(), calls=%async_computation.35 | async-start | bytes 1638400 | tf_op jit(solution)/shard_map/reduce_scatter | solution.py:102
  939.8 118.8 %reduce-scatter.24.cloned.1.call-start = ((), (), s32[]{:S(2)}) async-start(), calls=%async_computation.34 | async-start | bytes 1966080 | tf_op jit(solution)/shard_map/reduce_scatter | solution.py:102
  947.3 64.9 %collective-permute-start.31 = (bf16[256,2048]{1,0:T(8,128)(2,1)}, bf16[256,2048]{1,0:T(8,128)(2,1)}, u32[]{:S(2)}, u32[]{:S(2)}) collective-permute-start(bf16[256,2048]{1,0:T(8,128)(2,1)} %add_convert_fusion.9), channel_id=1, source_target_pairs={{0,2},{2,0},{1,3},{3,1},{4,6},{6,4},{5,7},{7,5},{8,10},{10,8},{9,1... | collective-permute-start | bytes 3145736 | tf_op jit(solution)/shard_map/ppermute | solution.py:56
  950.5 64.0 %collective-permute-start.32 = (bf16[4,256,768]{2,1,0:T(8,128)(2,1)}, bf16[4,256,768]{2,1,0:T(8,128)(2,1)}, u32[]{:S(2)}, u32[]{:S(2)}) collective-permute-start(bf16[4,256,768]{2,1,0:T(8,128)(2,1)} %get-tuple-element.130), channel_id=1, source_target_pairs={{0,4},{4,0},{1,5},{5,1},{2,6},{6,2},{3,7},{7,3},{8,12},{12,8},{9,1... | collective-permute-start | bytes 4718600 | tf_op jit(solution)/shard_map/ppermute | solution.py:91
  952.0 133.2 %reduce-scatter.22.cloned.1.call-start = ((), (), s32[]{:S(2)}) async-start(), calls=%async_computation.33 | async-start | bytes 1966080 | tf_op jit(solution)/shard_map/reduce_scatter | solution.py:102
  1050.4 71.2 %reduce-scatter.20.cloned.1.call-start = ((), (), s32[]{:S(2)}) async-start(), calls=%async_computation.32 | async-start | bytes 1966080 | tf_op jit(solution)/shard_map/reduce_scatter | solution.py:102
  (98 other events, 1608.5 us)
Sparse Core Ops, SparseCore 0:
  27.6 28.2 all-gather.6
  58.1 45.7 all-gather.8
  105.4 26.6 all-gather.10
  134.1 80.6 all-gather.12
  216.8 89.2 all-gather.14
  307.5 76.0 all-gather.16
  644.4 31.9 reduce-scatter.9
  679.3 49.3 reduce-scatter.11
  777.1 50.3 reduce-scatter.15
  830.2 60.8 reduce-scatter.13
  909.1 26.0 reduce-scatter.17
  939.9 30.2 reduce-scatter.25
  972.5 34.1 reduce-scatter.23
  1050.5 34.5 reduce-scatter.21
  1087.3 34.2 reduce-scatter.19

commit v3 on v2

--- a/solution.py
+++ b/solution.py
@@ -42,9 +42,9 @@
     if axis is None:
         return lax.all_gather(x, BATCH, axis=0, tiled=True)
     other = lax.ppermute(x, axis, SWAP)
-    near = jnp.concatenate([x, other], axis=0)
-    far = lax.ppermute(near, "c", SWAP)
-    return jnp.concatenate([near, far], axis=0)
+    far = lax.ppermute(x, "c", SWAP)
+    last = lax.ppermute(other, "c", SWAP)
+    return jnp.concatenate([x, other, far, last], axis=0)
 
 
 def reduce_peers(part, axis):
@@ -511,30 +511,31 @@
             w = w.reshape(rows, seq, peers, strip).transpose(2, 0, 1, 3)
         return w.reshape(peers, rows, -1)
 
-    mine = jnp.concatenate([columns(gate_weight), columns(up_weight)], axis=1)
-    mine = swap_peers(mine, fwd_axes)
-    gate_mine = mine[:, :rows].reshape(peers * rows, -1)
-    up_mine = mine[:, rows:].reshape(peers * rows, -1)
-
     merge_att = functools.partial(merge_rows, axis=att_rows, nz=nz)
     merge_ff = functools.partial(merge_rows, axis=fwd_rows, nz=nz)
     split = 2 if pair else 1
-    q_near = gather_z(qkv_mine[:, :third])
-    kv_near = gather_z(qkv_mine[:, third:])
-    q_near, gate_mine, up_mine = lax.optimization_barrier((q_near, gate_mine, up_mine))
-    q_full = merge_att(q_near, gather_far(q_near, att_rows))
-    kv_full = merge_att(kv_near, gather_far(kv_near, att_rows))
+    mine = jnp.concatenate([columns(gate_weight), columns(up_weight)], axis=1)
+    mine = swap_peers(after(mine, small), fwd_axes)
+    gate_mine = mine[:, :rows].reshape(peers * rows, -1)
+    up_mine = mine[:, rows:].reshape(peers * rows, -1)
+    kv_near, q_near = gather_z(qkv_mine[:, third:]), gather_z(qkv_mine[:, :third])
+    kv_near, gate_mine, up_mine = lax.optimization_barrier((kv_near, gate_mine, up_mine))
+    kv_far = gather_far(kv_near, att_rows)
+    gate_near = gather_z(gate_mine)
+    gate_far = gather_far(gate_near, fwd_rows)
     if own_head:
-        out_near = gather_z(out_weight)
+        out_near = gather_z(after(out_weight, gate_near))
     else:
         out_full = lax.all_gather(out_weight, ALL, axis=0, tiled=True)
         out_full = out_full.reshape(heads, peers, HEAD_DIM, width)
         out_full = lax.dynamic_index_in_dim(out_full, me_peer, 1, keepdims=False)
         out_full = out_full.reshape(heads * HEAD_DIM, width)
-    gate_near = gather_z(gate_mine)
-    gate_far = gather_far(gate_near, fwd_rows)
-
-    segment = gather_peers(segment_ids, att)
+
+    kv_far, q_near, segment = lax.optimization_barrier(
+        (kv_far, q_near, gather_peers(segment_ids, att))
+    )
+    q_far = gather_far(q_near, att_rows)
+    q_full, kv_full = merge_att(q_near, q_far), merge_att(kv_near, kv_far)
     start = jnp.zeros_like(segment)
     for doc in range(DOCS):
         count = jnp.sum((segment == doc).astype(jnp.int32), axis=1, keepdims=True)
@@ -555,23 +556,25 @@
     unit_one, scale_one = norm_stats(inputs)
     normed = (unit_one * gain_one + shift_one).astype(BF)
     normed_all = gather_peers(normed, att)
+    key_value = rotary_out(
+        dot(normed_all, kv_full), bias[:, third:], cosine, sine, pairs, rpg, t, 1
+    )
+    key_value = swap_seq(key_value)
     query = rotary_out(dot(normed_all, q_full), bias[:, :third], cosine, sine, pairs, rpg, t, 1)
-    query = swap_seq(query)
-    key_value = dot(normed_all, kv_full)
-    key_value = rotary_out(key_value, bias[:, third:], cosine, sine, pairs, rpg, t, 1)
-    if own_head:
-        key_value, out_near = lax.optimization_barrier((key_value, out_near))
-        out_full = merge_att(out_near, gather_far(out_near, att_rows))
-    key_value = swap_seq(key_value)
+    query = swap_seq(after(query, key_value))
+    qkv_full = jnp.concatenate([q_full, kv_full], axis=1)
     up_near = gather_z(up_mine)
-    up_far = gather_far(up_near, fwd_rows)
     down_near = gather_z(down_weight)
     grad_output = cotangent[0]
     grad_all = gather_peers(grad_output, fwd)
-    query, key_value, gate_far = lax.optimization_barrier((query, key_value, gate_far))
-    mixed = swap_seq(attend(query, key_value, start, window))
-    mixed, up_far, down_near, grad_all = lax.optimization_barrier(
-        (mixed, up_far, down_near, grad_all)
+    mixed = attend(query, key_value, start, window)
+    mixed, gate_far, up_near = lax.optimization_barrier((mixed, gate_far, up_near))
+    up_far = gather_far(up_near, fwd_rows)
+    mixed = swap_seq(mixed)
+    if own_head:
+        out_full = merge_att(out_near, gather_far(out_near, att_rows))
+    mixed, up_far, grad_all, qkv_full, out_full = lax.optimization_barrier(
+        (mixed, up_far, grad_all, qkv_full, out_full)
     )
 
     def token_rows(x):
@@ -584,10 +587,11 @@
 
     mixed = token_rows(mixed)
     hidden = inputs + reduce_peers(dot(mixed, out_full, BF), att)
+    hidden, down_near = lax.optimization_barrier((hidden, down_near))
 
     unit_two, scale_two = norm_stats(hidden)
     normed_two = (unit_two * gain_two + shift_two).astype(BF)
-    down_far = gather_far(after(down_near, hidden), fwd_rows)
+    down_far = gather_far(down_near, fwd_rows)
     if pair:
         here_x = lax.axis_index("x")
         normed_two = regroup(split_body, here_x, normed_two, "own_first")
@@ -597,33 +601,46 @@
         up_full = jnp.split(merge_ff(up_near, up_far), 2)
     normed_two_all = gather_peers(normed_two, fwd)
     gate, up, act = hidden_units(normed_two_all, gate_full, up_full)
-    down_full = merge_ff(down_near, down_far)
+    down_full = merge_ff(down_near, after(down_far, gate))
     down_part = dot(act, down_full, BF)
 
     send_att = functools.partial(send_rows, axis=att_rows, nz=nz, na=ny)
     send_ff = functools.partial(send_rows, axis=fwd_rows, nz=nz, na=nx if pair else ny)
     wide = width // 2
     down_one = send_ff(dot_tn(act, grad_all[:, :wide], BF))
-    down_two = send_ff(dot_tn(act, grad_all[:, wide:], BF))
+    down_two = dot_tn(act, grad_all[:, wide:], BF)
     grad_gate, grad_up = hidden_back(grad_all, down_full, gate, up, t)
     part = input_back(grad_gate, grad_up, gate_full, up_full)
     branch_two = reduce_peers(down_part, fwd)
-    part, branch_two, down_one = lax.optimization_barrier((part, branch_two, down_one))
+    down_one = add_rows(*down_one)
+    part, branch_two, down_one, down_two = lax.optimization_barrier(
+        (part, branch_two, down_one, down_two)
+    )
+    down_two = send_ff(down_two)
     block_out = (hidden + branch_two).astype(BF).reshape(tokens_in.shape)
     grad_normed_two = reduce_peers(part, fwd)
 
+    def dots(g):
+        if not pair:
+            return (dot_tn(normed_two_all, g, BF),)
+        return dot_tn(normed_two_all[:, wide:], g, BF), dot_tn(normed_two_all[:, :wide], g, BF)
+
     def send_columns(g):
         if not pair:
-            return send_ff(dot_tn(normed_two_all, g, BF))
-        far = dot_tn(normed_two_all[:, wide:], g, BF)
-        near = dot_tn(normed_two_all[:, :wide], g, BF)
-        return near, lax.ppermute(far, "x", SWAP)
+            return send_ff(g[0])
+        return g[1], lax.ppermute(g[0], "x", SWAP)
 
     cut_ff = grad_gate.shape[1] // 256 * 128 + LANES
-    pieces = [g[:, at] for g in (grad_gate, grad_up) for at in (slice(0, cut_ff), slice(cut_ff, None))]
-    gate_one, gate_two, up_one, up_two = [send_columns(g) for g in pieces]
-    grad_normed_two, down_two = lax.optimization_barrier((grad_normed_two, down_two))
-    grad_down = [reduce_z(*down_one), reduce_z(*down_two)]
+    gate_one, gate_two = dots(grad_gate[:, :cut_ff]), dots(grad_gate[:, cut_ff:])
+    grad_normed_two, gate_one, gate_two = lax.optimization_barrier(
+        (grad_normed_two, gate_one, gate_two)
+    )
+    gate_one, gate_two, up_w = [send_columns(g) for g in (gate_one, gate_two, dots(grad_up))]
+    down_one, down_two = scatter_z(down_one), add_rows(*down_two)
+    grad_normed_two, down_one, down_two = lax.optimization_barrier(
+        (grad_normed_two, down_one, down_two)
+    )
+    down_two = scatter_z(down_two)
     if pair:
         grad_normed_two = regroup(join_body, here_x, grad_normed_two, "own_back")
     back, grad_gain_two, grad_shift_two = norm_back(grad_normed_two, unit_two, scale_two, gain_two)
@@ -640,26 +657,28 @@
 
     branch = gather_peers(grad_hidden.astype(BF), att)
     grad_mixed = head_rows(dot_nt(branch, out_full, BF))
+    grad_mixed, down_two = lax.optimization_barrier((grad_mixed, down_two))
     grad_mixed = swap_seq(grad_mixed)
     grad_out = dot_tn(mixed, branch, BF)
+    gate_one = add_rows(*gate_one)
     grad_mixed, gate_one, grad_out = lax.optimization_barrier((grad_mixed, gate_one, grad_out))
-    gate_one = reduce_z(*gate_one)
+    gate_one = scatter_z(gate_one)
     grad_qkv = attend_back(query, key_value, start, grad_mixed, window)
     if own_head:
         grad_out = send_att(grad_out)
-    grad_qkv, gate_two = lax.optimization_barrier((grad_qkv, gate_two))
-    gate_two = reduce_z(*gate_two)
+    grad_qkv, gate_one, gate_two = lax.optimization_barrier((grad_qkv, gate_one, gate_two))
+    gate_two = scatter_z(add_rows(*gate_two))
     grad_qkv = swap_seq(grad_qkv)
-    grad_down = jnp.concatenate(grad_down, axis=1).astype(F32)
-    up_one, up_two = add_rows(*up_one), add_rows(*up_two)
+    grad_down = jnp.concatenate([down_one, down_two], axis=1).astype(F32)
+    up_w = add_rows(*up_w)
     if own_head:
         grad_out = add_rows(*grad_out)
-    grad_qkv, up_one, up_two, grad_out, grad_down = lax.optimization_barrier(
-        (grad_qkv, up_one, up_two, grad_out, grad_down)
+    grad_qkv, up_w, grad_out, grad_down, gate_two = lax.optimization_barrier(
+        (grad_qkv, up_w, grad_out, grad_down, gate_two)
     )
     if own_head:
         grad_out = scatter_z(grad_out)
-    up_one, up_two = scatter_z(up_one), scatter_z(up_two)
+    up_w = scatter_z(up_w)
     if not own_head:
         mine = (jnp.arange(peers) == me_peer).astype(BF)[None, :, None, None]
         grad_out = grad_out.reshape(heads, 1, HEAD_DIM, width) * mine
@@ -670,20 +689,26 @@
     cut = 3 * third // 2
     first = dot_tn(normed_all, grad_proj[:, :cut], BF)
     second = dot_tn(normed_all, grad_proj[:, cut:], BF)
-    grad_proj, first, second = lax.optimization_barrier((grad_proj, first, second))
+    grad_proj, first, second, grad_out = lax.optimization_barrier(
+        (grad_proj, first, second, grad_out)
+    )
     first, second = send_att(first), send_att(second)
-    grad_normed = dot_nt(grad_proj[:, :third], q_full) + dot_nt(grad_proj[:, third:], kv_full)
-    grad_normed = reduce_peers(grad_normed.astype(BF), att)
-    grad_gate_w = ff_columns(gate_one, gate_two)
-    grad_normed, first, grad_gate_w, grad_out = lax.optimization_barrier(
-        (grad_normed, first, grad_gate_w, grad_out)
-    )
-    first = reduce_z(*first)
+    grad_normed = reduce_peers(dot_nt(grad_proj, qkv_full, BF), att)
+    first = add_rows(*first)
+    first, up_w = lax.optimization_barrier((first, up_w))
+    if pair:
+        second = (second[0], after(second[1], first))
+    first = scatter_z(first)
     back, grad_gain_one, grad_shift_one = norm_back(grad_normed, unit_one, scale_one, gain_one)
     grad_tokens = (grad_hidden + back).astype(BF).reshape(tokens_in.shape)
-    second, grad_tokens = lax.optimization_barrier((second, grad_tokens))
-    second = reduce_z(*second)
-    grad_up_w = ff_columns(up_one, up_two)
+    second = add_rows(*second)
+    second, first, grad_tokens, gate_one, gate_two, up_w = lax.optimization_barrier(
+        (second, first, grad_tokens, gate_one, gate_two, up_w)
+    )
+    second = scatter_z(second)
+    grad_gate_w = ff_columns(gate_one, gate_two)
+    grad_up_w = ff_columns(up_w)
+    second, grad_gate_w, grad_up_w = lax.optimization_barrier((second, grad_gate_w, grad_up_w))
     grad_out = grad_out.astype(F32)
     grad_qkv_w = jnp.concatenate([first, second], axis=1)
     grad_qkv_w = swap_peers(grad_qkv_w.reshape(peers, rows, -1), BATCH)

time: 1170 us -> 1050 us (0.90)
  waiting for transfers between devices: 565 us -> 472 us
  blocking collectives: 57.2 us -> 29.8 us
  other arithmetic: 101 us -> 86.7 us
    all_gather x6, waiting for transfers between devices: 76.2 us -> 12.9 us  [gather_z(): return lax.all_gather(w, 'z', axis=0, tiled=True)]
    reduce_scatter x9 -> x8, waiting for transfers between devices: 51.1 us -> 5.37 us  [scatter_z(): return lax.psum_scatter(g, 'z', scatter_dimension=0, tiled=True)]
    ppermute x9 -> x13, waiting for transfers between devices: 47.7 us -> 78.6 us  [the longest x3 72.5 us: send_columns(): return (g[1], lax.ppermute(g[0], 'x', SWAP))]
    all_to_all x2, blocking collectives: 57.2 us -> 29.8 us  [swap_peers(): return lax.all_to_all(x, axes, split_axis=0, concat_axis=0, tiled=True)]
    ppermute x5, waiting for transfers between devices: 41.1 us -> 60.8 us  [send_rows(): return (keep, lax.ppermute(send, axis, SWAP))]
    ppermute x4, waiting for transfers between devices: 17.2 us -> 4.15 us  [reduce_peers(): got = lax.ppermute(part[2 * rows:], 'c', SWAP)]
    convert_element_type x9 -> x8, other arithmetic: 27.3 us -> 19.3 us  [add_rows(): got = (keep.astype(F32) + got.astype(F32)).astype(BF)]
    dot_general x13 -> x11, matrix products: 62.8 us -> 63.5 us  [dot_tn(): lax.dot_general(a, b, (((0,), (0,)), ((), ())), preferred_element_type=out)]
  transfers between devices with their start and end apart: 58 -> 61, of which waited for: 31 -> 28; matrix products, arithmetic and copies ran while one was open for 20% -> 23% of each run, Pallas kernels for 11% -> 14%
where the time goes in v3:
time: 1050 us; the launch traced here: 1030 us
  waiting for transfers between devices  472 us (45%)
  Pallas kernels  153 us (15%)
  matrix products  105 us (10%)
  local copies, waits for them, and re-layouts  96.4 us (9%)
  other arithmetic  86.7 us (8%)
  starting transfers between devices  77 us (7%)
  blocking collectives  29.8 us (3%)
  between operations  15.2 us (1%)
    ppermute x5, waiting for transfers between devices, gather_peers(): other = lax.ppermute(x, axis, SWAP)  104 us
    ppermute x6, waiting for transfers between devices, gather_far(): return lax.ppermute(near, axis, SWAP)  79.4 us
    ppermute x3, waiting for transfers between devices, send_columns(): return (g[1], lax.ppermute(g[0], 'x', SWAP))  72.5 us
    dot_general x11, matrix products, dot_tn(): lax.dot_general(a, b, (((0,), (0,)), ((), ())), preferred_element_type=out)  63.5 us
    ppermute x5, waiting for transfers between devices, send_rows(): return (keep, lax.ppermute(send, axis, SWAP))  60.8 us
    all_to_all x5, waiting for transfers between devices, swap_seq(): return lax.all_to_all(x, SEQ, split_axis=0, concat_axis=0, tiled=True)  56.1 us
    ppermute x4, waiting for transfers between devices, reduce_peers(): last = lax.ppermute(send, axis, SWAP)  43.7 us
    pallas_call x1, Pallas kernels, attend_back(): pl.pallas_call(functools.partial(backward_body, window), grid=(rpg, block...  40.7 us
  transfers between devices with their start and end apart: 61, of which 28 were waited for; matrix products, arithmetic and copies ran while one was open for 23% of the time, Pallas kernels for 14%

profile of v3, /device:TPU:0, one launch (start us, length us, event | category | flops | bytes accessed | tf_op | source)
XLA Modules:
  0.0 1034.9 jit_solution(5381315001648755802)
XLA Ops:
  11.0 15.8 %all_to_all.65 = bf16[4,64,1536]{2,1,0:T(8,128)(2,1)S(1)} all-to-all(bf16[4,64,1536]{2,1,0:T(8,128)(2,1)S(1)} %reshape.463), channel_id=1, replica_groups=mesh['z'=4,'y'=2,'x'=2,'c'=2] {'x','c'}, dimensions={0} | all-to-all | bytes 1572864 | tf_op jit(solution)/shard_map/all_to_all | solution.py:110
  54.2 17.1 %all-to-all-done.2 = bf16[4,128,1408]{2,1,0:T(8,128)(2,1)S(1)} async-done(((bf16[4,128,1408]{2,1,0:T(8,128)(2,1)}), bf16[4,128,1408]{2,1,0:T(8,128)(2,1)S(1)}, u32[]{:S(2)}, u32[]{:S(2)}) %all-to-all-start.2) | async-done | bytes 1441824 | tf_op jit(solution)/shard_map/all_to_all | solution.py:110
  79.8 22.8 %collective-permute-done.4 = s32[1,2048]{1,0:T(1,128)S(1)} collective-permute-done((s32[1,2048]{1,0:T(1,128)S(1)}, s32[1,2048]{1,0:T(1,128)S(1)}, u32[]{:S(2)}, u32[]{:S(2)}) %collective-permute-start.4) | collective-permute-done | bytes 8224 | tf_op jit(solution)/shard_map/ppermute | solution.py:44
  105.2 16.3 %collective-permute-done.3 = bf16[1024,1024]{1,0:T(8,128)(2,1)S(1)} collective-permute-done((bf16[1024,1024]{1,0:T(8,128)(2,1)}, bf16[1024,1024]{1,0:T(8,128)(2,1)S(1)}, u32[]{:S(2)}, u32[]{:S(2)}) %collective-permute-start.3) | collective-permute-done | bytes 2097184 | tf_op jit(solution)/shard_map/ppermute | solution.py:67
  155.9 11.3 %all-gather.11.cloned.1.call-done.gn_ref = bf16[1024,1408]{1,0:T(8,128)(2,1)} async-done(((bf16[256,1408]{1,0:T(8,128)(2,1)}), bf16[1024,1408]{1,0:T(8,128)(2,1)}) %all-gather.11.cloned.1.call-update) | async-done | bytes 2883600 | tf_op jit(solution)/shard_map/all_gather | solution.py:61
  168.6 30.9 %collective-permute-done.7 = bf16[1024,512]{1,0:T(8,128)(2,1)} collective-permute-done((bf16[1024,512]{1,0:T(8,128)(2,1)}, bf16[1024,512]{1,0:T(8,128)(2,1)}, u32[]{:S(2)}, u32[]{:S(2)}) %collective-permute-start.7) | collective-permute-done | bytes 1048608 | tf_op jit(solution)/shard_map/ppermute | solution.py:67
  213.0 23.3 %all-to-all-done.3.k_ref.v_ref = bf16[8,2,2,256,128]{4,3,2,1,0:T(8,128)(2,1)S(1)} async-done(((bf16[8,2,2,256,128]{4,3,2,1,0:T(8,128)(2,1)}), bf16[8,2,2,256,128]{4,3,2,1,0:T(8,128)(2,1)S(1)}, u32[]{:S(2)}, u32[]{:S(2)}) %all-to-all-start.3) | async-done | bytes 2097184 | tf_op jit(solution)/shard_map/all_to_all | solution.py:114
  244.1 32.8 %collective-permute-done.10 = bf16[256,2048]{1,0:T(8,128)(2,1)} collective-permute-done((bf16[256,2048]{1,0:T(8,128)(2,1)}, bf16[256,2048]{1,0:T(8,128)(2,1)}, u32[]{:S(2)}, u32[]{:S(2)}) %collective-permute-start.10) | collective-permute-done | bytes 1048608 | tf_op jit(solution)/shard_map/ppermute | solution.py:44
  280.3 30.6 %attend.1 = bf16[8,2,256,128]{3,2,1,0:T(8,128)(2,1)} custom-call(bf16[8,1,2,256,128]{4,3,2,1,0:T(8,128)(2,1)} %all-to-all-done.4.q_ref, bf16[8,2,2,256,128]{4,3,2,1,0:T(8,128)(2,1)} %copy-done, bf16[8,2,2,256,128]{4,3,2,1,0:T(8,128)(2,1)} %copy-done, s32[2,8,256,1]{3,2,1,0:T(8,128)} %reshape.517.start_ref), custom_call_target="tpu_custom_call" | custom-call | flops 1 | bytes 1 | tf_op jit(solution)/shard_map/attend/pallas_call | solution.py:260
  327.4 18.2 %collective-permute-done.13 = bf16[256,2048]{1,0:T(8,128)(2,1)} collective-permute-done((bf16[256,2048]{1,0:T(8,128)(2,1)}, bf16[256,2048]{1,0:T(8,128)(2,1)}, u32[]{:S(2)}, u32[]{:S(2)}) %collective-permute-start.13) | collective-permute-done | bytes 1048608 | tf_op jit(solution)/shard_map/ppermute | solution.py:67
  347.2 22.0 %all-to-all-done.5 = bf16[8,2,256,128]{3,2,1,0:T(8,128)(2,1)} async-done(((bf16[8,2,256,128]{3,2,1,0:T(8,128)(2,1)}), bf16[8,2,256,128]{3,2,1,0:T(8,128)(2,1)}, u32[]{:S(2)}, u32[]{:S(2)}) %all-to-all-start.5) | async-done | bytes 1048608 | tf_op jit(solution)/shard_map/all_to_all | solution.py:114
  389.3 23.7 %collective-permute-done.15 = bf16[256,2048]{1,0:T(8,128)(2,1)} collective-permute-done((bf16[256,2048]{1,0:T(8,128)(2,1)S(1)}, bf16[256,2048]{1,0:T(8,128)(2,1)}, u32[]{:S(2)}, u32[]{:S(2)}) %collective-permute-start.15) | collective-permute-done | bytes 1048608 | tf_op jit(solution)/shard_map/ppermute | solution.py:56
  421.8 24.2 %collective-permute-done.17 = bf16[256,2048]{1,0:T(8,128)(2,1)S(1)} collective-permute-done((bf16[256,2048]{1,0:T(8,128)(2,1)}, bf16[256,2048]{1,0:T(8,128)(2,1)S(1)}, u32[]{:S(2)}, u32[]{:S(2)}) %collective-permute-start.17) | collective-permute-done | bytes 1048608 | tf_op jit(solution)/shard_map/ppermute | solution.py:44
  452.4 20.0 %hidden_units.1 = (f32[1024,1408]{1,0:T(8,128)}, f32[1024,1408]{1,0:T(8,128)}, bf16[1024,1408]{1,0:T(8,128)(2,1)}) custom-call(bf16[1024,2048]{1,0:T(8,128)(2,1)} %pad_maximum_fusion.5.x_ref, bf16[1024,1408]{1,0:T(8,128)(2,1)} %all-gather.11.cloned.1.call-done.gn_ref, bf16[1024,1408]{1,0:T(8,128)(2,1)} %collective-permute-done.8.gf_ref, ...), custom_call_target="tpu_custom_call" | custom-call | flops 1 | bytes 1 | tf_op jit(solution)/shard_map/hidden_units/pallas_call | solution.py:386
  513.4 15.0 %hidden_back.1 = (bf16[1024,1408]{1,0:T(8,128)(2,1)}, bf16[1024,1408]{1,0:T(8,128)(2,1)}) custom-call(bf16[1024,2048]{1,0:T(8,128)(2,1)} %pad_maximum_fusion.4.grad_ref, bf16[1408,2048]{1,0:T(8,128)(2,1)} %bitcast.151, f32[1024,1408]{1,0:T(8,128)} %get-tuple-element.97.gate_ref, f32[1024,1408]{1,0:T(8,128)} %get-tuple-element.99.up_ref), custom_call_target="tpu_custom_call" | custom-call | flops 1 | bytes 1 | tf_op jit(solution)/shard_map/hidden_back/pallas_call | solution.py:409
  528.4 19.3 %input_back.1 = bf16[1024,2048]{1,0:T(8,128)(2,1)} custom-call(bf16[1024,1408]{1,0:T(8,128)(2,1)} %get-tuple-element.100.gg_ref, bf16[1024,1408]{1,0:T(8,128)(2,1)} %get-tuple-element.101.gu_ref, bf16[1024,1408]{1,0:T(8,128)(2,1)} %all-gather.11.cloned.1.call-done.gn_ref, bf16[1024,1408]{1,0:T(8,128)(2,1)} %collective-permute-done.8.gf_ref, ...), custom_call_target="tpu_custom_call" | custom-call | flops 1 | bytes 1 | tf_op jit(solution)/shard_map/input_back/pallas_call | solution.py:445
  579.4 18.9 %collective-permute-done.25 = bf16[4,176,1024]{2,1,0:T(8,128)(2,1)S(1)} collective-permute-done((bf16[4,176,1024]{2,1,0:T(8,128)(2,1)S(1)}, bf16[4,176,1024]{2,1,0:T(8,128)(2,1)S(1)}, u32[]{:S(2)}, u32[]{:S(2)}) %collective-permute-start.25) | collective-permute-done | bytes 1441824 | tf_op jit(solution)/shard_map/ppermute | solution.py:91
  614.4 24.0 %collective-permute-done.26 = bf16[256,2048]{1,0:T(8,128)(2,1)S(1)} collective-permute-done((bf16[256,2048]{1,0:T(8,128)(2,1)S(1)}, bf16[256,2048]{1,0:T(8,128)(2,1)S(1)}, u32[]{:S(2)}, u32[]{:S(2)}) %collective-permute-start.26) | collective-permute-done | bytes 1048608 | tf_op jit(solution)/shard_map/ppermute | solution.py:44
  654.1 21.5 %collective-permute-done.29 = bf16[1024,768]{1,0:T(8,128)(2,1)} collective-permute-done((bf16[1024,768]{1,0:T(8,128)(2,1)}, bf16[1024,768]{1,0:T(8,128)(2,1)}, u32[]{:S(2)}, u32[]{:S(2)}) %collective-permute-start.29) | collective-permute-done | bytes 1572896 | tf_op jit(solution)/shard_map/ppermute | solution.py:631
  685.6 40.7 %attend_back.1 = bf16[8,3,2,256,128]{4,3,2,1,0:T(8,128)(2,1)} custom-call(bf16[8,1,2,256,128]{4,3,2,1,0:T(8,128)(2,1)} %all-to-all-done.4.q_ref, bf16[8,2,2,256,128]{4,3,2,1,0:T(8,128)(2,1)} %copy-done, bf16[8,2,2,256,128]{4,3,2,1,0:T(8,128)(2,1)} %copy-done, s32[2,8,256,1]{3,2,1,0:T(8,128)} %reshape.517.start_ref, bf16[8,2,256,128]{3,2,1,0:T(8,128)(2,1)} %copy-done.19), custom_call_target="tpu_custom_call" | custom-call | flops 1 | bytes 1 | tf_op jit(solution)/shard_map/attend_back/pallas_call | solution.py:306
  754.0 51.0 %collective-permute-done.31 = bf16[1024,1408]{1,0:T(8,128)(2,1)} collective-permute-done((bf16[1024,1408]{1,0:T(8,128)(2,1)}, bf16[1024,1408]{1,0:T(8,128)(2,1)}, u32[]{:S(2)}, u32[]{:S(2)}) %collective-permute-start.31) | collective-permute-done | bytes 2883616 | tf_op jit(solution)/shard_map/ppermute | solution.py:631
  866.4 34.4 %collective-permute-done.34 = bf16[4,256,768]{2,1,0:T(8,128)(2,1)S(1)} collective-permute-done((bf16[4,256,768]{2,1,0:T(8,128)(2,1)S(1)}, bf16[4,256,768]{2,1,0:T(8,128)(2,1)S(1)}, u32[]{:S(2)}, u32[]{:S(2)}) %collective-permute-start.34) | collective-permute-done | bytes 1572896 | tf_op jit(solution)/shard_map/ppermute | solution.py:91
  915.0 20.0 %collective-permute-done.36 = bf16[256,2048]{1,0:T(8,128)(2,1)S(1)} collective-permute-done((bf16[256,2048]{1,0:T(8,128)(2,1)S(1)}, bf16[256,2048]{1,0:T(8,128)(2,1)S(1)}, u32[]{:S(2)}, u32[]{:S(2)}) %collective-permute-start.36) | collective-permute-done | bytes 1048608 | tf_op jit(solution)/shard_map/ppermute | solution.py:56
  951.5 14.0 %all_to_all.66 = bf16[4,64,1408]{2,1,0:T(8,128)(2,1)} all-to-all(bf16[4,64,1408]{2,1,0:T(8,128)(2,1)S(1)} %bitcast.197), channel_id=1, replica_groups=mesh['z'=4,'y'=2,'x'=2,'c'=2] {'y','c'}, dimensions={0} | all-to-all | bytes 1441792 | tf_op jit(solution)/shard_map/all_to_all | solution.py:110
  (385 shorter events, 451.9 us)
Async XLA Ops:
  7.2 66.9 %all-gather.7.cloned.1.call-start = ((), (), s32[]{:S(2)}) async-start(), calls=%async_computation.20 | async-start | bytes 2621440 | tf_op jit(solution)/shard_map/all_gather | solution.py:61
  52.6 52.6 %all-gather.9.cloned.1.call-start = ((), (), s32[]{:S(2)}) async-start(), calls=%async_computation.21 | async-start | bytes 1310720 | tf_op jit(solution)/shard_map/all_gather | solution.py:61
  53.7 113.5 %all-gather.11.cloned.1.call-start = ((), (), s32[]{:S(2)}) async-start(), calls=%async_computation.22 | async-start | bytes 3604480 | tf_op jit(solution)/shard_map/all_gather | solution.py:61
  74.0 47.5 %collective-permute-start.3 = (bf16[1024,1024]{1,0:T(8,128)(2,1)}, bf16[1024,1024]{1,0:T(8,128)(2,1)S(1)}, u32[]{:S(2)}, u32[]{:S(2)}) collective-permute-start(bf16[1024,1024]{1,0:T(8,128)(2,1)} %all-gather.7.cloned.1.call-done), channel_id=1, source_target_pairs={{0,4},{4,0},{1,5},{5,1},{2,6},{6,2},{3,7},{7,3},{8,12},{12,8},{9,1... | collective-permute-start | bytes 6291464 | tf_op jit(solution)/shard_map/ppermute | solution.py:67
  149.2 87.1 %all-to-all-start.3 = ((bf16[8,2,2,256,128]{4,3,2,1,0:T(8,128)(2,1)}), bf16[8,2,2,256,128]{4,3,2,1,0:T(8,128)(2,1)S(1)}, u32[]{:S(2)}, u32[]{:S(2)}) async-start(bf16[8,2,2,256,128]{4,3,2,1,0:T(8,128)(2,1)} %bitcast.164), calls=%async_computation.3 | async-start | bytes 4194304 | tf_op jit(solution)/shard_map/all_to_all | solution.py:114
  152.8 158.1 %all-gather.13.cloned.1.call-start = ((), (), s32[]{:S(2)}) async-start(), calls=%async_computation.23 | async-start | bytes 3604480 | tf_op jit(solution)/shard_map/all_gather | solution.py:61
  167.2 143.7 %collective-permute-start.8 = (bf16[1024,1408]{1,0:T(8,128)(2,1)}, bf16[1024,1408]{1,0:T(8,128)(2,1)}, u32[]{:S(2)}, u32[]{:S(2)}) collective-permute-start(bf16[1024,1408]{1,0:T(8,128)(2,1)} %all-gather.11.cloned.1.call-done.gn_ref), channel_id=1, source_target_pairs={{0,2},{2,0},{1,3},{3,1},{4,6},{6,4},{5,7},{7,5},{8,10},{10,8},{9,1... | collective-permute-start | bytes 8650760 | tf_op jit(solution)/shard_map/ppermute | solution.py:67
  240.7 71.6 %all-gather.15.cloned.1.call-start = ((), (), s32[]{:S(2)}) async-start(), calls=%async_computation.24 | async-start | bytes 1310720 | tf_op jit(solution)/shard_map/all_gather | solution.py:61
  244.0 171.6 %all-gather.17.cloned.1.call-start = ((), (), s32[]{:S(2)}) async-start(), calls=%async_computation.25 | async-start | bytes 3604480 | tf_op jit(solution)/shard_map/all_gather | solution.py:61
  244.0 74.2 %collective-permute-start.11 = (bf16[256,2048]{1,0:T(8,128)(2,1)}, bf16[256,2048]{1,0:T(8,128)(2,1)}, u32[]{:S(2)}, u32[]{:S(2)}) collective-permute-start(bf16[256,2048]{1,0:T(8,128)(2,1)} %bitcast.185), channel_id=1, source_target_pairs={{0,1},{1,0},{2,3},{3,2},{4,5},{5,4},{6,7},{7,6},{8,9},{9,8},{10,11... | collective-permute-start | bytes 3145736 | tf_op jit(solution)/shard_map/ppermute | solution.py:45
  310.8 65.3 %collective-permute-start.9 = (bf16[1024,1408]{1,0:T(8,128)(2,1)}, bf16[1024,1408]{1,0:T(8,128)(2,1)}, u32[]{:S(2)}, u32[]{:S(2)}) collective-permute-start(bf16[1024,1408]{1,0:T(8,128)(2,1)} %all-gather.13.cloned.1.call-done.un_ref), channel_id=1, source_target_pairs={{0,2},{2,0},{1,3},{3,1},{4,6},{6,4},{5,7},{7,5},{8,10},{10,8},{9,1... | collective-permute-start | bytes 8650760 | tf_op jit(solution)/shard_map/ppermute | solution.py:67
  312.4 56.8 %all-to-all-start.5 = ((bf16[8,2,256,128]{3,2,1,0:T(8,128)(2,1)}), bf16[8,2,256,128]{3,2,1,0:T(8,128)(2,1)}, u32[]{:S(2)}, u32[]{:S(2)}) async-start(bf16[8,2,256,128]{3,2,1,0:T(8,128)(2,1)} %attend.1), calls=%async_computation.5 | async-start | bytes 2097152 | tf_op jit(solution)/shard_map/all_to_all | solution.py:114
  318.1 285.0 %reduce-scatter.9.cloned.1.call-start = ((), (), s32[]{:S(2)}) async-start(), calls=%async_computation.26 | async-start | bytes 1802240 | tf_op jit(solution)/shard_map/reduce_scatter | solution.py:102
  415.6 64.1 %collective-permute-start.16 = (bf16[704,2048]{1,0:T(8,128)(2,1)}, bf16[704,2048]{1,0:T(8,128)(2,1)}, u32[]{:S(2)}, u32[]{:S(2)}) collective-permute-start(bf16[704,2048]{1,0:T(8,128)(2,1)} %all-gather.17.cloned.1.call-done), channel_id=1, source_target_pairs={{0,2},{2,0},{1,3},{3,1},{4,6},{6,4},{5,7},{7,5},{8,10},{10,8},{9,1... | collective-permute-start | bytes 8650760 | tf_op jit(solution)/shard_map/ppermute | solution.py:67
  562.6 85.6 %reduce-scatter.11.cloned.1.call-start = ((), (), s32[]{:S(2)}) async-start(), calls=%async_computation.27 | async-start | bytes 1802240 | tf_op jit(solution)/shard_map/reduce_scatter | solution.py:102
  654.0 72.3 %reduce-scatter.13.cloned.1.call-start = ((), (), s32[]{:S(2)}) async-start(), calls=%async_computation.28 | async-start | bytes 1966080 | tf_op jit(solution)/shard_map/reduce_scatter | solution.py:102
  727.4 97.4 %all-to-all-start.7 = ((bf16[8,3,2,256,128]{4,3,2,1,0:T(8,128)(2,1)}), bf16[8,3,2,256,128]{4,3,2,1,0:T(8,128)(2,1)S(1)}, u32[]{:S(2)}, u32[]{:S(2)}) async-start(bf16[8,3,2,256,128]{4,3,2,1,0:T(8,128)(2,1)} %attend_back.1), calls=%async_computation.10 | async-start | bytes 6291456 | tf_op jit(solution)/shard_map/all_to_all | solution.py:114
  733.2 80.8 %reduce-scatter.15.cloned.1.call-start = ((), (), s32[]{:S(2)}) async-start(), calls=%async_computation.29 | async-start | bytes 1638400 | tf_op jit(solution)/shard_map/reduce_scatter | solution.py:102
  740.9 64.1 %collective-permute-start.31 = (bf16[1024,1408]{1,0:T(8,128)(2,1)}, bf16[1024,1408]{1,0:T(8,128)(2,1)}, u32[]{:S(2)}, u32[]{:S(2)}) collective-permute-start(bf16[1024,1408]{1,0:T(8,128)(2,1)} %fusion.32), channel_id=1, source_target_pairs={{0,2},{2,0},{1,3},{3,1},{4,6},{6,4},{5,7},{7,5},{8,10},{10,8},{9,1... | collective-permute-start | bytes 8650760 | tf_op jit(solution)/shard_map/ppermute | solution.py:631
  743.5 108.4 %reduce-scatter.17.cloned.1.call-start = ((), (), s32[]{:S(2)}) async-start(), calls=%async_computation.30 | async-start | bytes 1310720 | tf_op jit(solution)/shard_map/reduce_scatter | solution.py:102
  746.0 65.4 %collective-permute-start.32 = (bf16[4,64,2048]{2,1,0:T(8,128)(2,1)}, bf16[4,64,2048]{2,1,0:T(8,128)(2,1)}, u32[]{:S(2)}, u32[]{:S(2)}) collective-permute-start(bf16[4,64,2048]{2,1,0:T(8,128)(2,1)} %dynamic-slice_bitcast_fusion.4), channel_id=1, source_target_pairs={{0,4},{4,0},{1,5},{5,1},{2,6},{6,2},{3,7},{7,3},{8,12},{12,8},{9,1... | collective-permute-start | bytes 3145736 | tf_op jit(solution)/shard_map/ppermute | solution.py:91
  824.8 82.9 %reduce-scatter.19.cloned.1.call-start = ((), (), s32[]{:S(2)}) async-start(), calls=%async_computation.31 | async-start | bytes 3604480 | tf_op jit(solution)/shard_map/reduce_scatter | solution.py:102
  836.2 114.2 %reduce-scatter.21.cloned.1.call-start = ((), (), s32[]{:S(2)}) async-start(), calls=%async_computation.32 | async-start | bytes 1966080 | tf_op jit(solution)/shard_map/reduce_scatter | solution.py:102
  907.7 94.2 %reduce-scatter.23.cloned.1.call-start = ((), (), s32[]{:S(2)}) async-start(), calls=%async_computation.33 | async-start | bytes 1966080 | tf_op jit(solution)/shard_map/reduce_scatter | solution.py:102
  (96 other events, 1775.0 us)
Sparse Core Ops, SparseCore 0:
  27.8 46.1 all-gather.6
  76.2 26.5 all-gather.8
  104.9 62.2 all-gather.10
  169.2 104.9 all-gather.12
  275.6 26.1 all-gather.14
  312.5 78.1 all-gather.16
  562.7 33.4 reduce-scatter.8
  609.0 33.5 reduce-scatter.10
  684.8 35.7 reduce-scatter.12
  743.6 52.0 reduce-scatter.14
  825.0 25.7 reduce-scatter.16
  852.9 54.8 reduce-scatter.18
  910.0 35.1 reduce-scatter.20
  950.6 34.6 reduce-scatter.22

commit v4 on v3

--- a/solution.py
+++ b/solution.py
@@ -47,14 +47,29 @@
     return jnp.concatenate([x, other, far, last], axis=0)
 
 
-def reduce_peers(part, axis):
+def reduce_peers(halves, axis):
+    near, far = halves
     if axis is None:
+        part = jnp.concatenate([near, far], axis=0)
         return lax.psum_scatter(part, BATCH, scatter_dimension=0, tiled=True).astype(F32)
-    rows = part.shape[0] // 4
-    got = lax.ppermute(part[2 * rows :], "c", SWAP)
-    send = (part[rows : 2 * rows].astype(F32) + got[rows:].astype(F32)).astype(BF)
+    rows = near.shape[0] // 2
+    got = lax.ppermute(far, "c", SWAP)
+    send = (near[rows:].astype(F32) + got[rows:].astype(F32)).astype(BF)
     last = lax.ppermute(send, axis, SWAP)
-    return part[:rows].astype(F32) + got[:rows].astype(F32) + last.astype(F32)
+    return near[:rows].astype(F32) + got[:rows].astype(F32) + last.astype(F32)
+
+
+def reduce_pieces(halves, axis):
+    near, far = halves
+    rows = near.shape[0] // 2
+    got = lax.ppermute(far, "c", SWAP)
+    send = (near[rows:].astype(F32) + got[rows:].astype(F32)).astype(BF)
+    return near, got, lax.ppermute(send, axis, SWAP)
+
+
+def halves_of(product, x, w):
+    rows = x.shape[0] // 2
+    return product(x[:rows], w, BF), product(x[rows:], w, BF)
 
 
 def gather_z(w):
@@ -234,15 +249,25 @@
     return weights / jnp.sum(weights, axis=-1, keepdims=True)
 
 
+def by_window(window, body):
+    number = pl.program_id(1)
+    for w in range(1, window + 1):
+        pl.when(number == w - 1 if w < window else number >= w - 1)(functools.partial(body, w))
+
+
 def forward_body(window, q_ref, k_ref, v_ref, start_ref, out_ref):
     number = pl.program_id(1)
     t = q_ref.shape[3]
-    first = jnp.maximum(number - (window - 1), 0)
-    keys = k_ref[pl.ds(first, window), 0, 0].reshape(window * t, LANES)
-    values = v_ref[pl.ds(first, window), 0, 0].reshape(window * t, LANES)
-    q2 = by_head(q_ref[0, 0, 0])
-    weights = window_weights(q2, keys, start_ref[0, 0], number * t, first * t)
-    out_ref[0, 0] = one_head(dot(weights.astype(BF), values)).astype(BF)
+
+    def body(w):
+        first = number - (w - 1)
+        keys = k_ref[pl.ds(first, w), 0, 0].reshape(w * t, LANES)
+        values = v_ref[pl.ds(first, w), 0, 0].reshape(w * t, LANES)
+        q2 = by_head(q_ref[0, 0, 0])
+        weights = window_weights(q2, keys, start_ref[0, 0], number * t, first * t)
+        out_ref[0, 0] = one_head(dot(weights.astype(BF), values)).astype(BF)
+
+    by_window(window, body)
 
 
 def attention_specs(blocks, t):
@@ -280,19 +305,22 @@
         dk_ref[...] = jnp.zeros_like(dk_ref)
         dv_ref[...] = jnp.zeros_like(dv_ref)
 
-    first = jnp.maximum(number - (window - 1), 0)
-    keys = k_ref[pl.ds(first, window), 0, 0].reshape(window * t, LANES)
-    values = v_ref[pl.ds(first, window), 0, 0].reshape(window * t, LANES)
-    q2 = by_head(q_ref[0, 0, 0])
-    do2 = by_head(do_ref[0, 0])
-    weights = window_weights(q2, keys, start_ref[0, 0], number * t, first * t)
-    grad = dot_nt(do2, values)
-    inner = jnp.sum(weights * grad, axis=-1, keepdims=True)
-    ds = (weights * (grad - inner)).astype(BF)
-    out_ref[number, 0, 0] = one_head(dot(ds, keys) * scale).astype(BF)
-    shape = (window, t, LANES)
-    dk_ref[pl.ds(first, window)] += dot_tn(ds, q2).reshape(shape)
-    dv_ref[pl.ds(first, window)] += dot_tn(weights.astype(BF), do2).reshape(shape)
+    def body(w):
+        first = number - (w - 1)
+        keys = k_ref[pl.ds(first, w), 0, 0].reshape(w * t, LANES)
+        values = v_ref[pl.ds(first, w), 0, 0].reshape(w * t, LANES)
+        q2 = by_head(q_ref[0, 0, 0])
+        do2 = by_head(do_ref[0, 0])
+        weights = window_weights(q2, keys, start_ref[0, 0], number * t, first * t)
+        grad = dot_nt(do2, values)
+        inner = jnp.sum(weights * grad, axis=-1, keepdims=True)
+        ds = (weights * (grad - inner)).astype(BF)
+        out_ref[number, 0, 0] = one_head(dot(ds, keys) * scale).astype(BF)
+        shape = (w, t, LANES)
+        dk_ref[pl.ds(first, w)] += dot_tn(ds, q2).reshape(shape)
+        dv_ref[pl.ds(first, w)] += dot_tn(weights.astype(BF), do2).reshape(shape)
+
+    by_window(window, body)
 
     @pl.when(number == pl.num_programs(1) - 1)
     def _():
@@ -324,46 +352,109 @@
 FREE = pl.CostEstimate(flops=1, bytes_accessed=1, transcendentals=0)
 
 
-def split_body(here_ref, x_ref, out_ref):
-    count = x_ref.shape[1] // LANES
-    first = here_ref[0] == 0
-    for i in range(count):
-        place = (i % 2) * (count // 2) + i // 2
-        other = (1 - i % 2) * (count // 2) + i // 2
-        value = x_ref[:, i * LANES : (i + 1) * LANES]
-
-        @pl.when(first)
-        def _():
-            out_ref[:, place * LANES : (place + 1) * LANES] = value
-
-        @pl.when(jnp.logical_not(first))
-        def _():
-            out_ref[:, other * LANES : (other + 1) * LANES] = value
-
-
-def join_body(here_ref, x_ref, out_ref):
-    count = x_ref.shape[1] // LANES
-    first = here_ref[0] == 0
-    for i in range(count):
-        place = (i % 2) * (count // 2) + i // 2
-        other = (1 - i % 2) * (count // 2) + i // 2
-        one = x_ref[:, place * LANES : (place + 1) * LANES]
-        two = x_ref[:, other * LANES : (other + 1) * LANES]
-        out_ref[:, i * LANES : (i + 1) * LANES] = jnp.where(first, one, two)
-
-
-def regroup(body, here, x, name):
+ROWS = 64
+
+
+def places(count):
+    half = count // 2
+    return [((i % 2) * half + i // 2, (1 - i % 2) * half + i // 2) for i in range(count)]
+
+
+def lanes_at(i):
+    return slice(i * LANES, (i + 1) * LANES)
+
+
+def unit_of(value):
+    centred = value - jnp.mean(value, axis=-1, keepdims=True)
+    scale = lax.rsqrt(jnp.mean(centred * centred, axis=-1, keepdims=True) + EPS)
+    return centred * scale, scale
+
+
+def hidden_norm_body(here_ref, x_ref, a_ref, b_ref, c_ref, gain_ref, shift_ref, hid_ref, out_ref):
+    total = a_ref[...].astype(F32) + b_ref[...].astype(F32) + c_ref[...].astype(F32)
+    hidden = x_ref[...].astype(F32) + total
+    hid_ref[...] = hidden
+    unit, _ = unit_of(hidden)
+    normed = (unit * gain_ref[...] + shift_ref[...]).astype(BF)
+    order = places(x_ref.shape[1] // LANES)
+
+    @pl.when(here_ref[0] == 0)
+    def _():
+        for i, (place, _) in enumerate(order):
+            out_ref[:, lanes_at(place)] = normed[:, lanes_at(i)]
+
+    @pl.when(here_ref[0] != 0)
+    def _():
+        for i, (_, place) in enumerate(order):
+            out_ref[:, lanes_at(place)] = normed[:, lanes_at(i)]
+
+
+def hidden_norm(here, x, pieces, gain, shift):
+    t, width = x.shape
+    tile = pl.BlockSpec((ROWS, width), lambda i: (i, 0))
+    line = pl.BlockSpec((1, width), lambda i: (0, 0))
     return pl.pallas_call(
-        body,
-        in_specs=[
-            pl.BlockSpec(memory_space=pltpu.SMEM),
-            pl.BlockSpec(memory_space=pltpu.VMEM),
+        hidden_norm_body,
+        grid=(t // ROWS,),
+        in_specs=[pl.BlockSpec(memory_space=pltpu.SMEM)] + [tile] * 4 + [line] * 2,
+        out_specs=[tile] * 2,
+        out_shape=[jax.ShapeDtypeStruct((t, width), F32), jax.ShapeDtypeStruct((t, width), BF)],
+        cost_estimate=FREE,
+        name="hidden_norm",
+    )(here.reshape(1), x, *pieces, gain, shift)
+
+
+def norm_back_body(
+    here_ref, hid_ref, cot_ref, a_ref, b_ref, c_ref, gain_ref, out_ref, bf_ref, sum_ref, tmp_ref
+):
+    grad = a_ref[...].astype(F32) + b_ref[...].astype(F32) + c_ref[...].astype(F32)
+    order = places(cot_ref.shape[1] // LANES)
+
+    @pl.when(here_ref[0] == 0)
+    def _():
+        for i, (place, _) in enumerate(order):
+            tmp_ref[:, lanes_at(i)] = grad[:, lanes_at(place)]
+
+    @pl.when(here_ref[0] != 0)
+    def _():
+        for i, (_, place) in enumerate(order):
+            tmp_ref[:, lanes_at(i)] = grad[:, lanes_at(place)]
+
+    grad = tmp_ref[...]
+    unit, scale = unit_of(hid_ref[...])
+    e = grad * gain_ref[...]
+    mean = jnp.mean(e, axis=-1, keepdims=True)
+    inner = jnp.mean(e * unit, axis=-1, keepdims=True)
+    total = cot_ref[...].astype(F32) + scale * (e - mean - unit * inner)
+    out_ref[...] = total
+    bf_ref[...] = total.astype(BF)
+
+    @pl.when(pl.program_id(0) == 0)
+    def _():
+        sum_ref[...] = jnp.zeros_like(sum_ref)
+
+    sum_ref[0:1] += jnp.sum(grad * unit, axis=0, keepdims=True)
+    sum_ref[1:2] += jnp.sum(grad, axis=0, keepdims=True)
+
+
+def hidden_norm_back(here, hidden, cotangent, pieces, gain):
+    t, width = hidden.shape
+    tile = pl.BlockSpec((ROWS, width), lambda i: (i, 0))
+    line = pl.BlockSpec((1, width), lambda i: (0, 0))
+    return pl.pallas_call(
+        norm_back_body,
+        grid=(t // ROWS,),
+        in_specs=[pl.BlockSpec(memory_space=pltpu.SMEM)] + [tile] * 5 + [line],
+        out_specs=[tile, tile, pl.BlockSpec((8, width), lambda i: (0, 0))],
+        out_shape=[
+            jax.ShapeDtypeStruct((t, width), F32),
+            jax.ShapeDtypeStruct((t, width), BF),
+            jax.ShapeDtypeStruct((8, width), F32),
         ],
-        out_specs=pl.BlockSpec(memory_space=pltpu.VMEM),
-        out_shape=jax.ShapeDtypeStruct(x.shape, x.dtype),
+        scratch_shapes=[pltpu.VMEM((ROWS, width), F32)],
         cost_estimate=FREE,
-        name=name,
-    )(here.reshape(1), x)
+        name="hidden_norm_back",
+    )(here.reshape(1), hidden, cotangent, *pieces, gain)
 
 
 def hidden_body(x_ref, gn_ref, gf_ref, un_ref, uf_ref, gate_ref, up_ref, act_ref):
@@ -422,16 +513,20 @@
     )(grad, down, gate, up)
 
 
-def input_back_body(steps, gg_ref, gu_ref, gn_ref, gf_ref, un_ref, uf_ref, out_ref):
+def input_back_body(steps, gg_ref, gu_ref, gn_ref, gf_ref, un_ref, uf_ref, one_ref, two_ref):
+    rows = one_ref.shape[0]
+
     @pl.when(pl.program_id(0) < steps)
     def _():
         part = dot_nt(gg_ref[...], gn_ref[...]) + dot_nt(gu_ref[...], un_ref[...])
-        out_ref[...] = part.astype(BF)
+        one_ref[...] = part[:rows].astype(BF)
+        two_ref[...] = part[rows:].astype(BF)
 
     @pl.when(pl.program_id(0) >= steps)
     def _():
         part = dot_nt(gg_ref[...], gf_ref[...]) + dot_nt(gu_ref[...], uf_ref[...])
-        out_ref[...] = part.astype(BF)
+        one_ref[...] = part[:rows].astype(BF)
+        two_ref[...] = part[rows:].astype(BF)
 
 
 def input_back(grad_gate, grad_up, gate, up):
@@ -446,8 +541,8 @@
         functools.partial(input_back_body, steps),
         grid=(2 * steps,),
         in_specs=[whole, whole, near, far, near, far],
-        out_specs=pl.BlockSpec((m, tile), lambda i: (0, i)),
-        out_shape=jax.ShapeDtypeStruct((m, 2 * k), BF),
+        out_specs=[pl.BlockSpec((m // 2, tile), lambda i: (0, i))] * 2,
+        out_shape=[jax.ShapeDtypeStruct((m // 2, 2 * k), BF)] * 2,
         cost_estimate=FREE,
         name="input_back",
     )(grad_gate, grad_up, *gate, *up)
@@ -564,15 +659,18 @@
     query = swap_seq(after(query, key_value))
     qkv_full = jnp.concatenate([q_full, kv_full], axis=1)
     up_near = gather_z(up_mine)
-    down_near = gather_z(down_weight)
     grad_output = cotangent[0]
     grad_all = gather_peers(grad_output, fwd)
+    query, key_value, up_near = lax.optimization_barrier((query, key_value, up_near))
     mixed = attend(query, key_value, start, window)
-    mixed, gate_far, up_near = lax.optimization_barrier((mixed, gate_far, up_near))
+    mixed, gate_far = lax.optimization_barrier((mixed, gate_far))
+    if own_head:
+        out_near = after(out_near, mixed)
     up_far = gather_far(up_near, fwd_rows)
     mixed = swap_seq(mixed)
     if own_head:
         out_full = merge_att(out_near, gather_far(out_near, att_rows))
+    down_near = gather_z(down_weight)
     mixed, up_far, grad_all, qkv_full, out_full = lax.optimization_barrier(
         (mixed, up_far, grad_all, qkv_full, out_full)
     )
@@ -586,39 +684,37 @@
         return x.reshape(seq, rpg, t, LANES)
 
     mixed = token_rows(mixed)
-    hidden = inputs + reduce_peers(dot(mixed, out_full, BF), att)
-    hidden, down_near = lax.optimization_barrier((hidden, down_near))
-
-    unit_two, scale_two = norm_stats(hidden)
-    normed_two = (unit_two * gain_two + shift_two).astype(BF)
-    down_far = gather_far(down_near, fwd_rows)
+    branch_one = halves_of(dot, mixed, out_full)
     if pair:
         here_x = lax.axis_index("x")
-        normed_two = regroup(split_body, here_x, normed_two, "own_first")
+        branch_one = reduce_pieces(branch_one, att)
+        hidden, normed_two = hidden_norm(here_x, tokens_in[0], branch_one, gain_two, shift_two)
         gate_full, up_full = (gate_near, gate_far), (up_near, up_far)
     else:
+        hidden = inputs + reduce_peers(branch_one, att)
+        unit_two, scale_two = norm_stats(hidden)
+        normed_two = (unit_two * gain_two + shift_two).astype(BF)
         gate_full = jnp.split(merge_ff(gate_near, gate_far), 2)
         up_full = jnp.split(merge_ff(up_near, up_far), 2)
+    ready = branch_one[2] if pair else normed_two
+    down_far = gather_far(after(down_near, ready), fwd_rows)
     normed_two_all = gather_peers(normed_two, fwd)
     gate, up, act = hidden_units(normed_two_all, gate_full, up_full)
     down_full = merge_ff(down_near, after(down_far, gate))
-    down_part = dot(act, down_full, BF)
 
     send_att = functools.partial(send_rows, axis=att_rows, nz=nz, na=ny)
     send_ff = functools.partial(send_rows, axis=fwd_rows, nz=nz, na=nx if pair else ny)
     wide = width // 2
     down_one = send_ff(dot_tn(act, grad_all[:, :wide], BF))
-    down_two = dot_tn(act, grad_all[:, wide:], BF)
     grad_gate, grad_up = hidden_back(grad_all, down_full, gate, up, t)
     part = input_back(grad_gate, grad_up, gate_full, up_full)
-    branch_two = reduce_peers(down_part, fwd)
     down_one = add_rows(*down_one)
-    part, branch_two, down_one, down_two = lax.optimization_barrier(
-        (part, branch_two, down_one, down_two)
-    )
-    down_two = send_ff(down_two)
-    block_out = (hidden + branch_two).astype(BF).reshape(tokens_in.shape)
-    grad_normed_two = reduce_peers(part, fwd)
+    part, down_one = lax.optimization_barrier((part, down_one))
+    down_two = send_ff(dot_tn(act, grad_all[:, wide:], BF))
+    if pair:
+        grad_normed_two = reduce_pieces(part, fwd)
+    else:
+        grad_normed_two = reduce_peers(part, fwd)
 
     def dots(g):
         if not pair:
@@ -642,43 +738,56 @@
     )
     down_two = scatter_z(down_two)
     if pair:
-        grad_normed_two = regroup(join_body, here_x, grad_normed_two, "own_back")
-    back, grad_gain_two, grad_shift_two = norm_back(grad_normed_two, unit_two, scale_two, gain_two)
-    grad_hidden = grad_output.astype(F32) + back
-
-    def ff_columns(*parts):
-        g = jnp.concatenate(parts, axis=1)
-        g = swap_peers(g.reshape(peers, rows, -1), fwd_axes)
+        grad_hidden, branch, sums = hidden_norm_back(
+            here_x, hidden, grad_output, grad_normed_two, gain_two
+        )
+        grad_gain_two, grad_shift_two = sums[0], sums[1]
+    else:
+        back, grad_gain_two, grad_shift_two = norm_back(
+            grad_normed_two, unit_two, scale_two, gain_two
+        )
+        grad_hidden = grad_output.astype(F32) + back
+        branch = grad_hidden.astype(BF)
+
+    def ff_swap(g):
+        return swap_peers(g.reshape(peers, rows, -1), fwd_axes)
+
+    def ff_columns(g):
         if pair:
             g = g.reshape(2, nc, rows, nz, 2, strip).transpose(2, 3, 0, 4, 1, 5)
         else:
             g = g.reshape(peers, rows, seq, strip).transpose(1, 2, 0, 3)
         return g.reshape(rows, ff).astype(F32)
 
-    branch = gather_peers(grad_hidden.astype(BF), att)
+    branch = gather_peers(branch, att)
     grad_mixed = head_rows(dot_nt(branch, out_full, BF))
     grad_mixed, down_two = lax.optimization_barrier((grad_mixed, down_two))
+    branch_two = reduce_peers(halves_of(dot, after(act, grad_mixed), down_full), fwd)
+    block_out = (hidden + branch_two).astype(BF).reshape(tokens_in.shape)
     grad_mixed = swap_seq(grad_mixed)
     grad_out = dot_tn(mixed, branch, BF)
+    if pair:
+        near, far, grad_out = lax.optimization_barrier((*gate_one, grad_out))
+        gate_one = near, far
     gate_one = add_rows(*gate_one)
-    grad_mixed, gate_one, grad_out = lax.optimization_barrier((grad_mixed, gate_one, grad_out))
+    grad_mixed, gate_one = lax.optimization_barrier((grad_mixed, gate_one))
     gate_one = scatter_z(gate_one)
     grad_qkv = attend_back(query, key_value, start, grad_mixed, window)
     if own_head:
         grad_out = send_att(grad_out)
-    grad_qkv, gate_one, gate_two = lax.optimization_barrier((grad_qkv, gate_one, gate_two))
+    grad_qkv, gate_one, gate_two, grad_out = lax.optimization_barrier(
+        (grad_qkv, gate_one, gate_two, grad_out)
+    )
+    if own_head:
+        grad_out = scatter_z(add_rows(*grad_out))
     gate_two = scatter_z(add_rows(*gate_two))
     grad_qkv = swap_seq(grad_qkv)
     grad_down = jnp.concatenate([down_one, down_two], axis=1).astype(F32)
-    up_w = add_rows(*up_w)
-    if own_head:
-        grad_out = add_rows(*grad_out)
-    grad_qkv, up_w, grad_out, grad_down, gate_two = lax.optimization_barrier(
-        (grad_qkv, up_w, grad_out, grad_down, gate_two)
-    )
-    if own_head:
-        grad_out = scatter_z(grad_out)
-    up_w = scatter_z(up_w)
+    up_sum = add_rows(*up_w)
+    up_w = scatter_z(up_sum)
+    grad_qkv, up_sum, grad_out, grad_down, block_out = lax.optimization_barrier(
+        (grad_qkv, up_sum, grad_out, grad_down, block_out)
+    )
     if not own_head:
         mine = (jnp.arange(peers) == me_peer).astype(BF)[None, :, None, None]
         grad_out = grad_out.reshape(heads, 1, HEAD_DIM, width) * mine
@@ -686,14 +795,17 @@
             grad_out.reshape(width, width), ALL, scatter_dimension=0, tiled=True
         )
     grad_proj = rotary_in(grad_qkv, cosine, sine, pairs)
+    gate_w = ff_swap(jnp.concatenate([gate_one, gate_two], axis=1))
     cut = 3 * third // 2
-    first = dot_tn(normed_all, grad_proj[:, :cut], BF)
+    first = send_att(dot_tn(normed_all, grad_proj[:, :cut], BF))
     second = dot_tn(normed_all, grad_proj[:, cut:], BF)
-    grad_proj, first, second, grad_out = lax.optimization_barrier(
-        (grad_proj, first, second, grad_out)
-    )
-    first, second = send_att(first), send_att(second)
-    grad_normed = reduce_peers(dot_nt(grad_proj, qkv_full, BF), att)
+    grad_normed = halves_of(dot_nt, grad_proj, qkv_full)
+    grad_normed, first, second, gate_w = lax.optimization_barrier(
+        (grad_normed, first, second, gate_w)
+    )
+    grad_gate_w = ff_columns(gate_w)
+    second = send_att(second)
+    grad_normed = reduce_peers(grad_normed, att)
     first = add_rows(*first)
     first, up_w = lax.optimization_barrier((first, up_w))
     if pair:
@@ -702,18 +814,19 @@
     back, grad_gain_one, grad_shift_one = norm_back(grad_normed, unit_one, scale_one, gain_one)
     grad_tokens = (grad_hidden + back).astype(BF).reshape(tokens_in.shape)
     second = add_rows(*second)
-    second, first, grad_tokens, gate_one, gate_two, up_w = lax.optimization_barrier(
-        (second, first, grad_tokens, gate_one, gate_two, up_w)
+    second, first, grad_tokens, up_w, grad_gate_w = lax.optimization_barrier(
+        (second, first, grad_tokens, up_w, grad_gate_w)
     )
     second = scatter_z(second)
-    grad_gate_w = ff_columns(gate_one, gate_two)
-    grad_up_w = ff_columns(up_w)
-    second, grad_gate_w, grad_up_w = lax.optimization_barrier((second, grad_gate_w, grad_up_w))
+    grad_up_w = ff_columns(ff_swap(up_w))
+    second, grad_up_w = lax.optimization_barrier((second, grad_up_w))
     grad_out = grad_out.astype(F32)
-    grad_qkv_w = jnp.concatenate([first, second], axis=1)
-    grad_qkv_w = swap_peers(grad_qkv_w.reshape(peers, rows, -1), BATCH)
-    grad_qkv_w = grad_qkv_w.reshape(peers, rows, 3, heads, HEAD_DIM).transpose(1, 2, 3, 0, 4)
-    grad_qkv_w = grad_qkv_w.reshape(rows, 3 * width).astype(F32)
+    grad_qkv_w = []
+    for half in (first, second):
+        half = swap_peers(half.reshape(peers, rows, -1), BATCH)
+        half = half.reshape(peers, rows, -1, HEAD_DIM).transpose(1, 2, 0, 3)
+        grad_qkv_w.append(half.reshape(rows, -1).astype(F32))
+    grad_qkv_w = jnp.concatenate(grad_qkv_w, axis=1)
     grad_bias = jnp.sum(grad_proj.astype(F32), axis=0).reshape(3, heads, 1, HEAD_DIM)
     mine = (jnp.arange(peers) == me_peer).astype(F32)[None, None, :, None]
     grad_bias = (grad_bias * mine).reshape(devices, -1)

time: 1050 us -> 974 us (0.928)
  waiting for transfers between devices: 472 us -> 407 us
  blocking collectives: 29.8 us -> 41.5 us
  other arithmetic: 86.7 us -> 76.2 us
    ppermute x4 -> x2, waiting for transfers between devices: 43.7 us -> 0.01 us  [reduce_peers(): last = lax.ppermute(send, axis, SWAP)]
    ppermute x6, waiting for transfers between devices: 79.4 us -> 107 us  [gather_far(): return lax.ppermute(near, axis, SWAP)]
    ppermute x4 -> x6, waiting for transfers between devices: 4.15 us -> 27.7 us  [the longest x2 26.4 us: reduce_pieces(): return (near, got, lax.ppermute(send, axis, SWAP))]
    ppermute x5, waiting for transfers between devices: 104 us -> 81.3 us  [gather_peers(): other = lax.ppermute(x, axis, SWAP)]
    ppermute x5, waiting for transfers between devices: 60.8 us -> 42.6 us  [send_rows(): return (keep, lax.ppermute(send, axis, SWAP))]
    all_to_all x5, waiting for transfers between devices: 56.1 us -> 38 us  [swap_seq(): return lax.all_to_all(x, SEQ, split_axis=0, concat_axis=0, tiled=True)]
    all_to_all x0 -> x1, blocking collectives: none -> 11.3 us  [local(): lax.all_to_all(vectors, ALL, split_axis=0, concat_axis=0, tiled=True)]
    dot_general x4 -> x6, matrix products: 26.5 us -> 36.9 us  [dot(): return jnp.dot(a, b, preferred_element_type=out)]
  transfers between devices with their start and end apart: 61 -> 61, of which waited for: 28 -> 26; matrix products, arithmetic and copies ran while one was open for 23% -> 26% of each run, Pallas kernels for 14% -> 15%
where the time goes in v4:
time: 974 us; the launch traced here: 963 us
  waiting for transfers between devices  407 us (42%)
  Pallas kernels  149 us (15%)
  matrix products  110 us (11%)
  local copies, waits for them, and re-layouts  89 us (9%)
  other arithmetic  76.2 us (8%)
  starting transfers between devices  74.8 us (8%)
  blocking collectives  41.5 us (4%)
  between operations  15.2 us (2%)
    ppermute x6, waiting for transfers between devices, gather_far(): return lax.ppermute(near, axis, SWAP)  107 us
    ppermute x5, waiting for transfers between devices, gather_peers(): other = lax.ppermute(x, axis, SWAP)  81.3 us
    ppermute x3, waiting for transfers between devices, send_columns(): return (g[1], lax.ppermute(g[0], 'x', SWAP))  65 us
    dot_general x11, matrix products, dot_tn(): lax.dot_general(a, b, (((0,), (0,)), ((), ())), preferred_element_type=out)  61.6 us
    ppermute x5, waiting for transfers between devices, send_rows(): return (keep, lax.ppermute(send, axis, SWAP))  42.6 us
    all_to_all x5, waiting for transfers between devices, swap_seq(): return lax.all_to_all(x, SEQ, split_axis=0, concat_axis=0, tiled=True)  38 us
    dot_general x6, matrix products, dot(): return jnp.dot(a, b, preferred_element_type=out)  36.9 us
    pallas_call x1, Pallas kernels, attend_back(): pl.pallas_call(functools.partial(backward_body, window), grid=(rpg, block...  35.5 us
  transfers between devices with their start and end apart: 61, of which 26 were waited for; matrix products, arithmetic and copies ran while one was open for 26% of the time, Pallas kernels for 15%

profile of v4, /device:TPU:0, one launch (start us, length us, event | category | flops | bytes accessed | tf_op | source)
XLA Modules:
  0.0 962.9 jit_solution(9065431979024223893)
XLA Ops:
  11.0 15.8 %all_to_all.70 = bf16[4,64,1536]{2,1,0:T(8,128)(2,1)S(1)} all-to-all(bf16[4,64,1536]{2,1,0:T(8,128)(2,1)S(1)} %reshape.445), channel_id=1, replica_groups=mesh['z'=4,'y'=2,'x'=2,'c'=2] {'x','c'}, dimensions={0} | all-to-all | bytes 1572864 | tf_op jit(solution)/shard_map/all_to_all | solution.py:125
  54.2 17.1 %all-to-all-done.2 = bf16[4,128,1408]{2,1,0:T(8,128)(2,1)S(1)} async-done(((bf16[4,128,1408]{2,1,0:T(8,128)(2,1)}), bf16[4,128,1408]{2,1,0:T(8,128)(2,1)S(1)}, u32[]{:S(2)}, u32[]{:S(2)}) %all-to-all-start.2) | async-done | bytes 1441824 | tf_op jit(solution)/shard_map/all_to_all | solution.py:125
  79.8 22.8 %collective-permute-done.4 = s32[1,2048]{1,0:T(1,128)S(1)} collective-permute-done((s32[1,2048]{1,0:T(1,128)S(1)}, s32[1,2048]{1,0:T(1,128)S(1)}, u32[]{:S(2)}, u32[]{:S(2)}) %collective-permute-start.4) | collective-permute-done | bytes 8224 | tf_op jit(solution)/shard_map/ppermute | solution.py:44
  105.2 16.4 %collective-permute-done.3 = bf16[1024,1024]{1,0:T(8,128)(2,1)S(1)} collective-permute-done((bf16[1024,1024]{1,0:T(8,128)(2,1)}, bf16[1024,1024]{1,0:T(8,128)(2,1)S(1)}, u32[]{:S(2)}, u32[]{:S(2)}) %collective-permute-start.3) | collective-permute-done | bytes 2097184 | tf_op jit(solution)/shard_map/ppermute | solution.py:82
  156.0 43.5 %collective-permute-done.7 = bf16[1024,512]{1,0:T(8,128)(2,1)S(1)} collective-permute-done((bf16[1024,512]{1,0:T(8,128)(2,1)S(1)}, bf16[1024,512]{1,0:T(8,128)(2,1)S(1)}, u32[]{:S(2)}, u32[]{:S(2)}) %collective-permute-start.7) | collective-permute-done | bytes 1048608 | tf_op jit(solution)/shard_map/ppermute | solution.py:82
  213.5 22.6 %all-to-all-done.3.k_ref.v_ref = bf16[8,2,2,256,128]{4,3,2,1,0:T(8,128)(2,1)S(1)} async-done(((bf16[8,2,2,256,128]{4,3,2,1,0:T(8,128)(2,1)}), bf16[8,2,2,256,128]{4,3,2,1,0:T(8,128)(2,1)S(1)}, u32[]{:S(2)}, u32[]{:S(2)}) %all-to-all-start.3) | async-done | bytes 2097184 | tf_op jit(solution)/shard_map/all_to_all | solution.py:129
  243.3 33.0 %collective-permute-done.10 = bf16[256,2048]{1,0:T(8,128)(2,1)} collective-permute-done((bf16[256,2048]{1,0:T(8,128)(2,1)}, bf16[256,2048]{1,0:T(8,128)(2,1)}, u32[]{:S(2)}, u32[]{:S(2)}) %collective-permute-start.10) | collective-permute-done | bytes 1048608 | tf_op jit(solution)/shard_map/ppermute | solution.py:44
  281.6 26.7 %attend.1 = bf16[8,2,256,128]{3,2,1,0:T(8,128)(2,1)} custom-call(bf16[8,1,2,256,128]{4,3,2,1,0:T(8,128)(2,1)} %copy-done.7, bf16[8,2,2,256,128]{4,3,2,1,0:T(8,128)(2,1)} %copy-done, bf16[8,2,2,256,128]{4,3,2,1,0:T(8,128)(2,1)} %copy-done, s32[2,8,256,1]{3,2,1,0:T(8,128)} %reshape.496.start_ref), custom_call_target="tpu_custom_call" | custom-call | flops 1 | bytes 1 | tf_op jit(solution)/shard_map/attend/pallas_call | solution.py:285
  322.8 20.4 %collective-permute-done.13 = bf16[256,2048]{1,0:T(8,128)(2,1)} collective-permute-done((bf16[256,2048]{1,0:T(8,128)(2,1)}, bf16[256,2048]{1,0:T(8,128)(2,1)}, u32[]{:S(2)}, u32[]{:S(2)}) %collective-permute-start.13) | collective-permute-done | bytes 1048608 | tf_op jit(solution)/shard_map/ppermute | solution.py:82
  358.8 23.9 %collective-permute-done.15.c_ref = bf16[256,2048]{1,0:T(8,128)(2,1)} collective-permute-done((bf16[256,2048]{1,0:T(8,128)(2,1)}, bf16[256,2048]{1,0:T(8,128)(2,1)}, u32[]{:S(2)}, u32[]{:S(2)}) %collective-permute-start.15) | collective-permute-done | bytes 1048608 | tf_op jit(solution)/shard_map/ppermute | solution.py:67
  389.4 20.0 %all-gather.17.cloned.1.call-done = bf16[704,2048]{1,0:T(8,128)(2,1)} async-done(((bf16[176,2048]{1,0:T(8,128)(2,1)}), bf16[704,2048]{1,0:T(8,128)(2,1)}) %all-gather.17.cloned.1.call-update) | async-done | bytes 2883600 | tf_op jit(solution)/shard_map/all_gather | solution.py:76
  419.8 20.0 %hidden_units.1 = (f32[1024,1408]{1,0:T(8,128)}, f32[1024,1408]{1,0:T(8,128)}, bf16[1024,1408]{1,0:T(8,128)(2,1)}) custom-call(bf16[1024,2048]{1,0:T(8,128)(2,1)} %constant_dynamic-update-slice_fusion.x_ref, bf16[1024,1408]{1,0:T(8,128)(2,1)} %all-gather.13.cloned.1.call-done.gn_ref, bf16[1024,1408]{1,0:T(8,128)(2,1)} %collective-permute-done.8.gf_ref, ...), custom_call_target="tpu_custom_call" | custom-call | flops 1 | bytes 1 | tf_op jit(solution)/shard_map/hidden_units/pallas_call | solution.py:477
  448.8 26.3 %collective-permute-done.16 = bf16[704,2048]{1,0:T(8,128)(2,1)} collective-permute-done((bf16[704,2048]{1,0:T(8,128)(2,1)}, bf16[704,2048]{1,0:T(8,128)(2,1)}, u32[]{:S(2)}, u32[]{:S(2)}) %collective-permute-start.16) | collective-permute-done | bytes 2883616 | tf_op jit(solution)/shard_map/ppermute | solution.py:82
  481.2 14.6 %hidden_back.1 = (bf16[1024,1408]{1,0:T(8,128)(2,1)}, bf16[1024,1408]{1,0:T(8,128)(2,1)}) custom-call(bf16[1024,2048]{1,0:T(8,128)(2,1)} %pad_maximum_fusion.4.grad_ref, bf16[1408,2048]{1,0:T(8,128)(2,1)} %bitcast.129, f32[1024,1408]{1,0:T(8,128)} %get-tuple-element.117.gate_ref, f32[1024,1408]{1,0:T(8,128)} %get-tuple-element.119.up_ref), custom_call_target="tpu_custom_call" | custom-call | flops 1 | bytes 1 | tf_op jit(solution)/shard_map/hidden_back/pallas_call | solution.py:500
  495.8 19.3 %input_back.1 = (bf16[512,2048]{1,0:T(8,128)(2,1)}, bf16[512,2048]{1,0:T(8,128)(2,1)}) custom-call(bf16[1024,1408]{1,0:T(8,128)(2,1)} %get-tuple-element.120.gg_ref, bf16[1024,1408]{1,0:T(8,128)(2,1)} %get-tuple-element.121.gu_ref, bf16[1024,1408]{1,0:T(8,128)(2,1)} %all-gather.13.cloned.1.call-done.gn_ref, ...), custom_call_target="tpu_custom_call" | custom-call | flops 1 | bytes 1 | tf_op jit(solution)/shard_map/input_back/pallas_call | solution.py:540
  571.4 23.3 %collective-permute-done.24 = bf16[256,2048]{1,0:T(8,128)(2,1)S(1)} collective-permute-done((bf16[256,2048]{1,0:T(8,128)(2,1)}, bf16[256,2048]{1,0:T(8,128)(2,1)S(1)}, u32[]{:S(2)}, u32[]{:S(2)}) %collective-permute-start.24) | collective-permute-done | bytes 1048608 | tf_op jit(solution)/shard_map/ppermute | solution.py:44
  612.4 19.5 %collective-permute-done.27 = bf16[1024,768]{1,0:T(8,128)(2,1)} collective-permute-done((bf16[1024,768]{1,0:T(8,128)(2,1)}, bf16[1024,768]{1,0:T(8,128)(2,1)}, u32[]{:S(2)}, u32[]{:S(2)}) %collective-permute-start.27) | collective-permute-done | bytes 1572896 | tf_op jit(solution)/shard_map/ppermute | solution.py:727
  639.4 35.5 %attend_back.1 = bf16[8,3,2,256,128]{4,3,2,1,0:T(8,128)(2,1)} custom-call(bf16[8,1,2,256,128]{4,3,2,1,0:T(8,128)(2,1)} %copy-done.7, bf16[8,2,2,256,128]{4,3,2,1,0:T(8,128)(2,1)} %copy-done, bf16[8,2,2,256,128]{4,3,2,1,0:T(8,128)(2,1)} %copy-done, s32[2,8,256,1]{3,2,1,0:T(8,128)} %reshape.496.start_ref, bf16[8,2,256,128]{3,2,1,0:T(8,128)(2,1)} %copy-done.17), custom_call_target="tpu_custom_call" | custom-call | flops 1 | bytes 1 | tf_op jit(solution)/shard_map/attend_back/pallas_call | solution.py:334
  715.9 45.6 %collective-permute-done.30 = bf16[1024,1408]{1,0:T(8,128)(2,1)} collective-permute-done((bf16[1024,1408]{1,0:T(8,128)(2,1)}, bf16[1024,1408]{1,0:T(8,128)(2,1)}, u32[]{:S(2)}, u32[]{:S(2)}) %collective-permute-start.30) | collective-permute-done | bytes 2883616 | tf_op jit(solution)/shard_map/ppermute | solution.py:727
  774.4 14.9 %all-to-all-done.7 = bf16[8,3,2,256,128]{4,3,2,1,0:T(8,128)(2,1)S(1)} async-done(((bf16[8,3,2,256,128]{4,3,2,1,0:T(8,128)(2,1)}), bf16[8,3,2,256,128]{4,3,2,1,0:T(8,128)(2,1)S(1)}, u32[]{:S(2)}, u32[]{:S(2)}) %all-to-all-start.7) | async-done | bytes 3145760 | tf_op jit(solution)/shard_map/all_to_all | solution.py:129
  830.4 18.0 %collective-permute-done.33 = bf16[4,256,768]{2,1,0:T(8,128)(2,1)} collective-permute-done((bf16[4,256,768]{2,1,0:T(8,128)(2,1)}, bf16[4,256,768]{2,1,0:T(8,128)(2,1)}, u32[]{:S(2)}, u32[]{:S(2)}) %collective-permute-start.33) | collective-permute-done | bytes 1572896 | tf_op jit(solution)/shard_map/ppermute | solution.py:106
  874.3 13.9 %collective-permute-done.34 = bf16[4,256,768]{2,1,0:T(8,128)(2,1)} collective-permute-done((bf16[4,256,768]{2,1,0:T(8,128)(2,1)}, bf16[4,256,768]{2,1,0:T(8,128)(2,1)}, u32[]{:S(2)}, u32[]{:S(2)}) %collective-permute-start.34) | collective-permute-done | bytes 1572896 | tf_op jit(solution)/shard_map/ppermute | solution.py:106
  900.4 11.3 %all_to_all.71 = f32[32,1,448]{2,1,0:T(1,128)S(1)} all-to-all(f32[32,1,448]{2,1,0:T(1,128)S(1)} %all_to_all.52), channel_id=1, replica_groups=mesh['z'=4,'y'=2,'x'=2,'c'=2] {'z','y','x','c'}, dimensions={0} | all-to-all | bytes 114688 | tf_op jit(solution)/shard_map/all_to_all | solution.py:837
  911.7 14.4 %all_to_all.72 = bf16[4,64,1408]{2,1,0:T(8,128)(2,1)S(1)} all-to-all(bf16[4,64,1408]{2,1,0:T(8,128)(2,1)} %bitcast.191), channel_id=1, replica_groups=mesh['z'=4,'y'=2,'x'=2,'c'=2] {'y','c'}, dimensions={0} | all-to-all | bytes 1441792 | tf_op jit(solution)/shard_map/all_to_all | solution.py:125
  (379 shorter events, 409.0 us)
Async XLA Ops:
  7.2 66.9 %all-gather.7.cloned.1.call-start = ((), (), s32[]{:S(2)}) async-start(), calls=%async_computation.21 | async-start | bytes 2621440 | tf_op jit(solution)/shard_map/all_gather | solution.py:76
  52.6 52.5 %all-gather.9.cloned.1.call-start = ((), (), s32[]{:S(2)}) async-start(), calls=%async_computation.22 | async-start | bytes 1310720 | tf_op jit(solution)/shard_map/all_gather | solution.py:76
  53.7 147.5 %all-gather.13.cloned.1.call-start = ((), (), s32[]{:S(2)}) async-start(), calls=%async_computation.24 | async-start | bytes 3604480 | tf_op jit(solution)/shard_map/all_gather | solution.py:76
  74.0 47.5 %collective-permute-start.3 = (bf16[1024,1024]{1,0:T(8,128)(2,1)}, bf16[1024,1024]{1,0:T(8,128)(2,1)S(1)}, u32[]{:S(2)}, u32[]{:S(2)}) collective-permute-start(bf16[1024,1024]{1,0:T(8,128)(2,1)} %all-gather.7.cloned.1.call-done), channel_id=1, source_target_pairs={{0,4},{4,0},{1,5},{5,1},{2,6},{6,2},{3,7},{7,3},{8,12},{12,8},{9,1... | collective-permute-start | bytes 6291464 | tf_op jit(solution)/shard_map/ppermute | solution.py:82
  149.1 87.0 %all-to-all-start.3 = ((bf16[8,2,2,256,128]{4,3,2,1,0:T(8,128)(2,1)}), bf16[8,2,2,256,128]{4,3,2,1,0:T(8,128)(2,1)S(1)}, u32[]{:S(2)}, u32[]{:S(2)}) async-start(bf16[8,2,2,256,128]{4,3,2,1,0:T(8,128)(2,1)} %bitcast.143), calls=%async_computation.3 | async-start | bytes 4194304 | tf_op jit(solution)/shard_map/all_to_all | solution.py:129
  152.9 123.5 %all-gather.11.cloned.1.call-start = ((), (), s32[]{:S(2)}) async-start(), calls=%async_computation.23 | async-start | bytes 3604480 | tf_op jit(solution)/shard_map/all_gather | solution.py:76
  201.2 107.1 %collective-permute-start.8 = (bf16[1024,1408]{1,0:T(8,128)(2,1)}, bf16[1024,1408]{1,0:T(8,128)(2,1)}, u32[]{:S(2)}, u32[]{:S(2)}) collective-permute-start(bf16[1024,1408]{1,0:T(8,128)(2,1)} %all-gather.13.cloned.1.call-done.gn_ref), channel_id=1, source_target_pairs={{0,2},{2,0},{1,3},{3,1},{4,6},{6,4},{5,7},{7,5},{8,10},{10,8},{9,1... | collective-permute-start | bytes 8650760 | tf_op jit(solution)/shard_map/ppermute | solution.py:82
  240.7 67.6 %all-gather.15.cloned.1.call-start = ((), (), s32[]{:S(2)}) async-start(), calls=%async_computation.25 | async-start | bytes 1310720 | tf_op jit(solution)/shard_map/all_gather | solution.py:76
  243.3 70.8 %collective-permute-start.11 = (bf16[256,2048]{1,0:T(8,128)(2,1)}, bf16[256,2048]{1,0:T(8,128)(2,1)}, u32[]{:S(2)}, u32[]{:S(2)}) collective-permute-start(bf16[256,2048]{1,0:T(8,128)(2,1)} %bitcast.171), channel_id=1, source_target_pairs={{0,1},{1,0},{2,3},{3,2},{4,5},{5,4},{6,7},{7,6},{8,9},{9,8},{10,11... | collective-permute-start | bytes 3145736 | tf_op jit(solution)/shard_map/ppermute | solution.py:45
  276.9 67.9 %collective-permute-start.9 = (bf16[1024,1408]{1,0:T(8,128)(2,1)}, bf16[1024,1408]{1,0:T(8,128)(2,1)}, u32[]{:S(2)}, u32[]{:S(2)}) collective-permute-start(bf16[1024,1408]{1,0:T(8,128)(2,1)} %all-gather.11.cloned.1.call-done.un_ref), channel_id=1, source_target_pairs={{0,2},{2,0},{1,3},{3,1},{4,6},{6,4},{5,7},{7,5},{8,10},{10,8},{9,1... | collective-permute-start | bytes 8650760 | tf_op jit(solution)/shard_map/ppermute | solution.py:82
  314.0 95.4 %all-gather.17.cloned.1.call-start = ((), (), s32[]{:S(2)}) async-start(), calls=%async_computation.26 | async-start | bytes 3604480 | tf_op jit(solution)/shard_map/all_gather | solution.py:76
  350.8 211.9 %reduce-scatter.9.cloned.1.call-start = ((), (), s32[]{:S(2)}) async-start(), calls=%async_computation.27 | async-start | bytes 1802240 | tf_op jit(solution)/shard_map/reduce_scatter | solution.py:117
  409.4 65.7 %collective-permute-start.16 = (bf16[704,2048]{1,0:T(8,128)(2,1)}, bf16[704,2048]{1,0:T(8,128)(2,1)}, u32[]{:S(2)}, u32[]{:S(2)}) collective-permute-start(bf16[704,2048]{1,0:T(8,128)(2,1)} %all-gather.17.cloned.1.call-done), channel_id=1, source_target_pairs={{0,2},{2,0},{1,3},{3,1},{4,6},{6,4},{5,7},{7,5},{8,10},{10,8},{9,1... | collective-permute-start | bytes 8650760 | tf_op jit(solution)/shard_map/ppermute | solution.py:82
  448.2 66.8 %collective-permute-start.20 = (bf16[4,176,1024]{2,1,0:T(8,128)(2,1)}, bf16[4,176,1024]{2,1,0:T(8,128)(2,1)S(1)}, u32[]{:S(2)}, u32[]{:S(2)}) collective-permute-start(bf16[4,176,1024]{2,1,0:T(8,128)(2,1)} %dynamic-slice_bitcast_fusion.4), channel_id=1, source_target_pairs={{0,2},{2,0},{1,3},{3,1},{4,6},{6,4},{5,7},{7,5},{8,10},{10,8},{9,1... | collective-permute-start | bytes 4325384 | tf_op jit(solution)/shard_map/ppermute | solution.py:106
  518.1 84.6 %reduce-scatter.11.cloned.1.call-start = ((), (), s32[]{:S(2)}) async-start(), calls=%async_computation.28 | async-start | bytes 1802240 | tf_op jit(solution)/shard_map/reduce_scatter | solution.py:117
  606.3 68.6 %reduce-scatter.13.cloned.1.call-start = ((), (), s32[]{:S(2)}) async-start(), calls=%async_computation.29 | async-start | bytes 1966080 | tf_op jit(solution)/shard_map/reduce_scatter | solution.py:117
  634.9 137.6 %reduce-scatter.17.cloned.1.call-start = ((), (), s32[]{:S(2)}) async-start(), calls=%async_computation.31 | async-start | bytes 1638400 | tf_op jit(solution)/shard_map/reduce_scatter | solution.py:117
  678.1 111.3 %all-to-all-start.7 = ((bf16[8,3,2,256,128]{4,3,2,1,0:T(8,128)(2,1)}), bf16[8,3,2,256,128]{4,3,2,1,0:T(8,128)(2,1)S(1)}, u32[]{:S(2)}, u32[]{:S(2)}) async-start(bf16[8,3,2,256,128]{4,3,2,1,0:T(8,128)(2,1)} %attend_back.1), calls=%async_computation.10 | async-start | bytes 6291456 | tf_op jit(solution)/shard_map/all_to_all | solution.py:129
  681.7 111.9 %reduce-scatter.15.cloned.1.call-start = ((), (), s32[]{:S(2)}) async-start(), calls=%async_computation.30 | async-start | bytes 1310720 | tf_op jit(solution)/shard_map/reduce_scatter | solution.py:117
  696.4 65.0 %collective-permute-start.30 = (bf16[1024,1408]{1,0:T(8,128)(2,1)}, bf16[1024,1408]{1,0:T(8,128)(2,1)}, u32[]{:S(2)}, u32[]{:S(2)}) collective-permute-start(bf16[1024,1408]{1,0:T(8,128)(2,1)} %fusion.28), channel_id=1, source_target_pairs={{0,2},{2,0},{1,3},{3,1},{4,6},{6,4},{5,7},{7,5},{8,10},{10,8},{9,1... | collective-permute-start | bytes 8650760 | tf_op jit(solution)/shard_map/ppermute | solution.py:727
  698.4 157.3 %reduce-scatter.19.cloned.1.call-start = ((), (), s32[]{:S(2)}) async-start(), calls=%async_computation.32 | async-start | bytes 3604480 | tf_op jit(solution)/shard_map/reduce_scatter | solution.py:117
  708.7 60.2 %collective-permute-start.32 = (bf16[256,2048]{1,0:T(8,128)(2,1)}, bf16[256,2048]{1,0:T(8,128)(2,1)}, u32[]{:S(2)}, u32[]{:S(2)}) collective-permute-start(bf16[256,2048]{1,0:T(8,128)(2,1)} %add_convert_fusion.6), channel_id=1, source_target_pairs={{0,4},{4,0},{1,5},{5,1},{2,6},{6,2},{3,7},{7,3},{8,12},{12,8},{9,1... | collective-permute-start | bytes 3145736 | tf_op jit(solution)/shard_map/ppermute | solution.py:58
  793.5 104.7 %reduce-scatter.21.cloned.1.call-start = ((), (), s32[]{:S(2)}) async-start(), calls=%async_computation.33 | async-start | bytes 1966080 | tf_op jit(solution)/shard_map/reduce_scatter | solution.py:117
  855.7 86.1 %reduce-scatter.23.cloned.1.call-start = ((), (), s32[]{:S(2)}) async-start(), calls=%async_computation.34 | async-start | bytes 1966080 | tf_op jit(solution)/shard_map/reduce_scatter | solution.py:117
  (92 other events, 1589.2 us)
Sparse Core Ops, SparseCore 0:
  27.8 46.1 all-gather.6
  76.2 26.5 all-gather.8
  104.9 62.1 all-gather.12
  169.1 105.1 all-gather.10
  275.7 26.1 all-gather.14
  350.9 58.4 all-gather.16
  518.3 32.2 reduce-scatter.8
  571.4 31.2 reduce-scatter.10
  635.0 34.2 reduce-scatter.12
  678.2 47.7 reduce-scatter.16
  728.8 51.5 reduce-scatter.14
  782.6 56.4 reduce-scatter.18
  855.8 32.8 reduce-scatter.20
  898.4 35.0 reduce-scatter.22

commit v5 on v4

--- a/solution.py
+++ b/solution.py
@@ -485,8 +485,9 @@
     )(x, *gate, *up)
 
 
-def hidden_back_body(grad_ref, down_ref, gate_ref, up_ref, gg_ref, gu_ref):
-    grad = dot_nt(grad_ref[...], down_ref[...])
+def hidden_back_body(grad_ref, one_ref, two_ref, gate_ref, up_ref, gg_ref, gu_ref):
+    k = one_ref.shape[1]
+    grad = dot_nt(grad_ref[:, :k], one_ref[...]) + dot_nt(grad_ref[:, k:], two_ref[...])
     gate = gate_ref[...]
     sigmoid = jax.nn.sigmoid(gate)
     gg_ref[...] = (grad * up_ref[...] * sigmoid * (1.0 + gate * (1.0 - sigmoid))).astype(BF)
@@ -495,14 +496,15 @@
 
 def hidden_back(grad, down, gate, up, t):
     m, width = grad.shape
-    n = down.shape[0]
+    n, k = down[0].shape
     tile = pl.BlockSpec((t, n), lambda i: (i, 0))
     return pl.pallas_call(
         hidden_back_body,
         grid=(m // t,),
         in_specs=[
             pl.BlockSpec((t, width), lambda i: (i, 0)),
-            pl.BlockSpec((n, width), lambda i: (0, 0)),
+            pl.BlockSpec((n, k), lambda i: (0, 0)),
+            pl.BlockSpec((n, k), lambda i: (0, 0)),
             tile,
             tile,
         ],
@@ -510,7 +512,7 @@
         out_shape=[jax.ShapeDtypeStruct((m, n), BF)] * 2,
         cost_estimate=FREE,
         name="hidden_back",
-    )(grad, down, gate, up)
+    )(grad, *down, gate, up)
 
 
 def input_back_body(steps, gg_ref, gu_ref, gn_ref, gf_ref, un_ref, uf_ref, one_ref, two_ref):
@@ -670,7 +672,8 @@
     mixed = swap_seq(mixed)
     if own_head:
         out_full = merge_att(out_near, gather_far(out_near, att_rows))
-    down_near = gather_z(down_weight)
+    wide = width // 2
+    down_near = gather_z(down_weight[:, :wide]), gather_z(down_weight[:, wide:])
     mixed, up_far, grad_all, qkv_full, out_full = lax.optimization_barrier(
         (mixed, up_far, grad_all, qkv_full, out_full)
     )
@@ -696,15 +699,16 @@
         normed_two = (unit_two * gain_two + shift_two).astype(BF)
         gate_full = jnp.split(merge_ff(gate_near, gate_far), 2)
         up_full = jnp.split(merge_ff(up_near, up_far), 2)
-    ready = branch_one[2] if pair else normed_two
-    down_far = gather_far(after(down_near, ready), fwd_rows)
+    down_one, down_two = down_near
+    normed_two, down_one = lax.optimization_barrier((normed_two, down_one))
+    down_far = [gather_far(w, fwd_rows) for w in (down_one, after(down_two, normed_two))]
     normed_two_all = gather_peers(normed_two, fwd)
+    normed_two_all, down_far[0] = lax.optimization_barrier((normed_two_all, down_far[0]))
     gate, up, act = hidden_units(normed_two_all, gate_full, up_full)
-    down_full = merge_ff(down_near, after(down_far, gate))
+    down_full = [merge_ff(near, after(far, gate)) for near, far in zip(down_near, down_far)]
 
     send_att = functools.partial(send_rows, axis=att_rows, nz=nz, na=ny)
     send_ff = functools.partial(send_rows, axis=fwd_rows, nz=nz, na=nx if pair else ny)
-    wide = width // 2
     down_one = send_ff(dot_tn(act, grad_all[:, :wide], BF))
     grad_gate, grad_up = hidden_back(grad_all, down_full, gate, up, t)
     part = input_back(grad_gate, grad_up, gate_full, up_full)
@@ -762,6 +766,7 @@
     branch = gather_peers(branch, att)
     grad_mixed = head_rows(dot_nt(branch, out_full, BF))
     grad_mixed, down_two = lax.optimization_barrier((grad_mixed, down_two))
+    down_full = jnp.concatenate([after(down_full[0], grad_mixed), down_full[1]], axis=1)
     branch_two = reduce_peers(halves_of(dot, after(act, grad_mixed), down_full), fwd)
     block_out = (hidden + branch_two).astype(BF).reshape(tokens_in.shape)
     grad_mixed = swap_seq(grad_mixed)

time: 974 us -> 948 us (0.973)
  waiting for transfers between devices: 407 us -> 392 us
    ppermute x6 -> x7, waiting for transfers between devices: 107 us -> 80.3 us  [gather_far(): return lax.ppermute(near, axis, SWAP)]
    ppermute x5, waiting for transfers between devices: 81.3 us -> 102 us  [gather_peers(): other = lax.ppermute(x, axis, SWAP)]
    all_gather x6 -> x7, waiting for transfers between devices: 21.6 us -> 9.72 us  [gather_z(): return lax.all_gather(w, 'z', axis=0, tiled=True)]
    convert_element_type x8 -> x7, other arithmetic: 22.7 us -> 18.7 us  [add_rows(): got = (keep.astype(F32) + got.astype(F32)).astype(BF)]
  transfers between devices with their start and end apart: 61 -> 63, of which waited for: 26 -> 25; matrix products, arithmetic and copies ran while one was open for 26% -> 25% of each run, Pallas kernels for 15% -> 15%
where the time goes in v5:
time: 948 us; the launch traced here: 938 us
  waiting for transfers between devices  392 us (41%)
  Pallas kernels  150 us (16%)
  matrix products  103 us (11%)
  local copies, waits for them, and re-layouts  86.6 us (9%)
  other arithmetic  76.2 us (8%)
  starting transfers between devices  73.7 us (8%)
  blocking collectives  40.8 us (4%)
  between operations  15.2 us (2%)
    ppermute x5, waiting for transfers between devices, gather_peers(): other = lax.ppermute(x, axis, SWAP)  102 us
    ppermute x7, waiting for transfers between devices, gather_far(): return lax.ppermute(near, axis, SWAP)  80.3 us
    ppermute x3, waiting for transfers between devices, send_columns(): return (g[1], lax.ppermute(g[0], 'x', SWAP))  63.3 us
    dot_general x11, matrix products, dot_tn(): lax.dot_general(a, b, (((0,), (0,)), ((), ())), preferred_element_type=out)  57.5 us
    ppermute x5, waiting for transfers between devices, send_rows(): return (keep, lax.ppermute(send, axis, SWAP))  49.7 us
    all_to_all x5, waiting for transfers between devices, swap_seq(): return lax.all_to_all(x, SEQ, split_axis=0, concat_axis=0, tiled=True)  36.7 us
    pallas_call x1, Pallas kernels, attend_back(): pl.pallas_call(functools.partial(backward_body, window), grid=(rpg, block...  35.6 us
    dot_general x6, matrix products, dot(): return jnp.dot(a, b, preferred_element_type=out)  34.2 us
  transfers between devices with their start and end apart: 63, of which 25 were waited for; matrix products, arithmetic and copies ran while one was open for 25% of the time, Pallas kernels for 15%

profile of v5, /device:TPU:0, one launch (start us, length us, event | category | flops | bytes accessed | tf_op | source)
XLA Modules:
  0.0 937.5 jit_solution(17825296272044296174)
XLA Ops:
  11.0 15.8 %all_to_all.70 = bf16[4,64,1536]{2,1,0:T(8,128)(2,1)S(1)} all-to-all(bf16[4,64,1536]{2,1,0:T(8,128)(2,1)S(1)} %reshape.494), channel_id=1, replica_groups=mesh['z'=4,'y'=2,'x'=2,'c'=2] {'x','c'}, dimensions={0} | all-to-all | bytes 1572864 | tf_op jit(solution)/shard_map/all_to_all | solution.py:125
  53.9 17.3 %all-to-all-done.2 = bf16[4,128,1408]{2,1,0:T(8,128)(2,1)S(1)} async-done(((bf16[4,128,1408]{2,1,0:T(8,128)(2,1)}), bf16[4,128,1408]{2,1,0:T(8,128)(2,1)S(1)}, u32[]{:S(2)}, u32[]{:S(2)}) %all-to-all-start.2) | async-done | bytes 1441824 | tf_op jit(solution)/shard_map/all_to_all | solution.py:125
  79.8 22.8 %collective-permute-done.4 = s32[1,2048]{1,0:T(1,128)S(1)} collective-permute-done((s32[1,2048]{1,0:T(1,128)S(1)}, s32[1,2048]{1,0:T(1,128)S(1)}, u32[]{:S(2)}, u32[]{:S(2)}) %collective-permute-start.4) | collective-permute-done | bytes 8224 | tf_op jit(solution)/shard_map/ppermute | solution.py:44
  105.2 16.4 %collective-permute-done.3 = bf16[1024,1024]{1,0:T(8,128)(2,1)S(1)} collective-permute-done((bf16[1024,1024]{1,0:T(8,128)(2,1)}, bf16[1024,1024]{1,0:T(8,128)(2,1)S(1)}, u32[]{:S(2)}, u32[]{:S(2)}) %collective-permute-start.3) | collective-permute-done | bytes 2097184 | tf_op jit(solution)/shard_map/ppermute | solution.py:82
  156.0 43.5 %collective-permute-done.7 = bf16[1024,512]{1,0:T(8,128)(2,1)S(1)} collective-permute-done((bf16[1024,512]{1,0:T(8,128)(2,1)S(1)}, bf16[1024,512]{1,0:T(8,128)(2,1)S(1)}, u32[]{:S(2)}, u32[]{:S(2)}) %collective-permute-start.7) | collective-permute-done | bytes 1048608 | tf_op jit(solution)/shard_map/ppermute | solution.py:82
  213.6 22.5 %all-to-all-done.3.k_ref.v_ref = bf16[8,2,2,256,128]{4,3,2,1,0:T(8,128)(2,1)S(1)} async-done(((bf16[8,2,2,256,128]{4,3,2,1,0:T(8,128)(2,1)}), bf16[8,2,2,256,128]{4,3,2,1,0:T(8,128)(2,1)S(1)}, u32[]{:S(2)}, u32[]{:S(2)}) %all-to-all-start.3) | async-done | bytes 2097184 | tf_op jit(solution)/shard_map/all_to_all | solution.py:129
  243.6 32.8 %collective-permute-done.10 = bf16[256,2048]{1,0:T(8,128)(2,1)} collective-permute-done((bf16[256,2048]{1,0:T(8,128)(2,1)}, bf16[256,2048]{1,0:T(8,128)(2,1)}, u32[]{:S(2)}, u32[]{:S(2)}) %collective-permute-start.10) | collective-permute-done | bytes 1048608 | tf_op jit(solution)/shard_map/ppermute | solution.py:44
  281.6 26.7 %attend.1 = bf16[8,2,256,128]{3,2,1,0:T(8,128)(2,1)} custom-call(bf16[8,1,2,256,128]{4,3,2,1,0:T(8,128)(2,1)} %copy-done.11, bf16[8,2,2,256,128]{4,3,2,1,0:T(8,128)(2,1)} %copy-done, bf16[8,2,2,256,128]{4,3,2,1,0:T(8,128)(2,1)} %copy-done, s32[2,8,256,1]{3,2,1,0:T(8,128)} %reshape.546.start_ref), custom_call_target="tpu_custom_call" | custom-call | flops 1 | bytes 1 | tf_op jit(solution)/shard_map/attend/pallas_call | solution.py:285
  322.8 20.4 %collective-permute-done.13 = bf16[256,2048]{1,0:T(8,128)(2,1)} collective-permute-done((bf16[256,2048]{1,0:T(8,128)(2,1)}, bf16[256,2048]{1,0:T(8,128)(2,1)}, u32[]{:S(2)}, u32[]{:S(2)}) %collective-permute-start.13) | collective-permute-done | bytes 1048608 | tf_op jit(solution)/shard_map/ppermute | solution.py:82
  360.1 23.7 %collective-permute-done.15.c_ref = bf16[256,2048]{1,0:T(8,128)(2,1)} collective-permute-done((bf16[256,2048]{1,0:T(8,128)(2,1)}, bf16[256,2048]{1,0:T(8,128)(2,1)}, u32[]{:S(2)}, u32[]{:S(2)}) %collective-permute-start.15) | collective-permute-done | bytes 1048608 | tf_op jit(solution)/shard_map/ppermute | solution.py:67
  390.8 23.1 %collective-permute-done.16 = bf16[256,2048]{1,0:T(8,128)(2,1)} collective-permute-done((bf16[256,2048]{1,0:T(8,128)(2,1)}, bf16[256,2048]{1,0:T(8,128)(2,1)}, u32[]{:S(2)}, u32[]{:S(2)}) %collective-permute-start.16) | collective-permute-done | bytes 1048608 | tf_op jit(solution)/shard_map/ppermute | solution.py:44
  427.2 20.6 %hidden_units.1 = (f32[1024,1408]{1,0:T(8,128)}, f32[1024,1408]{1,0:T(8,128)}, bf16[1024,1408]{1,0:T(8,128)(2,1)}) custom-call(bf16[1024,2048]{1,0:T(8,128)(2,1)} %pad_maximum_fusion.5.x_ref, bf16[1024,1408]{1,0:T(8,128)(2,1)} %all-gather.14.cloned.1.call-done.gn_ref, bf16[1024,1408]{1,0:T(8,128)(2,1)} %collective-permute-done.8.gf_ref, ...), custom_call_target="tpu_custom_call" | custom-call | flops 1 | bytes 1 | tf_op jit(solution)/shard_map/hidden_units/pallas_call | solution.py:477
  463.5 14.6 %hidden_back.1 = (bf16[1024,1408]{1,0:T(8,128)(2,1)}, bf16[1024,1408]{1,0:T(8,128)(2,1)}) custom-call(bf16[1024,2048]{1,0:T(8,128)(2,1)} %pad_maximum_fusion.4.grad_ref, bf16[1408,1024]{1,0:T(8,128)(2,1)} %bitcast.137, bf16[1408,1024]{1,0:T(8,128)(2,1)} %bitcast.140, f32[1024,1408]{1,0:T(8,128)} %get-tuple-element.126.gate_ref, ...), custom_call_target="tpu_custom_call" | custom-call | flops 1 | bytes 1 | tf_op jit(solution)/shard_map/hidden_back/pallas_call | solution.py:501
  478.1 19.2 %input_back.1 = (bf16[512,2048]{1,0:T(8,128)(2,1)}, bf16[512,2048]{1,0:T(8,128)(2,1)}) custom-call(bf16[1024,1408]{1,0:T(8,128)(2,1)} %get-tuple-element.131.gg_ref, bf16[1024,1408]{1,0:T(8,128)(2,1)} %get-tuple-element.132.gu_ref, bf16[1024,1408]{1,0:T(8,128)(2,1)} %all-gather.14.cloned.1.call-done.gn_ref, ...), custom_call_target="tpu_custom_call" | custom-call | flops 1 | bytes 1 | tf_op jit(solution)/shard_map/input_back/pallas_call | solution.py:542
  523.7 17.3 %collective-permute-done.24 = bf16[4,176,1024]{2,1,0:T(8,128)(2,1)S(1)} collective-permute-done((bf16[4,176,1024]{2,1,0:T(8,128)(2,1)S(1)}, bf16[4,176,1024]{2,1,0:T(8,128)(2,1)S(1)}, u32[]{:S(2)}, u32[]{:S(2)}) %collective-permute-start.24) | collective-permute-done | bytes 1441824 | tf_op jit(solution)/shard_map/ppermute | solution.py:106
  551.4 23.3 %collective-permute-done.25 = bf16[256,2048]{1,0:T(8,128)(2,1)S(1)} collective-permute-done((bf16[256,2048]{1,0:T(8,128)(2,1)}, bf16[256,2048]{1,0:T(8,128)(2,1)S(1)}, u32[]{:S(2)}, u32[]{:S(2)}) %collective-permute-start.25) | collective-permute-done | bytes 1048608 | tf_op jit(solution)/shard_map/ppermute | solution.py:44
  592.6 19.3 %collective-permute-done.28 = bf16[1024,768]{1,0:T(8,128)(2,1)} collective-permute-done((bf16[1024,768]{1,0:T(8,128)(2,1)}, bf16[1024,768]{1,0:T(8,128)(2,1)}, u32[]{:S(2)}, u32[]{:S(2)}) %collective-permute-start.28) | collective-permute-done | bytes 1572896 | tf_op jit(solution)/shard_map/ppermute | solution.py:731
  619.4 35.6 %attend_back.1 = bf16[8,3,2,256,128]{4,3,2,1,0:T(8,128)(2,1)} custom-call(bf16[8,1,2,256,128]{4,3,2,1,0:T(8,128)(2,1)} %copy-done.11, bf16[8,2,2,256,128]{4,3,2,1,0:T(8,128)(2,1)} %copy-done, bf16[8,2,2,256,128]{4,3,2,1,0:T(8,128)(2,1)} %copy-done, s32[2,8,256,1]{3,2,1,0:T(8,128)} %reshape.546.start_ref, bf16[8,2,256,128]{3,2,1,0:T(8,128)(2,1)} %copy-done.21), custom_call_target="tpu_custom_call" | custom-call | flops 1 | bytes 1 | tf_op jit(solution)/shard_map/attend_back/pallas_call | solution.py:334
  690.2 44.0 %collective-permute-done.31 = bf16[1024,1408]{1,0:T(8,128)(2,1)} collective-permute-done((bf16[1024,1408]{1,0:T(8,128)(2,1)}, bf16[1024,1408]{1,0:T(8,128)(2,1)}, u32[]{:S(2)}, u32[]{:S(2)}) %collective-permute-start.31) | collective-permute-done | bytes 2883616 | tf_op jit(solution)/shard_map/ppermute | solution.py:731
  749.4 13.6 %all-to-all-done.7 = bf16[8,3,2,256,128]{4,3,2,1,0:T(8,128)(2,1)S(1)} async-done(((bf16[8,3,2,256,128]{4,3,2,1,0:T(8,128)(2,1)}), bf16[8,3,2,256,128]{4,3,2,1,0:T(8,128)(2,1)S(1)}, u32[]{:S(2)}, u32[]{:S(2)}) %all-to-all-start.7) | async-done | bytes 3145760 | tf_op jit(solution)/shard_map/all_to_all | solution.py:129
  805.7 17.9 %collective-permute-done.34 = bf16[4,256,768]{2,1,0:T(8,128)(2,1)} collective-permute-done((bf16[4,256,768]{2,1,0:T(8,128)(2,1)}, bf16[4,256,768]{2,1,0:T(8,128)(2,1)}, u32[]{:S(2)}, u32[]{:S(2)}) %collective-permute-start.34) | collective-permute-done | bytes 1572896 | tf_op jit(solution)/shard_map/ppermute | solution.py:106
  848.9 14.5 %collective-permute-done.35 = bf16[4,256,768]{2,1,0:T(8,128)(2,1)} collective-permute-done((bf16[4,256,768]{2,1,0:T(8,128)(2,1)}, bf16[4,256,768]{2,1,0:T(8,128)(2,1)}, u32[]{:S(2)}, u32[]{:S(2)}) %collective-permute-start.35) | collective-permute-done | bytes 1572896 | tf_op jit(solution)/shard_map/ppermute | solution.py:106
  875.6 10.7 %all_to_all.71 = f32[32,1,448]{2,1,0:T(1,128)S(1)} all-to-all(f32[32,1,448]{2,1,0:T(1,128)S(1)} %all_to_all.52), channel_id=1, replica_groups=mesh['z'=4,'y'=2,'x'=2,'c'=2] {'z','y','x','c'}, dimensions={0} | all-to-all | bytes 114688 | tf_op jit(solution)/shard_map/all_to_all | solution.py:842
  886.3 14.4 %all_to_all.72 = bf16[4,64,1408]{2,1,0:T(8,128)(2,1)S(1)} all-to-all(bf16[4,64,1408]{2,1,0:T(8,128)(2,1)} %bitcast.201), channel_id=1, replica_groups=mesh['z'=4,'y'=2,'x'=2,'c'=2] {'y','c'}, dimensions={0} | all-to-all | bytes 1441792 | tf_op jit(solution)/shard_map/all_to_all | solution.py:125
  (393 shorter events, 392.3 us)
Async XLA Ops:
  7.2 66.9 %all-gather.8.cloned.1.call-start = ((), (), s32[]{:S(2)}) async-start(), calls=%async_computation.21 | async-start | bytes 2621440 | tf_op jit(solution)/shard_map/all_gather | solution.py:76
  52.6 52.5 %all-gather.10.cloned.1.call-start = ((), (), s32[]{:S(2)}) async-start(), calls=%async_computation.22 | async-start | bytes 1310720 | tf_op jit(solution)/shard_map/all_gather | solution.py:76
  53.7 147.6 %all-gather.14.cloned.1.call-start = ((), (), s32[]{:S(2)}) async-start(), calls=%async_computation.24 | async-start | bytes 3604480 | tf_op jit(solution)/shard_map/all_gather | solution.py:76
  74.0 47.5 %collective-permute-start.3 = (bf16[1024,1024]{1,0:T(8,128)(2,1)}, bf16[1024,1024]{1,0:T(8,128)(2,1)S(1)}, u32[]{:S(2)}, u32[]{:S(2)}) collective-permute-start(bf16[1024,1024]{1,0:T(8,128)(2,1)} %all-gather.8.cloned.1.call-done), channel_id=1, source_target_pairs={{0,4},{4,0},{1,5},{5,1},{2,6},{6,2},{3,7},{7,3},{8,12},{12,8},{9,1... | collective-permute-start | bytes 6291464 | tf_op jit(solution)/shard_map/ppermute | solution.py:82
  149.2 87.0 %all-to-all-start.3 = ((bf16[8,2,2,256,128]{4,3,2,1,0:T(8,128)(2,1)}), bf16[8,2,2,256,128]{4,3,2,1,0:T(8,128)(2,1)S(1)}, u32[]{:S(2)}, u32[]{:S(2)}) async-start(bf16[8,2,2,256,128]{4,3,2,1,0:T(8,128)(2,1)} %bitcast.149), calls=%async_computation.3 | async-start | bytes 4194304 | tf_op jit(solution)/shard_map/all_to_all | solution.py:129
  152.9 123.5 %all-gather.12.cloned.1.call-start = ((), (), s32[]{:S(2)}) async-start(), calls=%async_computation.23 | async-start | bytes 3604480 | tf_op jit(solution)/shard_map/all_gather | solution.py:76
  153.5 46.0 %collective-permute-start.7 = (bf16[1024,512]{1,0:T(8,128)(2,1)S(1)}, bf16[1024,512]{1,0:T(8,128)(2,1)S(1)}, u32[]{:S(2)}, u32[]{:S(2)}) collective-permute-start(bf16[1024,512]{1,0:T(8,128)(2,1)S(1)} %copy-done.33), channel_id=1, source_target_pairs={{0,4},{4,0},{1,5},{5,1},{2,6},{6,2},{3,7},{7,3},{8,12},{12,8},{9,1... | collective-permute-start | bytes 3145736 | tf_op jit(solution)/shard_map/ppermute | solution.py:82
  201.2 107.1 %collective-permute-start.8 = (bf16[1024,1408]{1,0:T(8,128)(2,1)}, bf16[1024,1408]{1,0:T(8,128)(2,1)}, u32[]{:S(2)}, u32[]{:S(2)}) collective-permute-start(bf16[1024,1408]{1,0:T(8,128)(2,1)} %all-gather.14.cloned.1.call-done.gn_ref), channel_id=1, source_target_pairs={{0,2},{2,0},{1,3},{3,1},{4,6},{6,4},{5,7},{7,5},{8,10},{10,8},{9,1... | collective-permute-start | bytes 8650760 | tf_op jit(solution)/shard_map/ppermute | solution.py:82
  240.7 67.6 %all-gather.16.cloned.1.call-start = ((), (), s32[]{:S(2)}) async-start(), calls=%async_computation.25 | async-start | bytes 1310720 | tf_op jit(solution)/shard_map/all_gather | solution.py:76
  243.5 70.6 %collective-permute-start.11 = (bf16[256,2048]{1,0:T(8,128)(2,1)}, bf16[256,2048]{1,0:T(8,128)(2,1)}, u32[]{:S(2)}, u32[]{:S(2)}) collective-permute-start(bf16[256,2048]{1,0:T(8,128)(2,1)} %bitcast.181), channel_id=1, source_target_pairs={{0,1},{1,0},{2,3},{3,2},{4,5},{5,4},{6,7},{7,6},{8,9},{9,8},{10,11... | collective-permute-start | bytes 3145736 | tf_op jit(solution)/shard_map/ppermute | solution.py:45
  276.9 67.9 %collective-permute-start.9 = (bf16[1024,1408]{1,0:T(8,128)(2,1)}, bf16[1024,1408]{1,0:T(8,128)(2,1)}, u32[]{:S(2)}, u32[]{:S(2)}) collective-permute-start(bf16[1024,1408]{1,0:T(8,128)(2,1)} %all-gather.12.cloned.1.call-done.un_ref), channel_id=1, source_target_pairs={{0,2},{2,0},{1,3},{3,1},{4,6},{6,4},{5,7},{7,5},{8,10},{10,8},{9,1... | collective-permute-start | bytes 8650760 | tf_op jit(solution)/shard_map/ppermute | solution.py:82
  314.0 74.8 %all-gather.18.cloned.1.call-start = ((), (), s32[]{:S(2)}) async-start(), calls=%async_computation.26 | async-start | bytes 1802240 | tf_op jit(solution)/shard_map/all_gather | solution.py:76
  351.8 70.2 %all-gather.20.cloned.1.call-start = ((), (), s32[]{:S(2)}) async-start(), calls=%async_computation.27 | async-start | bytes 1802240 | tf_op jit(solution)/shard_map/all_gather | solution.py:76
  358.5 184.2 %reduce-scatter.9.cloned.1.call-start = ((), (), s32[]{:S(2)}) async-start(), calls=%async_computation.28 | async-start | bytes 1802240 | tf_op jit(solution)/shard_map/reduce_scatter | solution.py:117
  500.5 82.5 %reduce-scatter.11.cloned.1.call-start = ((), (), s32[]{:S(2)}) async-start(), calls=%async_computation.29 | async-start | bytes 1802240 | tf_op jit(solution)/shard_map/reduce_scatter | solution.py:117
  586.5 68.6 %reduce-scatter.13.cloned.1.call-start = ((), (), s32[]{:S(2)}) async-start(), calls=%async_computation.30 | async-start | bytes 1966080 | tf_op jit(solution)/shard_map/reduce_scatter | solution.py:117
  656.0 107.0 %all-to-all-start.7 = ((bf16[8,3,2,256,128]{4,3,2,1,0:T(8,128)(2,1)}), bf16[8,3,2,256,128]{4,3,2,1,0:T(8,128)(2,1)S(1)}, u32[]{:S(2)}, u32[]{:S(2)}) async-start(bf16[8,3,2,256,128]{4,3,2,1,0:T(8,128)(2,1)} %attend_back.1), calls=%async_computation.10 | async-start | bytes 6291456 | tf_op jit(solution)/shard_map/all_to_all | solution.py:129
  659.7 87.8 %reduce-scatter.17.cloned.1.call-start = ((), (), s32[]{:S(2)}) async-start(), calls=%async_computation.32 | async-start | bytes 1638400 | tf_op jit(solution)/shard_map/reduce_scatter | solution.py:117
  662.8 105.8 %reduce-scatter.15.cloned.1.call-start = ((), (), s32[]{:S(2)}) async-start(), calls=%async_computation.31 | async-start | bytes 1310720 | tf_op jit(solution)/shard_map/reduce_scatter | solution.py:117
  670.5 63.7 %collective-permute-start.31 = (bf16[1024,1408]{1,0:T(8,128)(2,1)}, bf16[1024,1408]{1,0:T(8,128)(2,1)}, u32[]{:S(2)}, u32[]{:S(2)}) collective-permute-start(bf16[1024,1408]{1,0:T(8,128)(2,1)} %fusion.29), channel_id=1, source_target_pairs={{0,2},{2,0},{1,3},{3,1},{4,6},{6,4},{5,7},{7,5},{8,10},{10,8},{9,1... | collective-permute-start | bytes 8650760 | tf_op jit(solution)/shard_map/ppermute | solution.py:731
  677.3 153.4 %reduce-scatter.19.cloned.1.call-start = ((), (), s32[]{:S(2)}) async-start(), calls=%async_computation.33 | async-start | bytes 3604480 | tf_op jit(solution)/shard_map/reduce_scatter | solution.py:117
  688.3 55.5 %collective-permute-start.33 = (bf16[256,2048]{1,0:T(8,128)(2,1)}, bf16[256,2048]{1,0:T(8,128)(2,1)}, u32[]{:S(2)}, u32[]{:S(2)}) collective-permute-start(bf16[256,2048]{1,0:T(8,128)(2,1)} %add_convert_fusion.6), channel_id=1, source_target_pairs={{0,4},{4,0},{1,5},{5,1},{2,6},{6,2},{3,7},{7,3},{8,12},{12,8},{9,1... | collective-permute-start | bytes 3145736 | tf_op jit(solution)/shard_map/ppermute | solution.py:58
  767.2 106.3 %reduce-scatter.21.cloned.1.call-start = ((), (), s32[]{:S(2)}) async-start(), calls=%async_computation.34 | async-start | bytes 1966080 | tf_op jit(solution)/shard_map/reduce_scatter | solution.py:117
  830.8 85.7 %reduce-scatter.23.cloned.1.call-start = ((), (), s32[]{:S(2)}) async-start(), calls=%async_computation.35 | async-start | bytes 1966080 | tf_op jit(solution)/shard_map/reduce_scatter | solution.py:117
  (99 other events, 1778.3 us)
Sparse Core Ops, SparseCore 0:
  27.8 46.1 all-gather.7
  76.2 26.5 all-gather.9
  104.9 62.1 all-gather.13
  169.1 105.1 all-gather.11
  275.7 26.1 all-gather.15
  351.9 34.1 all-gather.17
  388.2 33.7 all-gather.19
  500.6 32.5 reduce-scatter.8
  551.4 31.4 reduce-scatter.10
  615.0 34.4 reduce-scatter.12
  663.3 53.4 reduce-scatter.16
  719.6 48.9 reduce-scatter.14
  770.9 54.9 reduce-scatter.18
  830.9 32.7 reduce-scatter.20
  873.6 34.4 reduce-scatter.22

commit v6 on v5

--- a/solution.py
+++ b/solution.py
@@ -730,7 +730,7 @@
             return send_ff(g[0])
         return g[1], lax.ppermute(g[0], "x", SWAP)
 
-    cut_ff = grad_gate.shape[1] // 256 * 128 + LANES
+    cut_ff = grad_gate.shape[1] // 256 * LANES - LANES
     gate_one, gate_two = dots(grad_gate[:, :cut_ff]), dots(grad_gate[:, cut_ff:])
     grad_normed_two, gate_one, gate_two = lax.optimization_barrier(
         (grad_normed_two, gate_one, gate_two)

time: 948 us -> 961 us (1.014)
  waiting for transfers between devices: 392 us -> 403 us
    all_to_all x5, waiting for transfers between devices: 36.7 us -> 52.8 us  [swap_seq(): return lax.all_to_all(x, SEQ, split_axis=0, concat_axis=0, tiled=True)]
where the time goes in v6:
time: 961 us; the launch traced here: 951 us
  waiting for transfers between devices  403 us (42%)
  Pallas kernels  150 us (16%)
  matrix products  103 us (11%)
  local copies, waits for them, and re-layouts  85.1 us (9%)
  starting transfers between devices  78.1 us (8%)
  other arithmetic  75 us (8%)
  blocking collectives  41.2 us (4%)
  between operations  15.2 us (2%)
    ppermute x5, waiting for transfers between devices, gather_peers(): other = lax.ppermute(x, axis, SWAP)  102 us
    ppermute x7, waiting for transfers between devices, gather_far(): return lax.ppermute(near, axis, SWAP)  80.3 us
    ppermute x3, waiting for transfers between devices, send_columns(): return (g[1], lax.ppermute(g[0], 'x', SWAP))  58.7 us
    dot_general x11, matrix products, dot_tn(): lax.dot_general(a, b, (((0,), (0,)), ((), ())), preferred_element_type=out)  57.5 us
    all_to_all x5, waiting for transfers between devices, swap_seq(): return lax.all_to_all(x, SEQ, split_axis=0, concat_axis=0, tiled=True)  52.8 us
    ppermute x5, waiting for transfers between devices, send_rows(): return (keep, lax.ppermute(send, axis, SWAP))  48.8 us
    pallas_call x1, Pallas kernels, attend_back(): pl.pallas_call(functools.partial(backward_body, window), grid=(rpg, block...  35.6 us
    dot_general x6, matrix products, dot(): return jnp.dot(a, b, preferred_element_type=out)  34.1 us
  transfers between devices with their start and end apart: 63, of which 25 were waited for; matrix products, arithmetic and copies ran while one was open for 25% of the time, Pallas kernels for 15%

profile of v6, /device:TPU:0, one launch (start us, length us, event | category | flops | bytes accessed | tf_op | source)
XLA Modules:
  0.0 951.0 jit_solution(8167240489078222714)
XLA Ops:
  11.0 15.8 %all_to_all.70 = bf16[4,64,1536]{2,1,0:T(8,128)(2,1)S(1)} all-to-all(bf16[4,64,1536]{2,1,0:T(8,128)(2,1)S(1)} %reshape.494), channel_id=1, replica_groups=mesh['z'=4,'y'=2,'x'=2,'c'=2] {'x','c'}, dimensions={0} | all-to-all | bytes 1572864 | tf_op jit(solution)/shard_map/all_to_all | solution.py:125
  53.9 17.3 %all-to-all-done.2 = bf16[4,128,1408]{2,1,0:T(8,128)(2,1)S(1)} async-done(((bf16[4,128,1408]{2,1,0:T(8,128)(2,1)}), bf16[4,128,1408]{2,1,0:T(8,128)(2,1)S(1)}, u32[]{:S(2)}, u32[]{:S(2)}) %all-to-all-start.2) | async-done | bytes 1441824 | tf_op jit(solution)/shard_map/all_to_all | solution.py:125
  79.8 22.8 %collective-permute-done.4 = s32[1,2048]{1,0:T(1,128)S(1)} collective-permute-done((s32[1,2048]{1,0:T(1,128)S(1)}, s32[1,2048]{1,0:T(1,128)S(1)}, u32[]{:S(2)}, u32[]{:S(2)}) %collective-permute-start.4) | collective-permute-done | bytes 8224 | tf_op jit(solution)/shard_map/ppermute | solution.py:44
  105.2 16.4 %collective-permute-done.3 = bf16[1024,1024]{1,0:T(8,128)(2,1)S(1)} collective-permute-done((bf16[1024,1024]{1,0:T(8,128)(2,1)}, bf16[1024,1024]{1,0:T(8,128)(2,1)S(1)}, u32[]{:S(2)}, u32[]{:S(2)}) %collective-permute-start.3) | collective-permute-done | bytes 2097184 | tf_op jit(solution)/shard_map/ppermute | solution.py:82
  156.0 43.5 %collective-permute-done.7 = bf16[1024,512]{1,0:T(8,128)(2,1)S(1)} collective-permute-done((bf16[1024,512]{1,0:T(8,128)(2,1)S(1)}, bf16[1024,512]{1,0:T(8,128)(2,1)S(1)}, u32[]{:S(2)}, u32[]{:S(2)}) %collective-permute-start.7) | collective-permute-done | bytes 1048608 | tf_op jit(solution)/shard_map/ppermute | solution.py:82
  213.6 22.6 %all-to-all-done.3.k_ref.v_ref = bf16[8,2,2,256,128]{4,3,2,1,0:T(8,128)(2,1)S(1)} async-done(((bf16[8,2,2,256,128]{4,3,2,1,0:T(8,128)(2,1)}), bf16[8,2,2,256,128]{4,3,2,1,0:T(8,128)(2,1)S(1)}, u32[]{:S(2)}, u32[]{:S(2)}) %all-to-all-start.3) | async-done | bytes 2097184 | tf_op jit(solution)/shard_map/all_to_all | solution.py:129
  243.6 32.8 %collective-permute-done.10 = bf16[256,2048]{1,0:T(8,128)(2,1)} collective-permute-done((bf16[256,2048]{1,0:T(8,128)(2,1)}, bf16[256,2048]{1,0:T(8,128)(2,1)}, u32[]{:S(2)}, u32[]{:S(2)}) %collective-permute-start.10) | collective-permute-done | bytes 1048608 | tf_op jit(solution)/shard_map/ppermute | solution.py:44
  281.6 26.7 %attend.1 = bf16[8,2,256,128]{3,2,1,0:T(8,128)(2,1)} custom-call(bf16[8,1,2,256,128]{4,3,2,1,0:T(8,128)(2,1)} %copy-done.11, bf16[8,2,2,256,128]{4,3,2,1,0:T(8,128)(2,1)} %copy-done, bf16[8,2,2,256,128]{4,3,2,1,0:T(8,128)(2,1)} %copy-done, s32[2,8,256,1]{3,2,1,0:T(8,128)} %reshape.546.start_ref), custom_call_target="tpu_custom_call" | custom-call | flops 1 | bytes 1 | tf_op jit(solution)/shard_map/attend/pallas_call | solution.py:285
  322.8 20.4 %collective-permute-done.13 = bf16[256,2048]{1,0:T(8,128)(2,1)} collective-permute-done((bf16[256,2048]{1,0:T(8,128)(2,1)}, bf16[256,2048]{1,0:T(8,128)(2,1)}, u32[]{:S(2)}, u32[]{:S(2)}) %collective-permute-start.13) | collective-permute-done | bytes 1048608 | tf_op jit(solution)/shard_map/ppermute | solution.py:82
  360.1 23.7 %collective-permute-done.15.c_ref = bf16[256,2048]{1,0:T(8,128)(2,1)} collective-permute-done((bf16[256,2048]{1,0:T(8,128)(2,1)}, bf16[256,2048]{1,0:T(8,128)(2,1)}, u32[]{:S(2)}, u32[]{:S(2)}) %collective-permute-start.15) | collective-permute-done | bytes 1048608 | tf_op jit(solution)/shard_map/ppermute | solution.py:67
  390.8 23.1 %collective-permute-done.16 = bf16[256,2048]{1,0:T(8,128)(2,1)} collective-permute-done((bf16[256,2048]{1,0:T(8,128)(2,1)}, bf16[256,2048]{1,0:T(8,128)(2,1)}, u32[]{:S(2)}, u32[]{:S(2)}) %collective-permute-start.16) | collective-permute-done | bytes 1048608 | tf_op jit(solution)/shard_map/ppermute | solution.py:44
  427.2 20.5 %hidden_units.1 = (f32[1024,1408]{1,0:T(8,128)}, f32[1024,1408]{1,0:T(8,128)}, bf16[1024,1408]{1,0:T(8,128)(2,1)}) custom-call(bf16[1024,2048]{1,0:T(8,128)(2,1)} %pad_maximum_fusion.5.x_ref, bf16[1024,1408]{1,0:T(8,128)(2,1)} %all-gather.14.cloned.1.call-done.gn_ref, bf16[1024,1408]{1,0:T(8,128)(2,1)} %collective-permute-done.8.gf_ref, ...), custom_call_target="tpu_custom_call" | custom-call | flops 1 | bytes 1 | tf_op jit(solution)/shard_map/hidden_units/pallas_call | solution.py:477
  463.5 14.6 %hidden_back.1 = (bf16[1024,1408]{1,0:T(8,128)(2,1)}, bf16[1024,1408]{1,0:T(8,128)(2,1)}) custom-call(bf16[1024,2048]{1,0:T(8,128)(2,1)} %pad_maximum_fusion.4.grad_ref, bf16[1408,1024]{1,0:T(8,128)(2,1)} %bitcast.137, bf16[1408,1024]{1,0:T(8,128)(2,1)} %bitcast.140, f32[1024,1408]{1,0:T(8,128)} %get-tuple-element.126.gate_ref, ...), custom_call_target="tpu_custom_call" | custom-call | flops 1 | bytes 1 | tf_op jit(solution)/shard_map/hidden_back/pallas_call | solution.py:501
  478.1 19.3 %input_back.1 = (bf16[512,2048]{1,0:T(8,128)(2,1)}, bf16[512,2048]{1,0:T(8,128)(2,1)}) custom-call(bf16[1024,1408]{1,0:T(8,128)(2,1)} %get-tuple-element.131.gg_ref, bf16[1024,1408]{1,0:T(8,128)(2,1)} %get-tuple-element.132.gu_ref, bf16[1024,1408]{1,0:T(8,128)(2,1)} %all-gather.14.cloned.1.call-done.gn_ref, ...), custom_call_target="tpu_custom_call" | custom-call | flops 1 | bytes 1 | tf_op jit(solution)/shard_map/input_back/pallas_call | solution.py:542
  523.4 17.3 %collective-permute-done.24 = bf16[4,176,1024]{2,1,0:T(8,128)(2,1)S(1)} collective-permute-done((bf16[4,176,1024]{2,1,0:T(8,128)(2,1)S(1)}, bf16[4,176,1024]{2,1,0:T(8,128)(2,1)S(1)}, u32[]{:S(2)}, u32[]{:S(2)}) %collective-permute-start.24) | collective-permute-done | bytes 1441824 | tf_op jit(solution)/shard_map/ppermute | solution.py:106
  551.4 23.3 %collective-permute-done.25 = bf16[256,2048]{1,0:T(8,128)(2,1)S(1)} collective-permute-done((bf16[256,2048]{1,0:T(8,128)(2,1)}, bf16[256,2048]{1,0:T(8,128)(2,1)S(1)}, u32[]{:S(2)}, u32[]{:S(2)}) %collective-permute-start.25) | collective-permute-done | bytes 1048608 | tf_op jit(solution)/shard_map/ppermute | solution.py:44
  594.1 17.3 %collective-permute-done.28 = bf16[1024,512]{1,0:T(8,128)(2,1)S(1)} collective-permute-done((bf16[1024,512]{1,0:T(8,128)(2,1)}, bf16[1024,512]{1,0:T(8,128)(2,1)S(1)}, u32[]{:S(2)}, u32[]{:S(2)}) %collective-permute-start.28) | collective-permute-done | bytes 1048608 | tf_op jit(solution)/shard_map/ppermute | solution.py:731
  617.3 35.6 %attend_back.1 = bf16[8,3,2,256,128]{4,3,2,1,0:T(8,128)(2,1)} custom-call(bf16[8,1,2,256,128]{4,3,2,1,0:T(8,128)(2,1)} %copy-done.11, bf16[8,2,2,256,128]{4,3,2,1,0:T(8,128)(2,1)} %copy-done, bf16[8,2,2,256,128]{4,3,2,1,0:T(8,128)(2,1)} %copy-done, s32[2,8,256,1]{3,2,1,0:T(8,128)} %reshape.546.start_ref, bf16[8,2,256,128]{3,2,1,0:T(8,128)(2,1)} %copy-done.21), custom_call_target="tpu_custom_call" | custom-call | flops 1 | bytes 1 | tf_op jit(solution)/shard_map/attend_back/pallas_call | solution.py:334
  691.6 40.7 %collective-permute-done.31 = bf16[1024,1408]{1,0:T(8,128)(2,1)} collective-permute-done((bf16[1024,1408]{1,0:T(8,128)(2,1)}, bf16[1024,1408]{1,0:T(8,128)(2,1)}, u32[]{:S(2)}, u32[]{:S(2)}) %collective-permute-start.31) | collective-permute-done | bytes 2883616 | tf_op jit(solution)/shard_map/ppermute | solution.py:731
  747.4 29.8 %all-to-all-done.7 = bf16[8,3,2,256,128]{4,3,2,1,0:T(8,128)(2,1)S(1)} async-done(((bf16[8,3,2,256,128]{4,3,2,1,0:T(8,128)(2,1)}), bf16[8,3,2,256,128]{4,3,2,1,0:T(8,128)(2,1)S(1)}, u32[]{:S(2)}, u32[]{:S(2)}) %all-to-all-start.7) | async-done | bytes 3145760 | tf_op jit(solution)/shard_map/all_to_all | solution.py:129
  818.6 18.1 %collective-permute-done.34 = bf16[4,256,768]{2,1,0:T(8,128)(2,1)} collective-permute-done((bf16[4,256,768]{2,1,0:T(8,128)(2,1)}, bf16[4,256,768]{2,1,0:T(8,128)(2,1)}, u32[]{:S(2)}, u32[]{:S(2)}) %collective-permute-start.34) | collective-permute-done | bytes 1572896 | tf_op jit(solution)/shard_map/ppermute | solution.py:106
  863.2 13.4 %collective-permute-done.35 = bf16[4,256,768]{2,1,0:T(8,128)(2,1)} collective-permute-done((bf16[4,256,768]{2,1,0:T(8,128)(2,1)}, bf16[4,256,768]{2,1,0:T(8,128)(2,1)}, u32[]{:S(2)}, u32[]{:S(2)}) %collective-permute-start.35) | collective-permute-done | bytes 1572896 | tf_op jit(solution)/shard_map/ppermute | solution.py:106
  888.8 11.0 %all_to_all.71 = f32[32,1,448]{2,1,0:T(1,128)S(1)} all-to-all(f32[32,1,448]{2,1,0:T(1,128)S(1)} %all_to_all.52), channel_id=1, replica_groups=mesh['z'=4,'y'=2,'x'=2,'c'=2] {'z','y','x','c'}, dimensions={0} | all-to-all | bytes 114688 | tf_op jit(solution)/shard_map/all_to_all | solution.py:842
  899.8 14.4 %all_to_all.72 = bf16[4,64,1408]{2,1,0:T(8,128)(2,1)S(1)} all-to-all(bf16[4,64,1408]{2,1,0:T(8,128)(2,1)} %bitcast.201), channel_id=1, replica_groups=mesh['z'=4,'y'=2,'x'=2,'c'=2] {'y','c'}, dimensions={0} | all-to-all | bytes 1441792 | tf_op jit(solution)/shard_map/all_to_all | solution.py:125
  (395 shorter events, 395.5 us)
Async XLA Ops:
  7.2 66.9 %all-gather.8.cloned.1.call-start = ((), (), s32[]{:S(2)}) async-start(), calls=%async_computation.21 | async-start | bytes 2621440 | tf_op jit(solution)/shard_map/all_gather | solution.py:76
  52.6 52.5 %all-gather.10.cloned.1.call-start = ((), (), s32[]{:S(2)}) async-start(), calls=%async_computation.22 | async-start | bytes 1310720 | tf_op jit(solution)/shard_map/all_gather | solution.py:76
  53.7 147.6 %all-gather.14.cloned.1.call-start = ((), (), s32[]{:S(2)}) async-start(), calls=%async_computation.24 | async-start | bytes 3604480 | tf_op jit(solution)/shard_map/all_gather | solution.py:76
  74.0 47.5 %collective-permute-start.3 = (bf16[1024,1024]{1,0:T(8,128)(2,1)}, bf16[1024,1024]{1,0:T(8,128)(2,1)S(1)}, u32[]{:S(2)}, u32[]{:S(2)}) collective-permute-start(bf16[1024,1024]{1,0:T(8,128)(2,1)} %all-gather.8.cloned.1.call-done), channel_id=1, source_target_pairs={{0,4},{4,0},{1,5},{5,1},{2,6},{6,2},{3,7},{7,3},{8,12},{12,8},{9,1... | collective-permute-start | bytes 6291464 | tf_op jit(solution)/shard_map/ppermute | solution.py:82
  149.2 87.0 %all-to-all-start.3 = ((bf16[8,2,2,256,128]{4,3,2,1,0:T(8,128)(2,1)}), bf16[8,2,2,256,128]{4,3,2,1,0:T(8,128)(2,1)S(1)}, u32[]{:S(2)}, u32[]{:S(2)}) async-start(bf16[8,2,2,256,128]{4,3,2,1,0:T(8,128)(2,1)} %bitcast.149), calls=%async_computation.3 | async-start | bytes 4194304 | tf_op jit(solution)/shard_map/all_to_all | solution.py:129
  152.9 123.5 %all-gather.12.cloned.1.call-start = ((), (), s32[]{:S(2)}) async-start(), calls=%async_computation.23 | async-start | bytes 3604480 | tf_op jit(solution)/shard_map/all_gather | solution.py:76
  153.5 46.1 %collective-permute-start.7 = (bf16[1024,512]{1,0:T(8,128)(2,1)S(1)}, bf16[1024,512]{1,0:T(8,128)(2,1)S(1)}, u32[]{:S(2)}, u32[]{:S(2)}) collective-permute-start(bf16[1024,512]{1,0:T(8,128)(2,1)S(1)} %copy-done.33), channel_id=1, source_target_pairs={{0,4},{4,0},{1,5},{5,1},{2,6},{6,2},{3,7},{7,3},{8,12},{12,8},{9,1... | collective-permute-start | bytes 3145736 | tf_op jit(solution)/shard_map/ppermute | solution.py:82
  201.2 107.1 %collective-permute-start.8 = (bf16[1024,1408]{1,0:T(8,128)(2,1)}, bf16[1024,1408]{1,0:T(8,128)(2,1)}, u32[]{:S(2)}, u32[]{:S(2)}) collective-permute-start(bf16[1024,1408]{1,0:T(8,128)(2,1)} %all-gather.14.cloned.1.call-done.gn_ref), channel_id=1, source_target_pairs={{0,2},{2,0},{1,3},{3,1},{4,6},{6,4},{5,7},{7,5},{8,10},{10,8},{9,1... | collective-permute-start | bytes 8650760 | tf_op jit(solution)/shard_map/ppermute | solution.py:82
  240.7 67.6 %all-gather.16.cloned.1.call-start = ((), (), s32[]{:S(2)}) async-start(), calls=%async_computation.25 | async-start | bytes 1310720 | tf_op jit(solution)/shard_map/all_gather | solution.py:76
  243.5 70.6 %collective-permute-start.11 = (bf16[256,2048]{1,0:T(8,128)(2,1)}, bf16[256,2048]{1,0:T(8,128)(2,1)}, u32[]{:S(2)}, u32[]{:S(2)}) collective-permute-start(bf16[256,2048]{1,0:T(8,128)(2,1)} %bitcast.181), channel_id=1, source_target_pairs={{0,1},{1,0},{2,3},{3,2},{4,5},{5,4},{6,7},{7,6},{8,9},{9,8},{10,11... | collective-permute-start | bytes 3145736 | tf_op jit(solution)/shard_map/ppermute | solution.py:45
  276.9 67.9 %collective-permute-start.9 = (bf16[1024,1408]{1,0:T(8,128)(2,1)}, bf16[1024,1408]{1,0:T(8,128)(2,1)}, u32[]{:S(2)}, u32[]{:S(2)}) collective-permute-start(bf16[1024,1408]{1,0:T(8,128)(2,1)} %all-gather.12.cloned.1.call-done.un_ref), channel_id=1, source_target_pairs={{0,2},{2,0},{1,3},{3,1},{4,6},{6,4},{5,7},{7,5},{8,10},{10,8},{9,1... | collective-permute-start | bytes 8650760 | tf_op jit(solution)/shard_map/ppermute | solution.py:82
  314.0 74.8 %all-gather.18.cloned.1.call-start = ((), (), s32[]{:S(2)}) async-start(), calls=%async_computation.26 | async-start | bytes 1802240 | tf_op jit(solution)/shard_map/all_gather | solution.py:76
  351.8 70.2 %all-gather.20.cloned.1.call-start = ((), (), s32[]{:S(2)}) async-start(), calls=%async_computation.27 | async-start | bytes 1802240 | tf_op jit(solution)/shard_map/all_gather | solution.py:76
  358.5 183.9 %reduce-scatter.9.cloned.1.call-start = ((), (), s32[]{:S(2)}) async-start(), calls=%async_computation.28 | async-start | bytes 1802240 | tf_op jit(solution)/shard_map/reduce_scatter | solution.py:117
  500.4 82.6 %reduce-scatter.11.cloned.1.call-start = ((), (), s32[]{:S(2)}) async-start(), calls=%async_computation.29 | async-start | bytes 1802240 | tf_op jit(solution)/shard_map/reduce_scatter | solution.py:117
  586.6 67.1 %reduce-scatter.13.cloned.1.call-start = ((), (), s32[]{:S(2)}) async-start(), calls=%async_computation.30 | async-start | bytes 1310720 | tf_op jit(solution)/shard_map/reduce_scatter | solution.py:117
  612.7 132.8 %reduce-scatter.17.cloned.1.call-start = ((), (), s32[]{:S(2)}) async-start(), calls=%async_computation.32 | async-start | bytes 2293760 | tf_op jit(solution)/shard_map/reduce_scatter | solution.py:117
  657.3 119.9 %all-to-all-start.7 = ((bf16[8,3,2,256,128]{4,3,2,1,0:T(8,128)(2,1)}), bf16[8,3,2,256,128]{4,3,2,1,0:T(8,128)(2,1)S(1)}, u32[]{:S(2)}, u32[]{:S(2)}) async-start(bf16[8,3,2,256,128]{4,3,2,1,0:T(8,128)(2,1)} %attend_back.1), calls=%async_computation.10 | async-start | bytes 6291456 | tf_op jit(solution)/shard_map/all_to_all | solution.py:129
  662.6 118.9 %reduce-scatter.15.cloned.1.call-start = ((), (), s32[]{:S(2)}) async-start(), calls=%async_computation.31 | async-start | bytes 1310720 | tf_op jit(solution)/shard_map/reduce_scatter | solution.py:117
  670.7 61.5 %collective-permute-start.31 = (bf16[1024,1408]{1,0:T(8,128)(2,1)}, bf16[1024,1408]{1,0:T(8,128)(2,1)}, u32[]{:S(2)}, u32[]{:S(2)}) collective-permute-start(bf16[1024,1408]{1,0:T(8,128)(2,1)} %fusion.32), channel_id=1, source_target_pairs={{0,2},{2,0},{1,3},{3,1},{4,6},{6,4},{5,7},{7,5},{8,10},{10,8},{9,1... | collective-permute-start | bytes 8650760 | tf_op jit(solution)/shard_map/ppermute | solution.py:731
  678.6 165.5 %reduce-scatter.19.cloned.1.call-start = ((), (), s32[]{:S(2)}) async-start(), calls=%async_computation.33 | async-start | bytes 3604480 | tf_op jit(solution)/shard_map/reduce_scatter | solution.py:117
  689.6 52.3 %collective-permute-start.33 = (bf16[256,2048]{1,0:T(8,128)(2,1)}, bf16[256,2048]{1,0:T(8,128)(2,1)}, u32[]{:S(2)}, u32[]{:S(2)}) collective-permute-start(bf16[256,2048]{1,0:T(8,128)(2,1)} %add_convert_fusion.5), channel_id=1, source_target_pairs={{0,4},{4,0},{1,5},{5,1},{2,6},{6,2},{3,7},{7,3},{8,12},{12,8},{9,1... | collective-permute-start | bytes 3145736 | tf_op jit(solution)/shard_map/ppermute | solution.py:58
  781.4 105.2 %reduce-scatter.21.cloned.1.call-start = ((), (), s32[]{:S(2)}) async-start(), calls=%async_computation.34 | async-start | bytes 1966080 | tf_op jit(solution)/shard_map/reduce_scatter | solution.py:117
  844.1 85.9 %reduce-scatter.23.cloned.1.call-start = ((), (), s32[]{:S(2)}) async-start(), calls=%async_computation.35 | async-start | bytes 1966080 | tf_op jit(solution)/shard_map/reduce_scatter | solution.py:117
  (100 other events, 1791.5 us)
Sparse Core Ops, SparseCore 0:
  27.8 46.1 all-gather.7
  76.2 26.5 all-gather.9
  104.9 62.1 all-gather.13
  169.1 105.1 all-gather.11
  275.8 26.1 all-gather.15
  351.9 34.1 all-gather.17
  388.2 33.7 all-gather.19
  500.5 32.5 reduce-scatter.8
  551.5 31.4 reduce-scatter.10
  612.8 28.1 reduce-scatter.12
  657.4 68.2 reduce-scatter.16
  728.4 49.5 reduce-scatter.14
  780.3 55.8 reduce-scatter.18
  844.2 32.6 reduce-scatter.20
  886.7 34.7 reduce-scatter.22
